TPU v7x, 128 devices: a whole 4x4x4 slice. The times are simulated.
128 devices in a mesh: dp: 8 (over x, core), mem: 16 (over z, y).
Axes of the slice: x: 4, y: 4, z: 4, core: 2. Of those that a mesh axis runs over, the one named last changes fastest.
Arguments:
- tokens: bfloat16 [16384, 2048], P(('dp', 'mem')), may hold values from -60 to 60
- norm_gain: float32 [2048], replicated, may hold values from 0.1 to 1.9
- query_weight: bfloat16 [2048, 2048], P(None, 'dp'), may hold values from -0.125 to 0.125
- values: bfloat16 [131072, 2048], P(('dp', 'mem')), may hold values from -6 to 6
- blocks: int32 [16384, 2], P(('dp', 'mem')), may hold values from 0 to 2047, as said below
- weights: float32 [16384, 2], P(('dp', 'mem')), may hold values from 0.25 to 1
- out_cotangent: bfloat16 [16384, 2048], P(('dp', 'mem')), may hold values from -6 to 6
Outputs:
- layer_out: float32 [16384, 2048], P(('dp', 'mem'))
- grad_tokens: float32 [16384, 2048], P(('dp', 'mem'))
- grad_values: bfloat16 [131072, 2048], P(('dp', 'mem'))
Inputs may be any that keep to these rules, and one draw needn't show every extreme that they name: Block b is held by device b // 16, devices counted as the tokens are (dp major, mem minor). The 2 blocks of one token differ. The tokens of one device make at most 4 lookups (repeats counted) into the blocks held by any one device, and in every draw some devices receive exactly 4 lookups from the tokens of every device.
All inputs are finite; a program needn't handle non-finite values.
Results may differ from a plain program's by a relative error of at most 0.012.
Values may be sent and summed in bfloat16 or wider, within the bound.
No kernel may reach another device: no remote copies, remote signals or barrier semaphores. Data moves between devices by JAX's collectives and lax.ppermute only.
A program may use at most 128 MiB of HBM per device.

v0:
```python
import functools

import jax
import jax.numpy as jnp
import numpy as np
from jax import lax
from jax.experimental import pallas as pl
from jax.experimental.pallas import tpu as pltpu
from jax.sharding import Mesh
from jax.sharding import PartitionSpec as P

BLOCK = 64
SLOTS = 4
CHUNK = 2 * SLOTS
LANES = 128
ALL = ("x", "core", "z", "y")
BF = jnp.bfloat16
F32 = jnp.float32


def params(megabytes):
    return pltpu.CompilerParams(vmem_limit_bytes=megabytes << 20)


def cost(flops, bytes_accessed):
    return pl.CostEstimate(
        flops=int(flops), bytes_accessed=int(bytes_accessed), transcendentals=0
    )


def whole(shape):
    return pl.BlockSpec(shape, lambda *_: (0,) * len(shape))


def nt(left, right):
    return lax.dot_general(left, right, (((1,), (1,)), ((), ())), preferred_element_type=F32)


def nn(left, right):
    return jnp.dot(left, right, preferred_element_type=F32)


def send_kernel(span, tok_ref, gain_ref, blk_ref, wgt_ref, cot_ref, x_ref, tgt_ref, rows_ref, route_ref):
    step = pl.program_id(0)
    count, features = tok_ref.shape
    step_rows = x_ref.shape[0]

    @pl.when(step == 0)
    def _():
        exact = tok_ref[...].astype(F32)
        rms = lax.rsqrt(jnp.mean(exact * exact, axis=1, keepdims=True) + 1e-06)
        rows_ref[:count, :] = ((exact * rms) * gain_ref[...]).astype(BF)
        rows_ref[count:, :] = cot_ref[...]
        square = (count, count)
        sub = lax.broadcasted_iota(jnp.int32, square, 0)
        lane = lax.broadcasted_iota(jnp.int32, square, 1)
        blocks = blk_ref[...]
        weights = wgt_ref[...]
        col = [jnp.broadcast_to(blocks[:, k : k + 1], square) for k in range(2)]
        row = [c.astype(F32).T.astype(jnp.int32) for c in col]
        wrow = [jnp.broadcast_to(weights[:, k : k + 1], square).T for k in range(2)]
        own_col = [c // span for c in col]
        own_row = [r // span for r in row]
        one = lambda hit: jnp.where(hit, 1, 0)
        before = [
            [one((own_col[0] == own_row[0]) & (sub < lane))],
            [one(own_col[0] == own_row[1]), one((own_col[1] == own_row[1]) & (sub < lane))],
        ]
        before_t = [
            [one((own_row[0] == own_col[0]) & (lane < sub))],
            [one(own_row[0] == own_col[1]), one((own_row[1] == own_col[1]) & (lane < sub))],
        ]
        for k in range(2):
            slot_row = sum(jnp.sum(e, axis=0, keepdims=True) for e in before[k])
            slot_col = sum(jnp.sum(e, axis=1, keepdims=True) for e in before_t[k])
            target = own_row[k][:1, :] * CHUNK + slot_row
            route_ref[k : k + 1, :] = target.astype(F32)
            route_ref[2 + k : 3 + k, :] = (row[k][:1, :] % span).astype(F32) + 1.0
            route_ref[4 + k : 5 + k, :] = wrow[k][:1, :]
            tgt_ref[:, k : k + 1] = own_col[k][:, :1] * CHUNK + slot_col

    route = route_ref[...]
    shape = (step_rows, count)
    number = (lax.broadcasted_iota(jnp.int32, shape, 0) + step * step_rows).astype(F32)
    t0, t1 = route[0:1, :], route[1:2, :]
    n0, n1 = number == t0, number == t1
    c0, c1 = number == t0 + SLOTS, number == t1 + SLOTS
    scale = jnp.sum(jnp.where(c0, route[4:5, :], 0.0) + jnp.where(c1, route[5:6, :], 0.0), axis=1, keepdims=True)
    ident = jnp.sum(
        jnp.where(n0 | c0, route[2:3, :], 0.0) + jnp.where(n1 | c1, route[3:4, :], 0.0),
        axis=1,
        keepdims=True,
    )
    is_cot = (lax.broadcasted_iota(jnp.int32, (step_rows, 1), 0) % CHUNK) >= SLOTS
    scale = jnp.where(is_cot, scale, 1.0)
    pick = jnp.concatenate(
        [jnp.where(n0 | n1, 1.0, 0.0), jnp.where(c0 | c1, 1.0, 0.0)], axis=1
    ).astype(BF)
    width = 512
    for at in range(0, features, width):
        rows = nn(pick, rows_ref[:, at : at + width])
        x_ref[:, at : at + width] = (rows * scale).astype(BF)
    x_ref[:, features:] = jnp.broadcast_to(ident - 1.0, (step_rows, LANES)).astype(BF)


def build_payload(tokens, gain, blocks, weights, cot, owners, span):
    count, features = tokens.shape
    rows = owners * CHUNK
    steps = 4
    return pl.pallas_call(
        functools.partial(send_kernel, span),
        out_shape=(
            jax.ShapeDtypeStruct((rows, features + LANES), BF),
            jax.ShapeDtypeStruct((count, 2), jnp.int32),
        ),
        grid=(steps,),
        in_specs=[
            whole((count, features)),
            whole((1, features)),
            whole((count, 2)),
            whole((count, 2)),
            whole((count, features)),
        ],
        out_specs=(
            pl.BlockSpec((rows // steps, features + LANES), lambda i: (i, 0)),
            whole((count, 2)),
        ),
        scratch_shapes=[pltpu.VMEM((2 * count, features), BF), pltpu.VMEM((8, count), F32)],
        compiler_params=params(24),
        cost_estimate=cost(2 * rows * 2 * count * features, 6 << 20),
    )(tokens, gain, blocks, weights, cot)


def slice_at(step, core, half):
    return jnp.where(step < half, 2 * step + core, 2 * (step - half) + 1 - core)


def slice_specs(half, features, width):
    return [
        pl.BlockSpec((1, features, width), lambda a, core: (jnp.minimum(a, half - 1), 0, 0)),
        pl.BlockSpec((1, features, width), lambda a, core: (jnp.maximum(a - half, 0), 0, 0)),
    ]


def with_slice(half, own_ref, sib_ref, use):
    step = pl.program_id(0)

    @pl.when(step < half)
    def _():
        use(own_ref)

    @pl.when(step >= half)
    def _():
        use(sib_ref)


def fold_kernel(half, core_ref, own_ref, sib_ref, val_ref, out_ref, acc_ref):
    step = pl.program_id(0)
    features = acc_ref.shape[0]
    tile = 256

    def use(w_ref):
        val = val_ref[...]

        @pl.loop(0, features // tile)
        def _(i):
            at = pl.ds(pl.multiple_of(i * tile, tile), tile)
            part = nt(w_ref[0, at, :], val)

            @pl.when(step == 0)
            def _():
                acc_ref[at, :] = part

            @pl.when(step > 0)
            def _():
                acc_ref[at, :] += part

            @pl.when(step == 2 * half - 1)
            def _():
                out_ref[at, :] = acc_ref[at, :].astype(BF)

    with_slice(half, own_ref, sib_ref, use)


def fold_weight(core, own, sib, values):
    half, features, width = own.shape
    value_rows = values.shape[0]
    return pl.pallas_call(
        functools.partial(fold_kernel, half),
        out_shape=jax.ShapeDtypeStruct((features, value_rows), BF),
        grid_spec=pltpu.PrefetchScalarGridSpec(
            num_scalar_prefetch=1,
            grid=(2 * half,),
            in_specs=slice_specs(half, features, width)
            + [pl.BlockSpec((value_rows, width), lambda a, core: (0, slice_at(a, core[0], half)))],
            out_specs=whole((features, value_rows)),
            scratch_shapes=[pltpu.VMEM((features, value_rows), F32)],
        ),
        compiler_params=params(32),
        cost_estimate=cost(2 * features * features * value_rows, 16 << 20),
    )(core, own, sib, values)


def serve_kernel(scale, x_hbm, fold_hbm, val_hbm, y_hbm, g_hbm,
                 x_buf, fold_buf, val_buf, n_buf, c_buf, id_buf, g_buf, y_buf, x_sem, f_sem, v_sem, y_sem, g_sem):
    rows = x_buf.shape[0]
    features = n_buf.shape[1]
    value_rows = val_buf.shape[0]
    parts = x_sem.shape[0]
    step_rows = rows // parts
    step_cols = value_rows // parts
    slots = rows // 2

    def x_copy(i):
        at = pl.ds(pl.multiple_of(i * step_rows, step_rows), step_rows)
        return pltpu.make_async_copy(x_hbm.at[at, :], x_buf.at[at, :], x_sem.at[i])

    def f_copy(i):
        return pltpu.make_async_copy(
            fold_hbm.at[:, pl.ds(pl.multiple_of(i * step_cols, step_cols), step_cols)],
            fold_buf.at[i],
            f_sem.at[i],
        )

    def v_copy(i):
        at = pl.ds(pl.multiple_of(i * step_cols, step_cols), step_cols)
        return pltpu.make_async_copy(val_hbm.at[at, :], val_buf.at[at, :], v_sem.at[i])

    for i in range(parts):
        x_copy(i).start()
    for i in range(parts):
        f_copy(i).start()
        v_copy(i).start()

    take = 32
    low = lax.broadcasted_iota(jnp.int32, (take // 16, 8, 1), 1) < SLOTS

    def split(x):
        pairs = x.astype(F32).reshape(take // 16, 16, x.shape[1])
        first, second = pairs[:, :8], pairs[:, 8:]
        upper = jnp.where(low, first, pltpu.roll(second, 4, 1))
        lower = jnp.where(low, pltpu.roll(first, 4, 1), second)
        return upper.reshape(take // 2, x.shape[1]), lower.reshape(take // 2, x.shape[1])

    for i in range(parts):
        x_copy(i).wait()

        @pl.loop(i * step_rows // take, (i + 1) * step_rows // take)
        def _(r):
            src = pl.ds(pl.multiple_of(r * take, take), take)
            dst = pl.ds(pl.multiple_of(r * (take // 2), take // 2), take // 2)
            upper, lower = split(x_buf[src, :features])
            n_buf[dst, :] = upper.astype(BF)
            c_buf[dst, :] = lower.astype(BF)
            ident, _ = split(x_buf[src, features:])
            id_buf[dst, :] = ident

    lows = lax.broadcasted_iota(jnp.int32, (slots // 8, 8, 1), 1) < SLOTS

    @pl.loop(0, parts)
    def _(j):
        f_copy(j).wait()
        v_copy(j).wait()
        at = pl.ds(pl.multiple_of(j * step_cols, step_cols), step_cols)
        scores = nn(n_buf[...], fold_buf[j]) * scale
        sig = 1.0 / (1.0 + jnp.exp(-scores))
        cot_scores = nt(c_buf[...], val_buf[at, :])
        block_of = (lax.broadcasted_iota(jnp.int32, (1, step_cols), 1) // BLOCK + j * (step_cols // BLOCK)).astype(F32)
        mine = id_buf[:, :1] == block_of
        gates = jnp.where(mine, sig, 0.0).reshape(slots // 8, 8, step_cols)
        grads = jnp.where(mine, cot_scores * sig * (1.0 - sig) * scale, 0.0).reshape(slots // 8, 8, step_cols)
        first = jnp.where(lows, gates, pltpu.roll(grads, 4, 1))
        second = jnp.where(lows, pltpu.roll(gates, 4, 1), grads)
        mixed = jnp.concatenate([first, second], axis=1).reshape(rows, step_cols).astype(BF)
        g_buf[j] = mixed

    def g_copy(i):
        return pltpu.make_async_copy(
            g_buf.at[i], g_hbm.at[:, pl.ds(i * step_cols, step_cols)], g_sem.at[i]
        )

    for i in range(parts):
        g_copy(i).start()

    tiles = y_sem.shape[0]
    width = features // tiles

    def y_copy(i):
        at = pl.ds(pl.multiple_of(i * width, width), width)
        return pltpu.make_async_copy(y_buf.at[i], y_hbm.at[:, at], y_sem.at[i])

    @pl.loop(0, tiles)
    def _(i):
        at = pl.ds(pl.multiple_of(i * width, width), width)
        total = nn(g_buf[0], val_buf[0:step_cols, at])
        for j in range(1, parts):
            total += nn(g_buf[j], val_buf[j * step_cols : (j + 1) * step_cols, at])
        y_buf[i] = total.astype(BF)
        y_copy(i).start()

    for i in range(parts):
        g_copy(i).wait()
    for i in range(tiles):
        y_copy(i).wait()


def serve(x, fold, values, features):
    rows = x.shape[0]
    value_rows = values.shape[0]
    parts, tiles = 4, 8
    step_cols = value_rows // parts
    any_spec = pl.BlockSpec(memory_space=pl.ANY)
    return pl.pallas_call(
        functools.partial(serve_kernel, float(features) ** (-0.5)),
        out_shape=(
            jax.ShapeDtypeStruct((rows, features), BF),
            jax.ShapeDtypeStruct((rows, value_rows), BF),
        ),
        in_specs=[any_spec] * 3,
        out_specs=(any_spec, any_spec),
        scratch_shapes=[
            pltpu.VMEM(x.shape, BF),
            pltpu.VMEM((parts, features, step_cols), BF),
            pltpu.VMEM(values.shape, BF),
            pltpu.VMEM((rows // 2, features), BF),
            pltpu.VMEM((rows // 2, features), BF),
            pltpu.VMEM((rows // 2, LANES), F32),
            pltpu.VMEM((parts, rows, step_cols), BF),
            pltpu.VMEM((tiles, rows, features // tiles), BF),
            pltpu.SemaphoreType.DMA((parts,)),
            pltpu.SemaphoreType.DMA((parts,)),
            pltpu.SemaphoreType.DMA((parts,)),
            pltpu.SemaphoreType.DMA((tiles,)),
            pltpu.SemaphoreType.DMA((parts,)),
        ],
        compiler_params=params(48),
        cost_estimate=cost(4 * rows * value_rows * features, 20 << 20),
    )(x, fold, values)


def grad_kernel(half, core_ref, own_ref, sib_ref, x_ref, part_ref, g_ref, out_ref, gt_ref):
    step = pl.program_id(0)
    rows = x_ref.shape[0]
    tile = 256

    @pl.when(step == 0)
    def _():
        for i in range(0, rows, tile):
            gt_ref[:, i : i + tile] = g_ref[i : i + tile, :].T

    def use(w_ref):
        features = w_ref.shape[1]
        width = w_ref.shape[2]
        low = lax.broadcasted_iota(jnp.int32, (tile // 8, 8, 1), 1) < SLOTS
        pieces = []
        for i in range(0, rows, tile):
            queries = nn(x_ref[i : i + tile, :features], w_ref[0]).reshape(tile // 8, 8, width)
            sent = part_ref[i : i + tile, :].astype(F32).reshape(tile // 8, 8, width)
            other = jnp.where(low, pltpu.roll(sent, 4, 1), pltpu.roll(queries, 4, 1))
            pieces.append(other.reshape(tile, width).astype(BF))
        other = jnp.concatenate(pieces, axis=0)
        for i in range(0, out_ref.shape[0], tile):
            out_ref[i : i + tile, :] = nn(gt_ref[i : i + tile, :], other).astype(BF)

    with_slice(half, own_ref, sib_ref, use)


def value_grads(core, own, sib, x, g):
    half, features, width = own.shape
    rows, value_rows = g.shape
    return pl.pallas_call(
        functools.partial(grad_kernel, half),
        out_shape=jax.ShapeDtypeStruct((value_rows, features), BF),
        grid_spec=pltpu.PrefetchScalarGridSpec(
            num_scalar_prefetch=1,
            grid=(2 * half,),
            in_specs=slice_specs(half, features, width)
            + [
                whole(x.shape),
                pl.BlockSpec((rows, width), lambda a, core: (0, slice_at(a, core[0], half))),
                whole(g.shape),
            ],
            out_specs=pl.BlockSpec((value_rows, width), lambda a, core: (0, slice_at(a, core[0], half))),
            scratch_shapes=[pltpu.VMEM((value_rows, rows), BF)],
        ),
        compiler_params=params(40),
        cost_estimate=cost(6 * rows * value_rows * features, 24 << 20),
    )(core, own, sib, x, x, g)


def home_kernel(half, core_ref, own_ref, sib_ref, back_ref, tgt_ref, wgt_ref, tok_ref, cot_ref, gain_ref,
                out_ref, grad_ref, query_ref, acc_ref):
    step = pl.program_id(0)
    count, features = tok_ref.shape
    rows = back_ref.shape[0]
    width = query_ref.shape[2]

    @pl.when(step == 0)
    def _():
        number = lax.broadcasted_iota(jnp.int32, (count, rows), 1)
        targets = tgt_ref[...]
        weights = wgt_ref[...]
        t0, t1 = targets[:, :1], targets[:, 1:]
        one = lambda hit: jnp.where(hit, 1.0, 0.0).astype(BF)
        pick = jnp.concatenate(
            [
                one(number == t0),
                one(number == t1),
                one((number == t0 + SLOTS) | (number == t1 + SLOTS)),
            ],
            axis=0,
        )
        for i in range(2 * half):
            at = slice(i * width, (i + 1) * width)
            got = nn(pick, back_ref[:, at])
            out_ref[:, at] = tok_ref[:, at].astype(F32) + (
                weights[:, :1] * got[:count] + weights[:, 1:] * got[count : 2 * count]
            )
            query_ref[i] = got[2 * count :].astype(BF)
        acc_ref[...] = jnp.zeros_like(acc_ref)

    at = slice_at(step, core_ref[0], half)

    def use(w_ref):
        acc_ref[...] += nt(query_ref[at], w_ref[0])

    with_slice(half, own_ref, sib_ref, use)

    @pl.when(step == 2 * half - 1)
    def _():
        exact = tok_ref[...].astype(F32)
        rms = lax.rsqrt(jnp.mean(exact * exact, axis=1, keepdims=True) + 1e-06)
        unit = exact * rms
        unit_grad = acc_ref[...] * gain_ref[...]
        mean = jnp.mean(unit_grad * unit, axis=1, keepdims=True)
        grad_ref[...] = cot_ref[...].astype(F32) + rms * (unit_grad - unit * mean)


def finish(core, own, sib, back, targets, weights, tokens, cot, gain):
    half, features, width = own.shape
    count = tokens.shape[0]
    return pl.pallas_call(
        functools.partial(home_kernel, half),
        out_shape=(
            jax.ShapeDtypeStruct((count, features), F32),
            jax.ShapeDtypeStruct((count, features), F32),
        ),
        grid_spec=pltpu.PrefetchScalarGridSpec(
            num_scalar_prefetch=1,
            grid=(2 * half,),
            in_specs=slice_specs(half, features, width)
            + [
                whole(back.shape),
                whole((count, 2)),
                whole((count, 2)),
                whole(tokens.shape),
                whole(cot.shape),
                whole((1, features)),
            ],
            out_specs=(whole((count, features)), whole((count, features))),
            scratch_shapes=[
                pltpu.VMEM((2 * half, count, width), BF),
                pltpu.VMEM((count, features), F32),
            ],
        ),
        compiler_params=params(40),
        cost_estimate=cost(4 * count * features * features, 14 << 20),
    )(core, own, sib, back, targets, weights, tokens, cot, gain)


def gather_weight(query_weight):
    own = lax.all_gather(query_weight, "x", axis=0, tiled=False)
    sib = lax.ppermute(own, "core", [(0, 1), (1, 0)])
    return own, sib


def exchange(rows):
    return lax.all_to_all(rows, ALL, split_axis=0, concat_axis=0, tiled=True)


def body(tokens, norm_gain, query_weight, values, blocks, weights, out_cotangent):
    features = tokens.shape[1]
    owners = lax.axis_size(ALL)
    core = lax.axis_index("core").astype(jnp.int32).reshape(1)
    gain = norm_gain.reshape(1, features)
    own, sib = gather_weight(query_weight)
    payload, targets = build_payload(
        tokens, gain, blocks, weights, out_cotangent, owners, values.shape[0] // BLOCK
    )
    got = exchange(payload)
    fold = fold_weight(core, own, sib, values)
    answers, mixed = serve(got, fold, values, features)
    back = exchange(answers)
    grad_values = value_grads(core, own, sib, got, mixed)
    layer_out, grad_tokens = finish(
        core, own, sib, back, targets, weights, tokens, out_cotangent, gain
    )
    return layer_out, grad_tokens, grad_values


def solution(mesh):
    fine = Mesh(np.asarray(mesh.devices).reshape(4, 2, 4, 4), ALL)
    rows = P(ALL, None)
    return jax.shard_map(
        body,
        mesh=fine,
        in_specs=(rows, P(), P(None, ("x", "core")), rows, rows, rows, rows),
        out_specs=(rows, rows, rows),
        check_vma=False,
    )
```

profile of v0, /device:TPU:7, one launch (start us, length us, event | category | flops | bytes accessed | tf_op | source)
XLA Modules:
  0.0 229.0 jit_solution(8605776409412438140)
XLA Ops:
  7.2 0.0 all-gather.3.cloned.1.call-start
  7.2 0.7 all-gather.3.cloned.1.call-update
  7.9 50.5 %all-gather.3.cloned.1.call-done = bf16[8192,256]{1,0:T(8,128)(2,1)} async-done(((bf16[2048,256]{1,0:T(8,128)(2,1)}), bf16[8192,256]{1,0:T(8,128)(2,1)}) %all-gather.3.cloned.1.call-update) | async-done | bytes 4194320 | tf_op jit(solution)/shard_map/all_gather | solution.py:472
  58.4 0.7 collective-permute-start
  59.1 0.8 copy.11.wgt_ref
  59.9 0.8 copy.10.blk_ref
  60.7 0.0 copy-start.4
  60.7 1.0 copy-done.4
  61.8 0.0 copy-start.6
  61.8 1.0 copy-done.6
  62.8 0.0 copy-start.8
  62.8 0.7 copy-done.8
  63.5 2.7 %shard_map.94 = (bf16[1024,2176]{1,0:T(8,128)(2,1)S(1)}, s32[128,2]{1,0:T(8,128)S(1)}) custom-call(bf16[128,2048]{1,0:T(8,128)(2,1)S(1)} %copy-done.4, f32[1,2048]{1,0:T(1,128)S(1)} %bitcast.12, s32[128,2]{1,0:T(8,128)S(1)} %copy.10.blk_ref, f32[128,2]{1,0:T(8,128)S(1)} %copy.11.wgt_ref, bf16[128,2048]{1,0:T(8,128)(2,1)S(1)} %copy-done.6), custom_call_target="tpu_custom_call" | custom-call | flops 1073741824 | bytes 6291456 | tf_op jit(solution)/shard_map/pallas_call | solution.py:110
  66.2 0.0 copy-start
  66.2 2.1 copy-done
  68.3 10.4 %all-to-all-start = ((bf16[128,8,2176]{2,1,0:T(8,128)(2,1)}), bf16[128,8,2176]{2,1,0:T(8,128)(2,1)}, u32[]{:S(2)}, u32[]{:S(2)}) async-start(bf16[128,8,2176]{2,1,0:T(8,128)(2,1)} %bitcast.7), calls=%async_computation | async-start | bytes 8912896 | tf_op jit(solution)/shard_map/all_to_all | solution.py:478
  78.7 0.0 collective-permute-done.sib_ref
  78.7 0.0 copy-start.1
  78.7 2.2 copy-done.1
  80.9 0.0 copy-start.10
  80.9 2.2 copy-done.10
  83.1 30.8 %shard_map.95.fold_hbm = bf16[2048,1024]{1,0:T(8,128)(2,1)S(1)} custom-call(s32[1]{0:T(128)} %bitcast.core_ref, bf16[4,2048,256]{2,1,0:T(8,128)(2,1)S(1)} %bitcast.9, bf16[4,2048,256]{2,1,0:T(8,128)(2,1)} %collective-permute-done.sib_ref, bf16[1024,2048]{1,0:T(8,128)(2,1)S(1)} %copy-done.10), custom_call_target="tpu_custom_call" | custom-call | flops 8589934592 | bytes 16777216 | tf_op jit(solution)/shard_map/pallas_call | solution.py:188
  113.9 0.0 copy-start.11
  113.9 2.0 copy-done.11
  115.9 17.8 %all-to-all-done = bf16[128,8,2176]{2,1,0:T(8,128)(2,1)} async-done(((bf16[128,8,2176]{2,1,0:T(8,128)(2,1)}), bf16[128,8,2176]{2,1,0:T(8,128)(2,1)}, u32[]{:S(2)}, u32[]{:S(2)}) %all-to-all-start) | async-done | bytes 4456480 | tf_op jit(solution)/shard_map/all_to_all | solution.py:478
  133.7 17.3 %shard_map.96 = (bf16[1024,2048]{1,0:T(8,128)(2,1)}, bf16[1024,1024]{1,0:T(8,128)(2,1)S(1)}) custom-call(bf16[1024,2176]{1,0:T(8,128)(2,1)} %bitcast.4.x_hbm.x_ref.part_ref, bf16[2048,1024]{1,0:T(8,128)(2,1)} %copy-done.11, bf16[1024,2048]{1,0:T(8,128)(2,1)} %val_hbm.1), custom_call_target="tpu_custom_call" | custom-call | flops 8589934592 | bytes 20971520 | tf_op jit(solution)/shard_map/pallas_call | solution.py:313
  151.0 5.3 %all-to-all-start.1 = ((bf16[128,8,2048]{2,1,0:T(8,128)(2,1)}), bf16[128,8,2048]{2,1,0:T(8,128)(2,1)}, u32[]{:S(2)}, u32[]{:S(2)}) async-start(bf16[128,8,2048]{2,1,0:T(8,128)(2,1)} %bitcast.14), calls=%async_computation.1 | async-start | bytes 8388608 | tf_op jit(solution)/shard_map/all_to_all | solution.py:478
  156.2 0.0 copy-start.2
  156.2 2.2 copy-done.2
  158.4 0.0 copy-start.5
  158.4 0.0 copy-start.7
  158.4 0.0 copy-start.9
  158.4 19.1 %shard_map.98 = bf16[1024,2048]{1,0:T(8,128)(2,1)} custom-call(s32[1]{0:T(128)} %bitcast.core_ref, bf16[4,2048,256]{2,1,0:T(8,128)(2,1)S(1)} %bitcast.10, bf16[4,2048,256]{2,1,0:T(8,128)(2,1)} %collective-permute-done.sib_ref, bf16[1024,2176]{1,0:T(8,128)(2,1)} %bitcast.4.x_hbm.x_ref.part_ref, bf16[1024,2176]{1,0:T(8,128)(2,1)} %bitcast.4.x_hbm.x_ref.part_ref, ...), custom_call_target="tpu_custom_call" | custom-call | flops 12884901888 | bytes 25165824 | tf_op jit(solution)/shard_map/pallas_call | solution.py:371
  177.6 30.6 %all-to-all-done.1 = bf16[128,8,2048]{2,1,0:T(8,128)(2,1)} async-done(((bf16[128,8,2048]{2,1,0:T(8,128)(2,1)}), bf16[128,8,2048]{2,1,0:T(8,128)(2,1)}, u32[]{:S(2)}, u32[]{:S(2)}) %all-to-all-start.1) | async-done | bytes 4194336 | tf_op jit(solution)/shard_map/all_to_all | solution.py:478
  208.2 0.0 copy-done.5
  208.2 0.0 copy-done.7
  208.2 0.0 copy-done.9
  208.2 0.0 copy-start.3
  208.2 2.2 copy-done.3
  210.4 11.7 %shard_map.97 = (f32[128,2048]{1,0:T(8,128)}, f32[128,2048]{1,0:T(8,128)}) custom-call(s32[1]{0:T(128)} %bitcast.core_ref, bf16[4,2048,256]{2,1,0:T(8,128)(2,1)S(1)} %bitcast.11, bf16[4,2048,256]{2,1,0:T(8,128)(2,1)} %collective-permute-done.sib_ref, bf16[1024,2048]{1,0:T(8,128)(2,1)} %bitcast.6.back_ref, s32[128,2]{1,0:T(8,128)S(1)} %get-tuple-element.11.tgt_ref, ...), custom_call_target="tpu_custom_call" | custom-call | flops 2147483648 | bytes 14680064 | tf_op jit(solution)/shard_map/pallas_call | solution.py:442
Async XLA Ops:
  7.2 51.2 %all-gather.3.cloned.1.call-start = ((), (), s32[]{:S(2)}) async-start(), calls=%async_computation.2 | async-start | bytes 5242880 | tf_op jit(solution)/shard_map/all_gather | solution.py:472
  58.4 20.3 %collective-permute-start = (bf16[4,2048,256]{2,1,0:T(8,128)(2,1)}, bf16[4,2048,256]{2,1,0:T(8,128)(2,1)}, u32[]{:S(2)}, u32[]{:S(2)}) collective-permute-start(bf16[4,2048,256]{2,1,0:T(8,128)(2,1)} %bitcast.8), channel_id=1, source_target_pairs={{0,16},{16,0},{1,17},{17,1},{2,18},{18,2},{3,19},{19,3},{4,20},{20... | collective-permute-start | bytes 12582920 | tf_op jit(solution)/shard_map/ppermute | solution.py:473
  60.7 1.0 copy-start.4
  61.8 1.0 copy-start.6
  62.8 0.7 copy-start.8
  66.2 2.1 copy-start
  68.3 65.4 %all-to-all-start = ((bf16[128,8,2176]{2,1,0:T(8,128)(2,1)}), bf16[128,8,2176]{2,1,0:T(8,128)(2,1)}, u32[]{:S(2)}, u32[]{:S(2)}) async-start(bf16[128,8,2176]{2,1,0:T(8,128)(2,1)} %bitcast.7), calls=%async_computation | async-start | bytes 8912896 | tf_op jit(solution)/shard_map/all_to_all | solution.py:478
  78.7 2.2 copy-start.1
  80.9 2.2 copy-start.10
  113.9 2.0 copy-start.11
  151.0 57.2 %all-to-all-start.1 = ((bf16[128,8,2048]{2,1,0:T(8,128)(2,1)}), bf16[128,8,2048]{2,1,0:T(8,128)(2,1)}, u32[]{:S(2)}, u32[]{:S(2)}) async-start(bf16[128,8,2048]{2,1,0:T(8,128)(2,1)} %bitcast.14), calls=%async_computation.1 | async-start | bytes 8388608 | tf_op jit(solution)/shard_map/all_to_all | solution.py:478
  156.2 2.2 copy-start.2
  158.4 49.8 %copy-start.5 = (bf16[128,2048]{1,0:T(8,128)(2,1)S(1)}, bf16[128,2048]{1,0:T(8,128)(2,1)}, u32[]{:S(2)}) copy-start(bf16[128,2048]{1,0:T(8,128)(2,1)} %tok_ref.3) | copy-start | bytes 1572868
  158.4 49.8 %copy-start.7 = (bf16[128,2048]{1,0:T(8,128)(2,1)S(1)}, bf16[128,2048]{1,0:T(8,128)(2,1)}, u32[]{:S(2)}) copy-start(bf16[128,2048]{1,0:T(8,128)(2,1)} %cot_ref.3) | copy-start | bytes 1572868
  158.4 49.8 %copy-start.9 = (f32[2048]{0:T(1024)S(1)}, f32[2048]{0:T(1024)}, u32[]{:S(2)}) copy-start(f32[2048]{0:T(1024)} %param.8) | copy-start | bytes 24580
  208.2 2.2 copy-start.3
Sparse Core Ops, SparseCore 0:
  9.7 48.6 all-gather.2
where the time goes:
time: 230 us; the launch traced here: 229 us
  waiting for transfers between devices  99.6 us (43%)
  Pallas kernels  81.6 us (35%)
  local copies, waits for them, and re-layouts  17.2 us (7%)
  starting transfers between devices  16.5 us (7%)
  between operations  14.1 us (6%)
    all_gather x1, waiting for transfers between devices, gather_weight(): own = lax.all_gather(query_weight, 'x', axis=0, tiled=False)  50.5 us
    all_to_all x2, waiting for transfers between devices, exchange(): return lax.all_to_all(rows, ALL, split_axis=0, concat_axis=0, tiled=True)  48.4 us
    pallas_call x1, Pallas kernels, fold_weight(): pl.pallas_call(functools.partial(fold_kernel, half), out_shape=jax.ShapeD...  30.8 us
    pallas_call x1, Pallas kernels, value_grads(): pl.pallas_call(functools.partial(grad_kernel, half), out_shape=jax.ShapeD...  19.1 us
    pallas_call x1, Pallas kernels, serve(): pl.pallas_call(functools.partial(serve_kernel, float(features) ** (-0.5))...  17.3 us
    unnamed x26, local copies, waits for them, and re-layouts  17.2 us
    all_to_all x2, starting transfers between devices, exchange(): return lax.all_to_all(rows, ALL, split_axis=0, concat_axis=0, tiled=True)  15.7 us
    pallas_call x1, Pallas kernels, finish(): pl.pallas_call(functools.partial(home_kernel, half), out_shape=(jax.Shape...  11.7 us
  transfers between devices with their start and end apart: 4, of which 3 were waited for; matrix products, arithmetic and copies ran while one was open for 1% of the time, Pallas kernels for 23%

commit v1 on v0

v1 whole, which is shorter than its diff:
```python
import functools

import jax
import jax.numpy as jnp
import numpy as np
from jax import lax
from jax.experimental import pallas as pl
from jax.experimental.pallas import tpu as pltpu
from jax.sharding import Mesh
from jax.sharding import PartitionSpec as P

BLOCK = 64
SLOTS = 4
CHUNK = 2 * SLOTS
LANES = 128
ALL = ("x", "core", "z", "y")
BF = jnp.bfloat16
F32 = jnp.float32
MB = 60


def params(megabytes):
    return pltpu.CompilerParams(vmem_limit_bytes=megabytes << 20)


def cost(flops, bytes_accessed):
    return pl.CostEstimate(
        flops=int(flops), bytes_accessed=int(bytes_accessed), transcendentals=0
    )


def whole(shape):
    return pl.BlockSpec(shape, lambda *_: (0,) * len(shape))


def nt(left, right):
    return lax.dot_general(left, right, (((1,), (1,)), ((), ())), preferred_element_type=F32)


def nn(left, right):
    return jnp.dot(left, right, preferred_element_type=F32)


def send_kernel(span, tok_ref, gain_ref, blk_ref, wgt_ref, cot_ref, x_ref, tgt_ref, rows_ref, route_ref):
    step = pl.program_id(0)
    count, features = tok_ref.shape
    step_rows = x_ref.shape[0]

    @pl.when(step == 0)
    def _():
        exact = tok_ref[...].astype(F32)
        rms = lax.rsqrt(jnp.mean(exact * exact, axis=1, keepdims=True) + 1e-06)
        rows_ref[:count, :] = ((exact * rms) * gain_ref[...]).astype(BF)
        rows_ref[count:, :] = cot_ref[...]
        square = (count, count)
        sub = lax.broadcasted_iota(jnp.int32, square, 0)
        lane = lax.broadcasted_iota(jnp.int32, square, 1)
        blocks = blk_ref[...]
        weights = wgt_ref[...]
        col = [jnp.broadcast_to(blocks[:, k : k + 1], square) for k in range(2)]
        row = [c.astype(F32).T.astype(jnp.int32) for c in col]
        wrow = [jnp.broadcast_to(weights[:, k : k + 1], square).T for k in range(2)]
        own_col = [c // span for c in col]
        own_row = [r // span for r in row]
        one = lambda hit: jnp.where(hit, 1, 0)
        before = [
            [one((own_col[0] == own_row[0]) & (sub < lane))],
            [one(own_col[0] == own_row[1]), one((own_col[1] == own_row[1]) & (sub < lane))],
        ]
        before_t = [
            [one((own_row[0] == own_col[0]) & (lane < sub))],
            [one(own_row[0] == own_col[1]), one((own_row[1] == own_col[1]) & (lane < sub))],
        ]
        for k in range(2):
            slot_row = sum(jnp.sum(e, axis=0, keepdims=True) for e in before[k])
            slot_col = sum(jnp.sum(e, axis=1, keepdims=True) for e in before_t[k])
            target = own_row[k][:1, :] * CHUNK + slot_row
            route_ref[k : k + 1, :] = target.astype(F32)
            route_ref[2 + k : 3 + k, :] = (row[k][:1, :] % span).astype(F32) + 1.0
            route_ref[4 + k : 5 + k, :] = wrow[k][:1, :]
            tgt_ref[:, k : k + 1] = own_col[k][:, :1] * CHUNK + slot_col

    route = route_ref[...]
    shape = (step_rows, count)
    number = (lax.broadcasted_iota(jnp.int32, shape, 0) + step * step_rows).astype(F32)
    t0, t1 = route[0:1, :], route[1:2, :]
    n0, n1 = number == t0, number == t1
    c0, c1 = number == t0 + SLOTS, number == t1 + SLOTS
    scale = jnp.sum(jnp.where(c0, route[4:5, :], 0.0) + jnp.where(c1, route[5:6, :], 0.0), axis=1, keepdims=True)
    ident = jnp.sum(
        jnp.where(n0 | c0, route[2:3, :], 0.0) + jnp.where(n1 | c1, route[3:4, :], 0.0),
        axis=1,
        keepdims=True,
    )
    is_cot = (lax.broadcasted_iota(jnp.int32, (step_rows, 1), 0) % CHUNK) >= SLOTS
    scale = jnp.where(is_cot, scale, 1.0)
    pick = jnp.concatenate(
        [jnp.where(n0 | n1, 1.0, 0.0), jnp.where(c0 | c1, 1.0, 0.0)], axis=1
    ).astype(BF)
    width = 512
    for at in range(0, features, width):
        rows = nn(pick, rows_ref[:, at : at + width])
        x_ref[:, at : at + width] = (rows * scale).astype(BF)
    x_ref[:, features:] = jnp.broadcast_to(ident - 1.0, (step_rows, LANES)).astype(BF)


def build_payload(tokens, gain, blocks, weights, cot, owners, span):
    count, features = tokens.shape
    rows = owners * CHUNK
    steps = 4
    return pl.pallas_call(
        functools.partial(send_kernel, span),
        out_shape=(
            jax.ShapeDtypeStruct((rows, features + LANES), BF),
            jax.ShapeDtypeStruct((count, 2), jnp.int32),
        ),
        grid=(steps,),
        in_specs=[
            whole((count, features)),
            whole((1, features)),
            whole((count, 2)),
            whole((count, 2)),
            whole((count, features)),
        ],
        out_specs=(
            pl.BlockSpec((rows // steps, features + LANES), lambda i: (i, 0)),
            whole((count, 2)),
        ),
        scratch_shapes=[pltpu.VMEM((2 * count, features), BF), pltpu.VMEM((8, count), F32)],
        compiler_params=params(MB),
        cost_estimate=cost(2 * rows * 2 * count * features, 6 << 20),
    )(tokens, gain, blocks, weights, cot)


def ring(axis, size, by):
    return lambda rows: lax.ppermute(rows, axis, [(i, (i + by) % size) for i in range(size)])


def both_ways(axis, size, piece):
    up, down = ring(axis, size, 1), ring(axis, size, -1)
    half = piece.shape[0] // 2
    before, after = up(piece), down(piece)
    return before, after, up(before[:half]), down(after[half:])


def assemble_kernel(at_ref, w_ref, *refs):
    pieces, out_ref, sems = refs[:-2], refs[-2], refs[-1]
    x, z, y = at_ref[0], at_ref[1], at_ref[2]
    width = w_ref.shape[1]
    half_rows = w_ref.shape[0] // 2
    columns = [lax.rem(x + d, 4) for d in (3, 1, 2)]
    copies = []

    def add(src, row, column, rows):
        copies.append(
            pltpu.make_async_copy(
                src,
                out_ref.at[
                    pl.ds(pl.multiple_of(row, 128), rows),
                    pl.ds(pl.multiple_of(column * width, width), width),
                ],
                sems.at[len(copies)],
            )
        )

    add(w_ref, 0, x, w_ref.shape[0])
    for part, me in ((0, y), (1, z)):
        mine, before, after, top, bottom = pieces[5 * part : 5 * part + 5]
        rows = mine.shape[0]
        base = part * half_rows
        across = lax.rem(me + 2, 4) * rows
        places = [
            (mine, me * rows),
            (before, lax.rem(me + 3, 4) * rows),
            (after, lax.rem(me + 1, 4) * rows),
            (top, across),
            (bottom, across + rows // 2),
        ]
        for piece, row in places:
            for k, column in enumerate(columns):
                add(
                    piece.at[:, k * width : (k + 1) * width],
                    base + row,
                    column,
                    piece.shape[0],
                )
    for copy in copies:
        copy.start()
    for copy in copies:
        copy.wait()


def gather_own(weight, after_this):
    features, width = weight.shape
    half, rows = features // 2, features // 8
    x, z, y = (lax.axis_index(n).astype(jnp.int32) for n in ("x", "z", "y"))
    mine = jnp.concatenate(
        [
            lax.dynamic_slice(weight, (y * rows, 0), (rows, width)),
            lax.dynamic_slice(weight, (half + z * rows, 0), (rows, width)),
        ],
        axis=0,
    )
    up, down = ring("x", 4, 1), ring("x", 4, -1)
    before, after = up(mine), down(mine)
    before, after, after_this = lax.optimization_barrier((before, after, after_this))
    across_y, across_z = up(before[:rows]), down(after[rows:])
    set_y = jnp.concatenate([before[:rows], after[:rows], across_y], axis=1)
    set_z = jnp.concatenate([before[rows:], after[rows:], across_z], axis=1)
    pieces = (set_y, *both_ways("y", 4, set_y), set_z, *both_ways("z", 4, set_z))
    any_spec = pl.BlockSpec(memory_space=pl.ANY)
    return pl.pallas_call(
        assemble_kernel,
        out_shape=jax.ShapeDtypeStruct((features, 4 * width), BF),
        in_specs=[pl.BlockSpec(memory_space=pltpu.SMEM)] + [any_spec] * 11,
        out_specs=any_spec,
        scratch_shapes=[pltpu.SemaphoreType.DMA((31,))],
        compiler_params=params(MB),
        cost_estimate=cost(1, 1),
    )(jnp.stack([x, z, y]), weight, *pieces)


def slice_at(step, core, half):
    return jnp.where(step < half, 2 * step + core, 2 * (step - half) + 1 - core)


def slice_specs(half, features, width):
    return [
        pl.BlockSpec((features, width), lambda a, core: (0, jnp.minimum(a, half - 1))),
        pl.BlockSpec((features, width), lambda a, core: (0, jnp.maximum(a - half, 0))),
    ]


def with_slice(half, own_ref, sib_ref, use):
    step = pl.program_id(0)

    @pl.when(step < half)
    def _():
        use(own_ref)

    @pl.when(step >= half)
    def _():
        use(sib_ref)


def fold_kernel(core_ref, own_ref, sib_ref, val_ref, out_ref, vt_own, vt_sib):
    width = own_ref.shape[1] // 4
    tile = 256

    @pl.when(pl.program_id(0) == 0)
    def _():
        core = core_ref[0]
        for x in range(4):
            to = slice(x * width, (x + 1) * width)
            for vt, c in ((vt_own, core), (vt_sib, 1 - core)):
                at = pl.ds(pl.multiple_of((2 * x + c) * width, width), width)
                vt[to, :] = val_ref[:, at].T

    for i in range(0, out_ref.shape[1], tile):
        at = slice(i, i + tile)
        total = nn(own_ref[...], vt_own[:, at]) + nn(sib_ref[...], vt_sib[:, at])
        out_ref[:, at] = total.astype(BF)


def fold_weight(core, own, sib, values):
    value_rows, features = values.shape
    steps = 4
    rows, half = features // steps, features // 2
    block = pl.BlockSpec((rows, half), lambda i, core: (i, 0))
    return pl.pallas_call(
        fold_kernel,
        out_shape=jax.ShapeDtypeStruct((features, value_rows), BF),
        grid_spec=pltpu.PrefetchScalarGridSpec(
            num_scalar_prefetch=1,
            grid=(steps,),
            in_specs=[block, block, whole(values.shape)],
            out_specs=pl.BlockSpec((rows, value_rows), lambda i, core: (i, 0)),
            scratch_shapes=[pltpu.VMEM((half, value_rows), BF), pltpu.VMEM((half, value_rows), BF)],
        ),
        compiler_params=params(MB),
        cost_estimate=cost(1, 1),
    )(core.reshape(1), own, sib, values)


def serve_kernel(scale, x_hbm, fold_hbm, val_hbm, y_hbm, n_hbm, c_hbm, g_hbm, s_hbm,
                 x_buf, fold_buf, val_buf, n_buf, c_buf, id_buf, g_buf, s_buf, y_buf,
                 x_sem, f_sem, v_sem, y_sem, o_sem):
    rows = x_buf.shape[0]
    features = n_buf.shape[1]
    value_rows = val_buf.shape[0]
    parts = x_sem.shape[0]
    step_rows = rows // parts
    step_cols = value_rows // parts
    slots = rows // 2

    def x_copy(i):
        at = pl.ds(i * step_rows, step_rows)
        return pltpu.make_async_copy(x_hbm.at[at, :], x_buf.at[at, :], x_sem.at[i])

    def f_copy(i):
        return pltpu.make_async_copy(
            fold_hbm.at[:, pl.ds(i * step_cols, step_cols)], fold_buf.at[i], f_sem.at[i]
        )

    def v_copy(i):
        at = pl.ds(i * step_cols, step_cols)
        return pltpu.make_async_copy(val_hbm.at[at, :], val_buf.at[at, :], v_sem.at[i])

    for i in range(parts):
        x_copy(i).start()
    for i in range(parts):
        f_copy(i).start()
        v_copy(i).start()

    take = 32
    low = lax.broadcasted_iota(jnp.int32, (take // 16, 8, 1), 1) < SLOTS

    def split(x):
        pairs = x.astype(F32).reshape(take // 16, 16, x.shape[1])
        first, second = pairs[:, :8], pairs[:, 8:]
        upper = jnp.where(low, first, pltpu.roll(second, 4, 1))
        lower = jnp.where(low, pltpu.roll(first, 4, 1), second)
        return upper.reshape(take // 2, x.shape[1]), lower.reshape(take // 2, x.shape[1])

    for i in range(parts):
        x_copy(i).wait()

        @pl.loop(i * step_rows // take, (i + 1) * step_rows // take)
        def _(r):
            src = pl.ds(pl.multiple_of(r * take, take), take)
            dst = pl.ds(pl.multiple_of(r * (take // 2), take // 2), take // 2)
            upper, lower = split(x_buf[src, :features])
            n_buf[dst, :] = upper.astype(BF)
            c_buf[dst, :] = lower.astype(BF)
            ident, _ = split(x_buf[src, features:])
            id_buf[dst, :] = ident

    kept = [pltpu.make_async_copy(n_buf, n_hbm, o_sem.at[0]), pltpu.make_async_copy(c_buf, c_hbm, o_sem.at[1])]
    for copy in kept:
        copy.start()

    for j in range(parts):
        f_copy(j).wait()
        v_copy(j).wait()
        scores = nn(n_buf[...], fold_buf[j]) * scale
        cot_scores = nt(c_buf[...], val_buf[j * step_cols : (j + 1) * step_cols, :])
        sig = 1.0 / (1.0 + jnp.exp(-scores))
        block_of = (lax.broadcasted_iota(jnp.int32, (1, step_cols), 1) // BLOCK + j * (step_cols // BLOCK)).astype(F32)
        mine = id_buf[:, :1] == block_of
        g_buf[j] = jnp.where(mine, sig, 0.0).astype(BF)
        s_buf[j] = jnp.where(mine, cot_scores * sig * (1.0 - sig) * scale, 0.0).astype(BF)
        at = pl.ds(j * step_cols, step_cols)
        kept.append(pltpu.make_async_copy(g_buf.at[j], g_hbm.at[:, at], o_sem.at[2 + j]))
        kept.append(pltpu.make_async_copy(s_buf.at[j], s_hbm.at[:, at], o_sem.at[2 + parts + j]))
        kept[-2].start()
        kept[-1].start()

    tiles = y_sem.shape[0]
    width = features // tiles
    lows = lax.broadcasted_iota(jnp.int32, (slots // 8, 8, 1), 1) < SLOTS

    def y_copy(i):
        at = pl.ds(pl.multiple_of(i * width, width), width)
        return pltpu.make_async_copy(y_buf.at[i], y_hbm.at[:, at], y_sem.at[i])

    @pl.loop(0, tiles)
    def _(i):
        at = pl.ds(pl.multiple_of(i * width, width), width)
        read = nn(g_buf[0], val_buf[0:step_cols, at])
        grad = nt(s_buf[0], fold_buf[0, at, :])
        for j in range(1, parts):
            read += nn(g_buf[j], val_buf[j * step_cols : (j + 1) * step_cols, at])
            grad += nt(s_buf[j], fold_buf[j, at, :])
        read = read.reshape(slots // 8, 8, width)
        grad = grad.reshape(slots // 8, 8, width)
        first = jnp.where(lows, read, pltpu.roll(grad, 4, 1))
        second = jnp.where(lows, pltpu.roll(read, 4, 1), grad)
        y_buf[i] = jnp.concatenate([first, second], axis=1).reshape(rows, width).astype(BF)
        y_copy(i).start()

    for copy in kept:
        copy.wait()
    for i in range(tiles):
        y_copy(i).wait()


def serve(x, fold, values, features):
    rows = x.shape[0]
    slots = rows // 2
    value_rows = values.shape[0]
    parts, tiles = 4, 8
    step_cols = value_rows // parts
    any_spec = pl.BlockSpec(memory_space=pl.ANY)
    return pl.pallas_call(
        functools.partial(serve_kernel, float(features) ** (-0.5)),
        out_shape=(
            jax.ShapeDtypeStruct((rows, features), BF),
            jax.ShapeDtypeStruct((slots, features), BF),
            jax.ShapeDtypeStruct((slots, features), BF),
            jax.ShapeDtypeStruct((slots, value_rows), BF),
            jax.ShapeDtypeStruct((slots, value_rows), BF),
        ),
        in_specs=[any_spec] * 3,
        out_specs=(any_spec,) * 5,
        scratch_shapes=[
            pltpu.VMEM(x.shape, BF),
            pltpu.VMEM((parts, features, step_cols), BF),
            pltpu.VMEM(values.shape, BF),
            pltpu.VMEM((slots, features), BF),
            pltpu.VMEM((slots, features), BF),
            pltpu.VMEM((slots, LANES), F32),
            pltpu.VMEM((parts, slots, step_cols), BF),
            pltpu.VMEM((parts, slots, step_cols), BF),
            pltpu.VMEM((tiles, rows, features // tiles), BF),
            pltpu.SemaphoreType.DMA((parts,)),
            pltpu.SemaphoreType.DMA((parts,)),
            pltpu.SemaphoreType.DMA((parts,)),
            pltpu.SemaphoreType.DMA((tiles,)),
            pltpu.SemaphoreType.DMA((2 + 2 * parts,)),
        ],
        compiler_params=params(MB),
        cost_estimate=cost(4 * rows * value_rows * features, 20 << 20),
    )(x, fold, values)


def grad_kernel(half, core_ref, own_ref, sib_ref, n_ref, c_ref, g_ref, s_ref, out_ref, gt_ref, st_ref):
    slots = n_ref.shape[0]
    tile = 256

    @pl.when(pl.program_id(0) == 0)
    def _():
        for i in range(0, slots, tile):
            gt_ref[:, i : i + tile] = g_ref[i : i + tile, :].T
            st_ref[:, i : i + tile] = s_ref[i : i + tile, :].T

    def use(w_ref):
        queries = nn(n_ref[...], w_ref[...]).astype(BF)
        for i in range(0, out_ref.shape[0], tile):
            total = nn(gt_ref[i : i + tile, :], c_ref[...]) + nn(st_ref[i : i + tile, :], queries)
            out_ref[i : i + tile, :] = total.astype(BF)

    with_slice(half, own_ref, sib_ref, use)


def value_grads(core, own, sib, n, c, g, s):
    half = 4
    features, width = own.shape[0], own.shape[1] // half
    slots, value_rows = g.shape
    return pl.pallas_call(
        functools.partial(grad_kernel, half),
        out_shape=jax.ShapeDtypeStruct((value_rows, features), BF),
        grid_spec=pltpu.PrefetchScalarGridSpec(
            num_scalar_prefetch=1,
            grid=(2 * half,),
            in_specs=slice_specs(half, features, width)
            + [
                whole(n.shape),
                pl.BlockSpec((slots, width), lambda a, core: (0, slice_at(a, core[0], half))),
                whole(g.shape),
                whole(s.shape),
            ],
            out_specs=pl.BlockSpec((value_rows, width), lambda a, core: (0, slice_at(a, core[0], half))),
            scratch_shapes=[pltpu.VMEM((value_rows, slots), BF), pltpu.VMEM((value_rows, slots), BF)],
        ),
        compiler_params=params(MB),
        cost_estimate=cost(6 * slots * value_rows * features, 24 << 20),
    )(core, own, sib, n, c, g, s)


def home_kernel(back_ref, tgt_ref, wgt_ref, tok_ref, cot_ref, gain_ref, out_ref, grad_ref, pick_ref, acc_ref, rms_ref, sum_ref):
    step = pl.program_id(0)
    count, features = tok_ref.shape
    rows, width = back_ref.shape

    @pl.when(step == 0)
    def _():
        number = lax.broadcasted_iota(jnp.int32, (count, rows), 1)
        targets = tgt_ref[...]
        t0, t1 = targets[:, :1], targets[:, 1:]
        one = lambda hit: jnp.where(hit, 1.0, 0.0).astype(BF)
        pick_ref[:count, :] = one(number == t0)
        pick_ref[count : 2 * count, :] = one(number == t1)
        pick_ref[2 * count :, :] = one((number == t0 + SLOTS) | (number == t1 + SLOTS))
        exact = tok_ref[...].astype(F32)
        rms_ref[...] = lax.rsqrt(jnp.mean(exact * exact, axis=1, keepdims=True) + 1e-06)
        sum_ref[...] = jnp.zeros_like(sum_ref)

    at = pl.ds(pl.multiple_of(step * width, width), width)
    weights = wgt_ref[...]
    got = nn(pick_ref[...], back_ref[...])
    exact = tok_ref[:, at].astype(F32)
    out_ref[...] = exact + (weights[:, :1] * got[:count] + weights[:, 1:] * got[count : 2 * count])
    unit_grad = got[2 * count :] * gain_ref[:, at]
    acc_ref[:, at] = unit_grad
    rms = rms_ref[...]
    sum_ref[...] += jnp.sum(unit_grad * (exact * rms), axis=1, keepdims=True)

    @pl.when(step == pl.num_programs(0) - 1)
    def _():
        mean = sum_ref[...] * (1.0 / features)
        for i in range(0, features, width):
            cols = slice(i, i + width)
            unit = tok_ref[:, cols].astype(F32) * rms
            grad_ref[:, cols] = cot_ref[:, cols].astype(F32) + rms * (acc_ref[:, cols] - unit * mean)


def finish(back, targets, weights, tokens, cot, gain):
    count, features = tokens.shape
    rows = back.shape[0]
    steps = 4
    width = features // steps
    return pl.pallas_call(
        home_kernel,
        out_shape=(
            jax.ShapeDtypeStruct((count, features), F32),
            jax.ShapeDtypeStruct((count, features), F32),
        ),
        grid=(steps,),
        in_specs=[
            pl.BlockSpec((rows, width), lambda i: (0, i)),
            whole((count, 2)),
            whole((count, 2)),
            whole(tokens.shape),
            whole(cot.shape),
            whole((1, features)),
        ],
        out_specs=(pl.BlockSpec((count, width), lambda i: (0, i)), whole((count, features))),
        scratch_shapes=[
            pltpu.VMEM((3 * count, rows), BF),
            pltpu.VMEM((count, features), F32),
            pltpu.VMEM((count, 1), F32),
            pltpu.VMEM((count, 1), F32),
        ],
        compiler_params=params(MB),
        cost_estimate=cost(6 * count * rows * features, 10 << 20),
    )(back, targets, weights, tokens, cot, gain)


def exchange(rows):
    return lax.all_to_all(rows, ALL, split_axis=0, concat_axis=0, tiled=True)


def body(tokens, norm_gain, query_weight, values, blocks, weights, out_cotangent):
    features = tokens.shape[1]
    owners = lax.axis_size(ALL)
    core = lax.axis_index("core").astype(jnp.int32)
    gain = norm_gain.reshape(1, features)
    payload, targets = build_payload(
        tokens, gain, blocks, weights, out_cotangent, owners, values.shape[0] // BLOCK
    )
    got = exchange(payload)
    own = gather_own(query_weight, targets)
    sib = lax.ppermute(own, "core", [(0, 1), (1, 0)])
    fold = fold_weight(core, own, sib, values)
    answers, n, c, g, s = serve(got, fold, values, features)
    back = exchange(answers)
    grad_values = value_grads(core.reshape(1), own, sib, n, c, g, s)
    layer_out, grad_tokens = finish(back, targets, weights, tokens, out_cotangent, gain)
    return layer_out, grad_tokens, grad_values


def solution(mesh):
    fine = Mesh(np.asarray(mesh.devices).reshape(4, 2, 4, 4), ALL)
    rows = P(ALL, None)
    return jax.shard_map(
        body,
        mesh=fine,
        in_specs=(rows, P(), P(None, ("x", "core")), rows, rows, rows, rows),
        out_specs=(rows, rows, rows),
        check_vma=False,
    )
```

time: 230 us -> 330 us (1.43)
  Pallas kernels: 81.6 us -> 196 us
  starting transfers between devices: 16.5 us -> 40.5 us
  waiting for transfers between devices: 99.6 us -> 85.4 us
  between operations: 14.1 us -> 0.87 us
  local copies, waits for them, and re-layouts: 17.2 us -> 5.35 us
    pallas_call x2 -> x3, Pallas kernels: 42.5 us -> 150 us  [the longest x1 129 us: gather_own(): pl.pallas_call(assemble_kernel, out_shape=jax.ShapeDtypeStruct((features,...]
    ppermute x1 -> x13, waiting for transfers between devices: 0.01 us -> 57.2 us  [the longest x12 50.1 us: ring(): lax.ppermute(rows, axis, [(i, (i + by) % size) for i in range(size)])]
    all_gather x1 -> x0, waiting for transfers between devices: 50.5 us -> none  [gather_weight(): own = lax.all_gather(query_weight, 'x', axis=0, tiled=False)]
    all_to_all x2, waiting for transfers between devices: 48.4 us -> 28.2 us  [exchange(): return lax.all_to_all(rows, ALL, split_axis=0, concat_axis=0, tiled=True)]
    ppermute x1 -> x13, starting transfers between devices: 0.73 us -> 19.6 us  [the longest x12 18.2 us: ring(): lax.ppermute(rows, axis, [(i, (i + by) % size) for i in range(size)])]
    unnamed x26 -> x22, local copies, waits for them, and re-layouts: 17.2 us -> 4.26 us
    all_to_all x2, starting transfers between devices: 15.7 us -> 20.9 us  [exchange(): return lax.all_to_all(rows, ALL, split_axis=0, concat_axis=0, tiled=True)]
    pallas_call x1, Pallas kernels: 19.1 us -> 23.8 us  [value_grads(): pl.pallas_call(functools.partial(grad_kernel, half), out_shape=jax.ShapeD...]
  transfers between devices with their start and end apart: 4 -> 15, of which waited for: 3 -> 5; matrix products, arithmetic and copies ran while one was open for 1% -> 1% of each run, Pallas kernels for 23% -> 53%
where the time goes in v1:
time: 330 us; the launch traced here: 329 us
  Pallas kernels  196 us (59%)
  waiting for transfers between devices  85.4 us (26%)
  starting transfers between devices  40.5 us (12%)
  local copies, waits for them, and re-layouts  5.35 us (2%)
    pallas_call x1, Pallas kernels, gather_own(): pl.pallas_call(assemble_kernel, out_shape=jax.ShapeDtypeStruct((features,...  129 us
    ppermute x12, waiting for transfers between devices, ring(): lax.ppermute(rows, axis, [(i, (i + by) % size) for i in range(size)])  50.1 us
    all_to_all x2, waiting for transfers between devices, exchange(): return lax.all_to_all(rows, ALL, split_axis=0, concat_axis=0, tiled=True)  28.2 us
    pallas_call x1, Pallas kernels, value_grads(): pl.pallas_call(functools.partial(grad_kernel, half), out_shape=jax.ShapeD...  23.8 us
    all_to_all x2, starting transfers between devices, exchange(): return lax.all_to_all(rows, ALL, split_axis=0, concat_axis=0, tiled=True)  20.9 us
    ppermute x12, starting transfers between devices, ring(): lax.ppermute(rows, axis, [(i, (i + by) % size) for i in range(size)])  18.2 us
    pallas_call x1, Pallas kernels, serve(): pl.pallas_call(functools.partial(serve_kernel, float(features) ** (-0.5))...  16.9 us
    pallas_call x1, Pallas kernels, fold_weight(): pl.pallas_call(fold_kernel, out_shape=jax.ShapeDtypeStruct((features, val...  14.4 us
  transfers between devices with their start and end apart: 15, of which 5 were waited for; matrix products, arithmetic and copies ran while one was open for 1% of the time, Pallas kernels for 53%

profile of v1, /device:TPU:7, one launch (start us, length us, event | category | flops | bytes accessed | tf_op | source)
XLA Modules:
  0.0 329.1 jit_solution(5072302020460331972)
XLA Ops:
  0.6 1.0 constant_dynamic-slice_fusion.1
  1.7 0.6 collective-permute-start.1
  2.3 2.1 collective-permute-start
  4.4 1.4 copy.11.wgt_ref
  5.8 1.4 copy.10.blk_ref
  7.2 5.5 %shard_map.94 = (bf16[1024,2176]{1,0:T(8,128)(2,1)}, s32[128,2]{1,0:T(8,128)}) custom-call(bf16[128,2048]{1,0:T(8,128)(2,1)} %tok_ref.3, f32[1,2048]{1,0:T(1,128)} %bitcast.11, s32[128,2]{1,0:T(8,128)} %copy.10.blk_ref, f32[128,2]{1,0:T(8,128)} %copy.11.wgt_ref, bf16[128,2048]{1,0:T(8,128)(2,1)} %cot_ref.3), custom_call_target="tpu_custom_call" | custom-call | flops 1073741824 | bytes 6291456 | tf_op jit(solution)/shard_map/pallas_call | solution.py:111
  12.8 0.0 collective-permute-done.1
  12.8 0.0 collective-permute-done
  12.8 0.1 collective-permute-start.7
  12.9 2.7 collective-permute-start.2
  15.6 2.3 collective-permute-done.7
  17.9 0.0 copy-start
  17.9 3.8 %collective-permute-start.9 = (bf16[256,768]{1,0:T(8,128)(2,1)S(1)}, bf16[256,768]{1,0:T(8,128)(2,1)S(1)}, u32[]{:S(2)}, u32[]{:S(2)}) collective-permute-start(bf16[256,768]{1,0:T(8,128)(2,1)S(1)} %pad_maximum_fusion.1.refs_5_), channel_id=1, source_target_pairs={{0,12},{4,0},{8,4},{12,8},{1,13},{5,1},{9,5},{13,9},{2,14},{6,2},{... | collective-permute-start | bytes 1179656 | tf_op jit(solution)/shard_map/ppermute | solution.py:136
  21.8 0.0 collective-permute-start.8
  21.8 0.0 collective-permute-done.2
  21.8 0.0 copy-start.1
  21.8 2.8 collective-permute-start.4
  24.6 0.0 collective-permute-start.3
  24.6 0.0 copy-done
  24.6 0.0 copy-done.1
  24.6 12.4 %all-to-all-start = ((bf16[128,8,2176]{2,1,0:T(8,128)(2,1)}), bf16[128,8,2176]{2,1,0:T(8,128)(2,1)}, u32[]{:S(2)}, u32[]{:S(2)}) async-start(bf16[128,8,2176]{2,1,0:T(8,128)(2,1)} %bitcast.9), calls=%async_computation | async-start | bytes 8912896 | tf_op jit(solution)/shard_map/all_to_all | solution.py:540
  37.1 0.0 collective-permute-done.9.refs_7_
  37.1 0.0 copy-start.2
  37.1 3.2 collective-permute-start.11
  40.3 0.0 collective-permute-done.8.refs_6_
  40.3 0.0 copy-start.3
  40.3 0.1 collective-permute-start.10
  40.4 0.0 collective-permute-done.4.refs_2_
  40.4 0.0 copy-start.4
  40.4 2.7 collective-permute-start.6
  43.1 0.0 collective-permute-done.3.refs_1_
  43.1 0.0 copy-start.5
  43.1 0.1 collective-permute-start.5
  43.2 0.6 pad_add_fusion.at_ref
  43.8 45.2 %collective-permute-done.11.refs_9_ = bf16[128,768]{1,0:T(8,128)(2,1)S(1)} collective-permute-done((bf16[128,768]{1,0:T(8,128)(2,1)S(1)}, bf16[128,768]{1,0:T(8,128)(2,1)S(1)}, u32[]{:S(2)}, u32[]{:S(2)}) %collective-permute-start.11) | collective-permute-done | bytes 196640 | tf_op jit(solution)/shard_map/ppermute | solution.py:136
  89.0 0.0 copy-start.6
  89.0 2.6 collective-permute-done.10.refs_8_
  91.6 0.0 copy-start.7
  91.6 0.0 collective-permute-done.6.refs_4_
  91.6 0.0 copy-start.8
  91.6 0.0 collective-permute-done.5.refs_3_
  91.6 0.0 copy-done.2
  91.6 0.0 copy-done.3
  91.6 0.0 copy-done.4
  91.6 0.0 copy-done.5
  91.6 0.0 copy-done.6
  91.7 0.6 copy-done.7
  92.3 0.1 copy-done.8
  92.4 0.0 copy-start.9
  92.4 0.7 copy-done.9
  93.1 129.1 %shard_map.95.own_ref = bf16[2048,1024]{1,0:T(8,128)(2,1)} custom-call(s32[3]{0:T(128)} %pad_add_fusion.at_ref, bf16[2048,256]{1,0:T(8,128)(2,1)} %w_ref.1, bf16[256,768]{1,0:T(8,128)(2,1)} %copy-done.1, bf16[256,768]{1,0:T(8,128)(2,1)} %copy-done.5, bf16[256,768]{1,0:T(8,128)(2,1)} %copy-done.4, bf16[128,768]{1,0:T(8,128)(2,1)} %copy-done.9, ...), custom_call_target="tpu_custom_call" | custom-call | flops 1 | bytes 1 | tf_op jit(solution)/shard_map/pallas_call | solution.py:212
  222.2 1.4 collective-permute-start.12
  223.6 7.1 %collective-permute-done.12.sib_ref = bf16[2048,1024]{1,0:T(8,128)(2,1)} collective-permute-done((bf16[2048,1024]{1,0:T(8,128)(2,1)}, bf16[2048,1024]{1,0:T(8,128)(2,1)}, u32[]{:S(2)}, u32[]{:S(2)}) %collective-permute-start.12) | collective-permute-done | bytes 4194336 | tf_op jit(solution)/shard_map/ppermute | solution.py:553
  230.7 14.4 %shard_map.96.fold_hbm = bf16[2048,1024]{1,0:T(8,128)(2,1)} custom-call(s32[1]{0:T(128)} %bitcast.3.core_ref, bf16[2048,1024]{1,0:T(8,128)(2,1)} %shard_map.95.own_ref, bf16[2048,1024]{1,0:T(8,128)(2,1)} %collective-permute-done.12.sib_ref, bf16[1024,2048]{1,0:T(8,128)(2,1)} %val_hbm.1), custom_call_target="tpu_custom_call" | custom-call | flops 1 | bytes 1 | tf_op jit(solution)/shard_map/pallas_call | solution.py:270
  245.1 0.0 all-to-all-done
  245.1 16.9 %shard_map.97 = (bf16[1024,2048]{1,0:T(8,128)(2,1)}, bf16[512,2048]{1,0:T(8,128)(2,1)}, bf16[512,2048]{1,0:T(8,128)(2,1)}, bf16[512,1024]{1,0:T(8,128)(2,1)}, bf16[512,1024]{1,0:T(8,128)(2,1)}) custom-call(bf16[1024,2176]{1,0:T(8,128)(2,1)} %bitcast.2.x_hbm, bf16[2048,1024]{1,0:T(8,128)(2,1)} %shard_map.96.fold_hbm, bf16[1024,2048]{1,0:T(8,128)(2,1)} %val_hbm.1), custom_call_target="tpu_custom_call" | custom-call | flops 8589934592 | bytes 20971520 | tf_op jit(solution)/shard_map/pallas_call | solution.py:394
  262.0 8.5 %all-to-all-start.1 = ((bf16[128,8,2048]{2,1,0:T(8,128)(2,1)}), bf16[128,8,2048]{2,1,0:T(8,128)(2,1)}, u32[]{:S(2)}, u32[]{:S(2)}) async-start(bf16[128,8,2048]{2,1,0:T(8,128)(2,1)} %bitcast.10), calls=%async_computation.1 | async-start | bytes 8388608 | tf_op jit(solution)/shard_map/all_to_all | solution.py:540
  270.5 23.8 %shard_map.99 = bf16[1024,2048]{1,0:T(8,128)(2,1)} custom-call(s32[1]{0:T(128)} %bitcast.3.core_ref, bf16[2048,1024]{1,0:T(8,128)(2,1)} %shard_map.95.own_ref, bf16[2048,1024]{1,0:T(8,128)(2,1)} %collective-permute-done.12.sib_ref, bf16[512,2048]{1,0:T(8,128)(2,1)} %get-tuple-element.21.n_ref, bf16[512,2048]{1,0:T(8,128)(2,1)} %get-tuple-element.22.c_ref, ...), custom_call_target="tpu_custom_call" | custom-call | flops 6442450944 | bytes 25165824 | tf_op jit(solution)/shard_map/pallas_call | solution.py:449
  294.2 28.2 %all-to-all-done.1 = bf16[128,8,2048]{2,1,0:T(8,128)(2,1)} async-done(((bf16[128,8,2048]{2,1,0:T(8,128)(2,1)}), bf16[128,8,2048]{2,1,0:T(8,128)(2,1)}, u32[]{:S(2)}, u32[]{:S(2)}) %all-to-all-start.1) | async-done | bytes 4194336 | tf_op jit(solution)/shard_map/all_to_all | solution.py:540
  322.4 6.7 %shard_map.98 = (f32[128,2048]{1,0:T(8,128)}, f32[128,2048]{1,0:T(8,128)}) custom-call(bf16[1024,2048]{1,0:T(8,128)(2,1)} %bitcast.8.back_ref, s32[128,2]{1,0:T(8,128)} %get-tuple-element.15.tgt_ref, f32[128,2]{1,0:T(8,128)} %copy.11.wgt_ref, bf16[128,2048]{1,0:T(8,128)(2,1)} %tok_ref.3, bf16[128,2048]{1,0:T(8,128)(2,1)} %cot_ref.3, f32[1,2048]{1,0:T(1,128)} %bitcast.12), custom_call_target="tpu_custom_call" | custom-call | flops 1610612736 | bytes 10485760 | tf_op jit(solution)/shard_map/pallas_call | solution.py:512
  (9 shorter events, 0.2 us)
Async XLA Ops:
  1.7 11.1 %collective-permute-start.1 = (bf16[512,256]{1,0:T(8,128)(2,1)S(1)}, bf16[512,256]{1,0:T(8,128)(2,1)S(1)}, u32[]{:S(2)}, u32[]{:S(2)}) collective-permute-start(bf16[512,256]{1,0:T(8,128)(2,1)S(1)} %pad_maximum_fusion.2), channel_id=1, source_target_pairs={{0,96},{32,0},{64,32},{96,64},{1,97},{33,1},{65,33},{97,65},{2,98}... | collective-permute-start | bytes 786440 | tf_op jit(solution)/shard_map/ppermute | solution.py:136
  2.3 10.5 %collective-permute-start = (bf16[512,256]{1,0:T(8,128)(2,1)S(1)}, bf16[512,256]{1,0:T(8,128)(2,1)S(1)}, u32[]{:S(2)}, u32[]{:S(2)}) collective-permute-start(bf16[512,256]{1,0:T(8,128)(2,1)S(1)} %pad_maximum_fusion.2), channel_id=1, source_target_pairs={{0,32},{32,64},{64,96},{96,0},{1,33},{33,65},{65,97},{97,1},{2,34}... | collective-permute-start | bytes 786440 | tf_op jit(solution)/shard_map/ppermute | solution.py:136
  12.8 5.1 %collective-permute-start.7 = (bf16[256,256]{1,0:T(8,128)(2,1)S(1)}, bf16[256,256]{1,0:T(8,128)(2,1)S(1)}, u32[]{:S(2)}, u32[]{:S(2)}) collective-permute-start(bf16[256,256]{1,0:T(8,128)(2,1)S(1)} %get-tuple-element.29), channel_id=1, source_target_pairs={{0,96},{32,0},{64,32},{96,64},{1,97},{33,1},{65,33},{97,65},{2,98}... | collective-permute-start | bytes 393224 | tf_op jit(solution)/shard_map/ppermute | solution.py:136
  12.9 8.9 %collective-permute-start.2 = (bf16[256,256]{1,0:T(8,128)(2,1)S(1)}, bf16[256,256]{1,0:T(8,128)(2,1)S(1)}, u32[]{:S(2)}, u32[]{:S(2)}) collective-permute-start(bf16[256,256]{1,0:T(8,128)(2,1)S(1)} %get-tuple-element.28), channel_id=1, source_target_pairs={{0,32},{32,64},{64,96},{96,0},{1,33},{33,65},{65,97},{97,1},{2,34}... | collective-permute-start | bytes 393224 | tf_op jit(solution)/shard_map/ppermute | solution.py:136
  17.9 6.7 %copy-start = (bf16[256,768]{1,0:T(8,128)(2,1)}, bf16[256,768]{1,0:T(8,128)(2,1)S(1)}, u32[]{:S(2)}) copy-start(bf16[256,768]{1,0:T(8,128)(2,1)S(1)} %pad_maximum_fusion.1.refs_5_) | copy-start | bytes 1179652
  17.9 19.1 %collective-permute-start.9 = (bf16[256,768]{1,0:T(8,128)(2,1)S(1)}, bf16[256,768]{1,0:T(8,128)(2,1)S(1)}, u32[]{:S(2)}, u32[]{:S(2)}) collective-permute-start(bf16[256,768]{1,0:T(8,128)(2,1)S(1)} %pad_maximum_fusion.1.refs_5_), channel_id=1, source_target_pairs={{0,12},{4,0},{8,4},{12,8},{1,13},{5,1},{9,5},{13,9},{2,14},{6,2},{... | collective-permute-start | bytes 1179656 | tf_op jit(solution)/shard_map/ppermute | solution.py:136
  21.8 18.5 %collective-permute-start.8 = (bf16[256,768]{1,0:T(8,128)(2,1)S(1)}, bf16[256,768]{1,0:T(8,128)(2,1)S(1)}, u32[]{:S(2)}, u32[]{:S(2)}) collective-permute-start(bf16[256,768]{1,0:T(8,128)(2,1)S(1)} %pad_maximum_fusion.1.refs_5_), channel_id=1, source_target_pairs={{0,4},{4,8},{8,12},{12,0},{1,5},{5,9},{9,13},{13,1},{2,6},{6,10},{... | collective-permute-start | bytes 1179656 | tf_op jit(solution)/shard_map/ppermute | solution.py:136
  21.8 2.8 copy-start.1
  21.8 18.6 %collective-permute-start.4 = (bf16[256,768]{1,0:T(8,128)(2,1)S(1)}, bf16[256,768]{1,0:T(8,128)(2,1)S(1)}, u32[]{:S(2)}, u32[]{:S(2)}) collective-permute-start(bf16[256,768]{1,0:T(8,128)(2,1)S(1)} %pad_maximum_fusion.refs_0_), channel_id=1, source_target_pairs={{0,3},{1,0},{2,1},{3,2},{4,7},{5,4},{6,5},{7,6},{8,11},{9,8},{10,9... | collective-permute-start | bytes 1179656 | tf_op jit(solution)/shard_map/ppermute | solution.py:136
  24.6 18.5 %collective-permute-start.3 = (bf16[256,768]{1,0:T(8,128)(2,1)S(1)}, bf16[256,768]{1,0:T(8,128)(2,1)S(1)}, u32[]{:S(2)}, u32[]{:S(2)}) collective-permute-start(bf16[256,768]{1,0:T(8,128)(2,1)S(1)} %pad_maximum_fusion.refs_0_), channel_id=1, source_target_pairs={{0,1},{1,2},{2,3},{3,0},{4,5},{5,6},{6,7},{7,4},{8,9},{9,10},{10,1... | collective-permute-start | bytes 1179656 | tf_op jit(solution)/shard_map/ppermute | solution.py:136
  24.6 220.5 %all-to-all-start = ((bf16[128,8,2176]{2,1,0:T(8,128)(2,1)}), bf16[128,8,2176]{2,1,0:T(8,128)(2,1)}, u32[]{:S(2)}, u32[]{:S(2)}) async-start(bf16[128,8,2176]{2,1,0:T(8,128)(2,1)} %bitcast.9), calls=%async_computation | async-start | bytes 8912896 | tf_op jit(solution)/shard_map/all_to_all | solution.py:540
  37.1 54.5 %copy-start.2 = (bf16[256,768]{1,0:T(8,128)(2,1)}, bf16[256,768]{1,0:T(8,128)(2,1)S(1)}, u32[]{:S(2)}) copy-start(bf16[256,768]{1,0:T(8,128)(2,1)S(1)} %collective-permute-done.9.refs_7_) | copy-start | bytes 1179652
  37.1 51.9 %collective-permute-start.11 = (bf16[128,768]{1,0:T(8,128)(2,1)S(1)}, bf16[128,768]{1,0:T(8,128)(2,1)S(1)}, u32[]{:S(2)}, u32[]{:S(2)}) collective-permute-start(bf16[128,768]{1,0:T(8,128)(2,1)S(1)} %slice.37), channel_id=1, source_target_pairs={{0,12},{4,0},{8,4},{12,8},{1,13},{5,1},{9,5},{13,9},{2,14},{6,2},{... | collective-permute-start | bytes 589832 | tf_op jit(solution)/shard_map/ppermute | solution.py:136
  40.3 51.3 %copy-start.3 = (bf16[256,768]{1,0:T(8,128)(2,1)}, bf16[256,768]{1,0:T(8,128)(2,1)S(1)}, u32[]{:S(2)}) copy-start(bf16[256,768]{1,0:T(8,128)(2,1)S(1)} %collective-permute-done.8.refs_6_) | copy-start | bytes 1179652
  40.3 51.3 %collective-permute-start.10 = (bf16[128,768]{1,0:T(8,128)(2,1)S(1)}, bf16[128,768]{1,0:T(8,128)(2,1)S(1)}, u32[]{:S(2)}, u32[]{:S(2)}) collective-permute-start(bf16[128,768]{1,0:T(8,128)(2,1)S(1)} %slice.36), channel_id=1, source_target_pairs={{0,4},{4,8},{8,12},{12,0},{1,5},{5,9},{9,13},{13,1},{2,6},{6,10},{... | collective-permute-start | bytes 589832 | tf_op jit(solution)/shard_map/ppermute | solution.py:136
  40.4 51.2 %copy-start.4 = (bf16[256,768]{1,0:T(8,128)(2,1)}, bf16[256,768]{1,0:T(8,128)(2,1)S(1)}, u32[]{:S(2)}) copy-start(bf16[256,768]{1,0:T(8,128)(2,1)S(1)} %collective-permute-done.4.refs_2_) | copy-start | bytes 1179652
  40.4 51.2 %collective-permute-start.6 = (bf16[128,768]{1,0:T(8,128)(2,1)S(1)}, bf16[128,768]{1,0:T(8,128)(2,1)S(1)}, u32[]{:S(2)}, u32[]{:S(2)}) collective-permute-start(bf16[128,768]{1,0:T(8,128)(2,1)S(1)} %slice.35), channel_id=1, source_target_pairs={{0,3},{1,0},{2,1},{3,2},{4,7},{5,4},{6,5},{7,6},{8,11},{9,8},{10,9... | collective-permute-start | bytes 589832 | tf_op jit(solution)/shard_map/ppermute | solution.py:136
  43.1 48.5 %copy-start.5 = (bf16[256,768]{1,0:T(8,128)(2,1)}, bf16[256,768]{1,0:T(8,128)(2,1)S(1)}, u32[]{:S(2)}) copy-start(bf16[256,768]{1,0:T(8,128)(2,1)S(1)} %collective-permute-done.3.refs_1_) | copy-start | bytes 1179652
  43.1 48.5 %collective-permute-start.5 = (bf16[128,768]{1,0:T(8,128)(2,1)S(1)}, bf16[128,768]{1,0:T(8,128)(2,1)S(1)}, u32[]{:S(2)}, u32[]{:S(2)}) collective-permute-start(bf16[128,768]{1,0:T(8,128)(2,1)S(1)} %slice.34), channel_id=1, source_target_pairs={{0,1},{1,2},{2,3},{3,0},{4,5},{5,6},{6,7},{7,4},{8,9},{9,10},{10,1... | collective-permute-start | bytes 589832 | tf_op jit(solution)/shard_map/ppermute | solution.py:136
  89.0 2.7 copy-start.6
  91.6 0.7 copy-start.7
  91.6 0.8 copy-start.8
  92.4 0.7 copy-start.9
  222.2 8.5 %collective-permute-start.12 = (bf16[2048,1024]{1,0:T(8,128)(2,1)}, bf16[2048,1024]{1,0:T(8,128)(2,1)}, u32[]{:S(2)}, u32[]{:S(2)}) collective-permute-start(bf16[2048,1024]{1,0:T(8,128)(2,1)} %shard_map.95.own_ref), channel_id=1, source_target_pairs={{0,16},{16,0},{1,17},{17,1},{2,18},{18,2},{3,19},{19,3},{4,20},{20... | collective-permute-start | bytes 12582920 | tf_op jit(solution)/shard_map/ppermute | solution.py:553
  262.0 60.4 %all-to-all-start.1 = ((bf16[128,8,2048]{2,1,0:T(8,128)(2,1)}), bf16[128,8,2048]{2,1,0:T(8,128)(2,1)}, u32[]{:S(2)}, u32[]{:S(2)}) async-start(bf16[128,8,2048]{2,1,0:T(8,128)(2,1)} %bitcast.10), calls=%async_computation.1 | async-start | bytes 8388608 | tf_op jit(solution)/shard_map/all_to_all | solution.py:540

commit v2 on v1

--- a/solution.py
+++ b/solution.py
@@ -132,141 +132,47 @@
     )(tokens, gain, blocks, weights, cot)
 
 
-def ring(axis, size, by):
-    return lambda rows: lax.ppermute(rows, axis, [(i, (i + by) % size) for i in range(size)])
-
-
-def both_ways(axis, size, piece):
-    up, down = ring(axis, size, 1), ring(axis, size, -1)
-    half = piece.shape[0] // 2
-    before, after = up(piece), down(piece)
-    return before, after, up(before[:half]), down(after[half:])
-
-
-def assemble_kernel(at_ref, w_ref, *refs):
-    pieces, out_ref, sems = refs[:-2], refs[-2], refs[-1]
-    x, z, y = at_ref[0], at_ref[1], at_ref[2]
-    width = w_ref.shape[1]
-    half_rows = w_ref.shape[0] // 2
-    columns = [lax.rem(x + d, 4) for d in (3, 1, 2)]
-    copies = []
-
-    def add(src, row, column, rows):
-        copies.append(
-            pltpu.make_async_copy(
-                src,
-                out_ref.at[
-                    pl.ds(pl.multiple_of(row, 128), rows),
-                    pl.ds(pl.multiple_of(column * width, width), width),
-                ],
-                sems.at[len(copies)],
-            )
-        )
-
-    add(w_ref, 0, x, w_ref.shape[0])
-    for part, me in ((0, y), (1, z)):
-        mine, before, after, top, bottom = pieces[5 * part : 5 * part + 5]
-        rows = mine.shape[0]
-        base = part * half_rows
-        across = lax.rem(me + 2, 4) * rows
-        places = [
-            (mine, me * rows),
-            (before, lax.rem(me + 3, 4) * rows),
-            (after, lax.rem(me + 1, 4) * rows),
-            (top, across),
-            (bottom, across + rows // 2),
-        ]
-        for piece, row in places:
-            for k, column in enumerate(columns):
-                add(
-                    piece.at[:, k * width : (k + 1) * width],
-                    base + row,
-                    column,
-                    piece.shape[0],
-                )
-    for copy in copies:
-        copy.start()
-    for copy in copies:
-        copy.wait()
-
-
-def gather_own(weight, after_this):
-    features, width = weight.shape
-    half, rows = features // 2, features // 8
-    x, z, y = (lax.axis_index(n).astype(jnp.int32) for n in ("x", "z", "y"))
-    mine = jnp.concatenate(
-        [
-            lax.dynamic_slice(weight, (y * rows, 0), (rows, width)),
-            lax.dynamic_slice(weight, (half + z * rows, 0), (rows, width)),
-        ],
-        axis=0,
-    )
-    up, down = ring("x", 4, 1), ring("x", 4, -1)
-    before, after = up(mine), down(mine)
-    before, after, after_this = lax.optimization_barrier((before, after, after_this))
-    across_y, across_z = up(before[:rows]), down(after[rows:])
-    set_y = jnp.concatenate([before[:rows], after[:rows], across_y], axis=1)
-    set_z = jnp.concatenate([before[rows:], after[rows:], across_z], axis=1)
-    pieces = (set_y, *both_ways("y", 4, set_y), set_z, *both_ways("z", 4, set_z))
-    any_spec = pl.BlockSpec(memory_space=pl.ANY)
-    return pl.pallas_call(
-        assemble_kernel,
-        out_shape=jax.ShapeDtypeStruct((features, 4 * width), BF),
-        in_specs=[pl.BlockSpec(memory_space=pltpu.SMEM)] + [any_spec] * 11,
-        out_specs=any_spec,
-        scratch_shapes=[pltpu.SemaphoreType.DMA((31,))],
-        compiler_params=params(MB),
-        cost_estimate=cost(1, 1),
-    )(jnp.stack([x, z, y]), weight, *pieces)
-
-
-def slice_at(step, core, half):
-    return jnp.where(step < half, 2 * step + core, 2 * (step - half) + 1 - core)
-
-
-def slice_specs(half, features, width):
-    return [
-        pl.BlockSpec((features, width), lambda a, core: (0, jnp.minimum(a, half - 1))),
-        pl.BlockSpec((features, width), lambda a, core: (0, jnp.maximum(a - half, 0))),
-    ]
-
-
-def with_slice(half, own_ref, sib_ref, use):
-    step = pl.program_id(0)
-
-    @pl.when(step < half)
-    def _():
-        use(own_ref)
-
-    @pl.when(step >= half)
-    def _():
-        use(sib_ref)
-
-
-def fold_kernel(core_ref, own_ref, sib_ref, val_ref, out_ref, vt_own, vt_sib):
-    width = own_ref.shape[1] // 4
+def shifted(rows, by):
+    return lax.ppermute(rows, "x", [(i, (i + by) % 4) for i in range(4)])
+
+
+def gather_weight(weight):
+    own = jnp.stack([weight, shifted(weight, 1), shifted(weight, 3), shifted(weight, 2)])
+    return own, lax.ppermute(own, "core", [(0, 1), (1, 0)])
+
+
+def slice_at(step, at):
+    turn = jnp.where(step % 4 == 0, 0, jnp.where(step % 4 == 1, 3, step % 4 - 1))
+    return 2 * ((at[0] + turn) % 4) + jnp.where(step < 4, at[1], 1 - at[1])
+
+
+def fold_kernel(at_ref, own_ref, sib_ref, val_ref, out_ref, vt_ref, left_ref):
+    half, _, width = own_ref.shape
     tile = 256
 
     @pl.when(pl.program_id(0) == 0)
     def _():
-        core = core_ref[0]
-        for x in range(4):
-            to = slice(x * width, (x + 1) * width)
-            for vt, c in ((vt_own, core), (vt_sib, 1 - core)):
-                at = pl.ds(pl.multiple_of((2 * x + c) * width, width), width)
-                vt[to, :] = val_ref[:, at].T
-
+        for a in range(2 * half):
+            turn = (0, 3, 1, 2)[a % half]
+            parity = at_ref[1] if a < half else 1 - at_ref[1]
+            column = 2 * lax.rem(at_ref[0] + turn, 4) + parity
+            at = pl.ds(pl.multiple_of(column * width, width), width)
+            vt_ref[a * width : (a + 1) * width, :] = val_ref[:, at].T
+
+    for a in range(half):
+        left_ref[:, a * width : (a + 1) * width] = own_ref[a]
+        left_ref[:, (half + a) * width : (half + a + 1) * width] = sib_ref[a]
     for i in range(0, out_ref.shape[1], tile):
         at = slice(i, i + tile)
-        total = nn(own_ref[...], vt_own[:, at]) + nn(sib_ref[...], vt_sib[:, at])
-        out_ref[:, at] = total.astype(BF)
-
-
-def fold_weight(core, own, sib, values):
+        out_ref[:, at] = nn(left_ref[...], vt_ref[:, at]).astype(BF)
+
+
+def fold_weight(at, own, sib, values):
     value_rows, features = values.shape
+    half, _, width = own.shape
     steps = 4
-    rows, half = features // steps, features // 2
-    block = pl.BlockSpec((rows, half), lambda i, core: (i, 0))
+    rows = features // steps
+    block = pl.BlockSpec((half, rows, width), lambda i, at: (0, i, 0))
     return pl.pallas_call(
         fold_kernel,
         out_shape=jax.ShapeDtypeStruct((features, value_rows), BF),
@@ -274,12 +180,12 @@
             num_scalar_prefetch=1,
             grid=(steps,),
             in_specs=[block, block, whole(values.shape)],
-            out_specs=pl.BlockSpec((rows, value_rows), lambda i, core: (i, 0)),
-            scratch_shapes=[pltpu.VMEM((half, value_rows), BF), pltpu.VMEM((half, value_rows), BF)],
+            out_specs=pl.BlockSpec((rows, value_rows), lambda i, at: (i, 0)),
+            scratch_shapes=[pltpu.VMEM((features, value_rows), BF), pltpu.VMEM((rows, features), BF)],
         ),
         compiler_params=params(MB),
         cost_estimate=cost(1, 1),
-    )(core.reshape(1), own, sib, values)
+    )(at, own, sib, values)
 
 
 def serve_kernel(scale, x_hbm, fold_hbm, val_hbm, y_hbm, n_hbm, c_hbm, g_hbm, s_hbm,
@@ -423,7 +329,7 @@
     )(x, fold, values)
 
 
-def grad_kernel(half, core_ref, own_ref, sib_ref, n_ref, c_ref, g_ref, s_ref, out_ref, gt_ref, st_ref):
+def grad_kernel(at_ref, own_ref, sib_ref, n_ref, c_ref, g_ref, s_ref, out_ref, gt_ref, st_ref):
     slots = n_ref.shape[0]
     tile = 256
 
@@ -433,38 +339,36 @@
             gt_ref[:, i : i + tile] = g_ref[i : i + tile, :].T
             st_ref[:, i : i + tile] = s_ref[i : i + tile, :].T
 
-    def use(w_ref):
-        queries = nn(n_ref[...], w_ref[...]).astype(BF)
-        for i in range(0, out_ref.shape[0], tile):
-            total = nn(gt_ref[i : i + tile, :], c_ref[...]) + nn(st_ref[i : i + tile, :], queries)
-            out_ref[i : i + tile, :] = total.astype(BF)
-
-    with_slice(half, own_ref, sib_ref, use)
-
-
-def value_grads(core, own, sib, n, c, g, s):
-    half = 4
-    features, width = own.shape[0], own.shape[1] // half
+    weight = jnp.where(pl.program_id(0) < 4, own_ref[0], sib_ref[0])
+    queries = nn(n_ref[...], weight).astype(BF)
+    for i in range(0, out_ref.shape[0], tile):
+        total = nn(gt_ref[i : i + tile, :], c_ref[...]) + nn(st_ref[i : i + tile, :], queries)
+        out_ref[i : i + tile, :] = total.astype(BF)
+
+
+def value_grads(at, own, sib, n, c, g, s):
+    half, features, width = own.shape
     slots, value_rows = g.shape
     return pl.pallas_call(
-        functools.partial(grad_kernel, half),
+        grad_kernel,
         out_shape=jax.ShapeDtypeStruct((value_rows, features), BF),
         grid_spec=pltpu.PrefetchScalarGridSpec(
             num_scalar_prefetch=1,
             grid=(2 * half,),
-            in_specs=slice_specs(half, features, width)
-            + [
+            in_specs=[
+                pl.BlockSpec((1, features, width), lambda a, x: (jnp.minimum(a, half - 1), 0, 0)),
+                pl.BlockSpec((1, features, width), lambda a, x: (jnp.maximum(a - half, 0), 0, 0)),
                 whole(n.shape),
-                pl.BlockSpec((slots, width), lambda a, core: (0, slice_at(a, core[0], half))),
+                pl.BlockSpec((slots, width), lambda a, x: (0, slice_at(a, x))),
                 whole(g.shape),
                 whole(s.shape),
             ],
-            out_specs=pl.BlockSpec((value_rows, width), lambda a, core: (0, slice_at(a, core[0], half))),
+            out_specs=pl.BlockSpec((value_rows, width), lambda a, x: (0, slice_at(a, x))),
             scratch_shapes=[pltpu.VMEM((value_rows, slots), BF), pltpu.VMEM((value_rows, slots), BF)],
         ),
         compiler_params=params(MB),
         cost_estimate=cost(6 * slots * value_rows * features, 24 << 20),
-    )(core, own, sib, n, c, g, s)
+    )(at, own, sib, n, c, g, s)
 
 
 def home_kernel(back_ref, tgt_ref, wgt_ref, tok_ref, cot_ref, gain_ref, out_ref, grad_ref, pick_ref, acc_ref, rms_ref, sum_ref):
@@ -543,18 +447,17 @@
 def body(tokens, norm_gain, query_weight, values, blocks, weights, out_cotangent):
     features = tokens.shape[1]
     owners = lax.axis_size(ALL)
-    core = lax.axis_index("core").astype(jnp.int32)
+    at = jnp.stack([lax.axis_index("x"), lax.axis_index("core")]).astype(jnp.int32)
     gain = norm_gain.reshape(1, features)
     payload, targets = build_payload(
         tokens, gain, blocks, weights, out_cotangent, owners, values.shape[0] // BLOCK
     )
+    own, sib = gather_weight(query_weight)
     got = exchange(payload)
-    own = gather_own(query_weight, targets)
-    sib = lax.ppermute(own, "core", [(0, 1), (1, 0)])
-    fold = fold_weight(core, own, sib, values)
+    fold = fold_weight(at, own, sib, values)
     answers, n, c, g, s = serve(got, fold, values, features)
     back = exchange(answers)
-    grad_values = value_grads(core.reshape(1), own, sib, n, c, g, s)
+    grad_values = value_grads(at, own, sib, n, c, g, s)
     layer_out, grad_tokens = finish(back, targets, weights, tokens, out_cotangent, gain)
     return layer_out, grad_tokens, grad_values
 

time: 330 us -> 185 us (0.56)
  Pallas kernels: 196 us -> 68.5 us
  starting transfers between devices: 40.5 us -> 21.9 us
    pallas_call x2 -> x1, Pallas kernels: 153 us -> 24.4 us  [value_grads(): pl.pallas_call(grad_kernel, out_shape=jax.ShapeDtypeStruct((value_rows, f...]
    all_to_all x2, waiting for transfers between devices: 28.2 us -> 53.2 us  [exchange(): return lax.all_to_all(rows, ALL, split_axis=0, concat_axis=0, tiled=True)]
    ppermute x13 -> x4, waiting for transfers between devices: 57.2 us -> 33.6 us  [the longest x3 27.2 us: shifted(): return lax.ppermute(rows, 'x', [(i, (i + by) % 4) for i in range(4)])]
    ppermute x13 -> x4, starting transfers between devices: 19.6 us -> 2.99 us  [the longest x3 2.4 us: shifted(): return lax.ppermute(rows, 'x', [(i, (i + by) % 4) for i in range(4)])]
    another operation x1 -> x2, other arithmetic: 0.59 us -> 3.9 us  [the longest x1 3.24 us: gather_weight(): jnp.stack([weight, shifted(weight, 1), shifted(weight, 3), shifted(weight...]
  transfers between devices with their start and end apart: 15 -> 6, of which waited for: 5 -> 6; matrix products, arithmetic and copies ran while one was open for 1% -> 4% of each run, Pallas kernels for 53% -> 24%
where the time goes in v2:
time: 185 us
  waiting for transfers between devices  86.8 us (47%)
  Pallas kernels  68.5 us (37%)
  starting transfers between devices  21.9 us (12%)
  other arithmetic  3.9 us (2%)
  local copies, waits for them, and re-layouts  2.82 us (2%)
    all_to_all x2, waiting for transfers between devices, exchange(): return lax.all_to_all(rows, ALL, split_axis=0, concat_axis=0, tiled=True)  53.2 us
    ppermute x3, waiting for transfers between devices, shifted(): return lax.ppermute(rows, 'x', [(i, (i + by) % 4) for i in range(4)])  27.2 us
    pallas_call x1, Pallas kernels, value_grads(): pl.pallas_call(grad_kernel, out_shape=jax.ShapeDtypeStruct((value_rows, f...  24.4 us
    all_to_all x2, starting transfers between devices, exchange(): return lax.all_to_all(rows, ALL, split_axis=0, concat_axis=0, tiled=True)  18.9 us
    pallas_call x1, Pallas kernels, serve(): pl.pallas_call(functools.partial(serve_kernel, float(features) ** (-0.5))...  16.9 us
    pallas_call x1, Pallas kernels, fold_weight(): pl.pallas_call(fold_kernel, out_shape=jax.ShapeDtypeStruct((features, val...  15.1 us
    pallas_call x1, Pallas kernels, finish(): pl.pallas_call(home_kernel, out_shape=(jax.ShapeDtypeStruct((count, featu...  6.73 us
    ppermute x1, waiting for transfers between devices, gather_weight(): return (own, lax.ppermute(own, 'core', [(0, 1), (1, 0)]))  6.47 us
  transfers between devices with their start and end apart: 6, of which 6 were waited for; matrix products, arithmetic and copies ran while one was open for 4% of the time, Pallas kernels for 24%

profile of v2, /device:TPU:7, one launch (start us, length us, event | category | flops | bytes accessed | tf_op | source)
XLA Modules:
  0.0 184.6 jit_solution(9364285449074018821)
XLA Ops:
  0.6 0.1 collective-permute-start
  0.7 2.3 %collective-permute-start.2 = (bf16[2048,256]{1,0:T(8,128)(2,1)}, bf16[2048,256]{1,0:T(8,128)(2,1)S(1)}, u32[]{:S(2)}, u32[]{:S(2)}) collective-permute-start(bf16[2048,256]{1,0:T(8,128)(2,1)} %param.9), channel_id=1, source_target_pairs={{0,64},{32,96},{64,0},{96,32},{1,65},{33,97},{65,1},{97,33},{2,66}... | collective-permute-start | bytes 3145736 | tf_op jit(solution)/shard_map/ppermute | solution.py:136
  3.0 0.0 collective-permute-start.1
  3.0 1.4 copy.11.wgt_ref
  4.4 1.4 copy.10.blk_ref
  5.9 5.4 %shard_map.94 = (bf16[1024,2176]{1,0:T(8,128)(2,1)}, s32[128,2]{1,0:T(8,128)}) custom-call(bf16[128,2048]{1,0:T(8,128)(2,1)} %tok_ref.3, f32[1,2048]{1,0:T(1,128)} %bitcast.16, s32[128,2]{1,0:T(8,128)} %copy.10.blk_ref, f32[128,2]{1,0:T(8,128)} %copy.11.wgt_ref, bf16[128,2048]{1,0:T(8,128)(2,1)} %cot_ref.3), custom_call_target="tpu_custom_call" | custom-call | flops 1073741824 | bytes 6291456 | tf_op jit(solution)/shard_map/pallas_call | solution.py:111
  11.3 0.0 copy-start
  11.3 12.1 %all-to-all-start = ((bf16[128,8,2176]{2,1,0:T(8,128)(2,1)}), bf16[128,8,2176]{2,1,0:T(8,128)(2,1)}, u32[]{:S(2)}, u32[]{:S(2)}) async-start(bf16[128,8,2176]{2,1,0:T(8,128)(2,1)} %bitcast.11), calls=%async_computation | async-start | bytes 8912896 | tf_op jit(solution)/shard_map/all_to_all | solution.py:444
  23.4 1.6 collective-permute-done
  24.9 1.3 collective-permute-done.2
  26.2 24.3 %collective-permute-done.1 = bf16[2048,256]{1,0:T(8,128)(2,1)} collective-permute-done((bf16[2048,256]{1,0:T(8,128)(2,1)}, bf16[2048,256]{1,0:T(8,128)(2,1)}, u32[]{:S(2)}, u32[]{:S(2)}) %collective-permute-start.1) | collective-permute-done | bytes 1048608 | tf_op jit(solution)/shard_map/ppermute | solution.py:136
  50.5 0.0 copy-done
  50.5 3.2 %pad_maximum_fusion.own_ref = bf16[4,2048,256]{2,1,0:T(8,128)(2,1)} fusion(bf16[1,2048,256]{2,1,0:T(8,128)(2,1)S(1)} %bitcast.15, bf16[1,2048,256]{2,1,0:T(8,128)(2,1)} %bitcast.7, bf16[1,2048,256]{2,1,0:T(8,128)(2,1)S(1)} %bitcast.14, bf16[1,2048,256]{2,1,0:T(8,128)(2,1)S(1)} %bitcast.13), kind=kLoop, calls=%fused_computation | loop fusion | flops 6291456 | bytes 8388608 | tf_op jit(solution)/shard_map/stack | solution.py:140
  53.8 0.6 collective-permute-start.3
  54.4 0.7 pad_add_fusion.at_ref
  55.0 6.5 %collective-permute-done.3.sib_ref = bf16[4,2048,256]{2,1,0:T(8,128)(2,1)} collective-permute-done((bf16[4,2048,256]{2,1,0:T(8,128)(2,1)}, bf16[4,2048,256]{2,1,0:T(8,128)(2,1)}, u32[]{:S(2)}, u32[]{:S(2)}) %collective-permute-start.3) | collective-permute-done | bytes 4194336 | tf_op jit(solution)/shard_map/ppermute | solution.py:141
  61.5 15.1 %shard_map.95.fold_hbm = bf16[2048,1024]{1,0:T(8,128)(2,1)} custom-call(s32[2]{0:T(128)} %pad_add_fusion.at_ref, bf16[4,2048,256]{2,1,0:T(8,128)(2,1)} %pad_maximum_fusion.own_ref, bf16[4,2048,256]{2,1,0:T(8,128)(2,1)} %collective-permute-done.3.sib_ref, bf16[1024,2048]{1,0:T(8,128)(2,1)} %val_hbm.1), custom_call_target="tpu_custom_call" | custom-call | flops 1 | bytes 1 | tf_op jit(solution)/shard_map/pallas_call | solution.py:176
  76.6 25.7 %all-to-all-done = bf16[128,8,2176]{2,1,0:T(8,128)(2,1)} async-done(((bf16[128,8,2176]{2,1,0:T(8,128)(2,1)}), bf16[128,8,2176]{2,1,0:T(8,128)(2,1)}, u32[]{:S(2)}, u32[]{:S(2)}) %all-to-all-start) | async-done | bytes 4456480 | tf_op jit(solution)/shard_map/all_to_all | solution.py:444
  102.3 16.9 %shard_map.96 = (bf16[1024,2048]{1,0:T(8,128)(2,1)}, bf16[512,2048]{1,0:T(8,128)(2,1)}, bf16[512,2048]{1,0:T(8,128)(2,1)}, bf16[512,1024]{1,0:T(8,128)(2,1)}, bf16[512,1024]{1,0:T(8,128)(2,1)}) custom-call(bf16[1024,2176]{1,0:T(8,128)(2,1)} %bitcast.2.x_hbm, bf16[2048,1024]{1,0:T(8,128)(2,1)} %shard_map.95.fold_hbm, bf16[1024,2048]{1,0:T(8,128)(2,1)} %val_hbm.1), custom_call_target="tpu_custom_call" | custom-call | flops 8589934592 | bytes 20971520 | tf_op jit(solution)/shard_map/pallas_call | solution.py:300
  119.2 6.8 %all-to-all-start.1 = ((bf16[128,8,2048]{2,1,0:T(8,128)(2,1)}), bf16[128,8,2048]{2,1,0:T(8,128)(2,1)}, u32[]{:S(2)}, u32[]{:S(2)}) async-start(bf16[128,8,2048]{2,1,0:T(8,128)(2,1)} %bitcast.12), calls=%async_computation.1 | async-start | bytes 8388608 | tf_op jit(solution)/shard_map/all_to_all | solution.py:444
  125.9 24.4 %shard_map.98 = bf16[1024,2048]{1,0:T(8,128)(2,1)} custom-call(s32[2]{0:T(128)} %pad_add_fusion.at_ref, bf16[4,2048,256]{2,1,0:T(8,128)(2,1)} %pad_maximum_fusion.own_ref, bf16[4,2048,256]{2,1,0:T(8,128)(2,1)} %collective-permute-done.3.sib_ref, bf16[512,2048]{1,0:T(8,128)(2,1)} %get-tuple-element.17.n_ref, bf16[512,2048]{1,0:T(8,128)(2,1)} %get-tuple-element.18.c_ref, ...), custom_call_target="tpu_custom_call" | custom-call | flops 6442450944 | bytes 25165824 | tf_op jit(solution)/shard_map/pallas_call | solution.py:352
  150.4 27.5 %all-to-all-done.1 = bf16[128,8,2048]{2,1,0:T(8,128)(2,1)} async-done(((bf16[128,8,2048]{2,1,0:T(8,128)(2,1)}), bf16[128,8,2048]{2,1,0:T(8,128)(2,1)}, u32[]{:S(2)}, u32[]{:S(2)}) %all-to-all-start.1) | async-done | bytes 4194336 | tf_op jit(solution)/shard_map/all_to_all | solution.py:444
  177.9 6.7 %shard_map.97 = (f32[128,2048]{1,0:T(8,128)}, f32[128,2048]{1,0:T(8,128)}) custom-call(bf16[1024,2048]{1,0:T(8,128)(2,1)} %bitcast.10.back_ref, s32[128,2]{1,0:T(8,128)} %get-tuple-element.14.tgt_ref, f32[128,2]{1,0:T(8,128)} %copy.11.wgt_ref, bf16[128,2048]{1,0:T(8,128)(2,1)} %tok_ref.3, bf16[128,2048]{1,0:T(8,128)(2,1)} %cot_ref.3, f32[1,2048]{1,0:T(1,128)} %bitcast.17), custom_call_target="tpu_custom_call" | custom-call | flops 1610612736 | bytes 10485760 | tf_op jit(solution)/shard_map/pallas_call | solution.py:416
Async XLA Ops:
  0.6 24.3 %collective-permute-start = (bf16[2048,256]{1,0:T(8,128)(2,1)}, bf16[2048,256]{1,0:T(8,128)(2,1)S(1)}, u32[]{:S(2)}, u32[]{:S(2)}) collective-permute-start(bf16[2048,256]{1,0:T(8,128)(2,1)} %param.9), channel_id=1, source_target_pairs={{0,32},{32,64},{64,96},{96,0},{1,33},{33,65},{65,97},{97,1},{2,34}... | collective-permute-start | bytes 3145736 | tf_op jit(solution)/shard_map/ppermute | solution.py:136
  0.7 25.5 %collective-permute-start.2 = (bf16[2048,256]{1,0:T(8,128)(2,1)}, bf16[2048,256]{1,0:T(8,128)(2,1)S(1)}, u32[]{:S(2)}, u32[]{:S(2)}) collective-permute-start(bf16[2048,256]{1,0:T(8,128)(2,1)} %param.9), channel_id=1, source_target_pairs={{0,64},{32,96},{64,0},{96,32},{1,65},{33,97},{65,1},{97,33},{2,66}... | collective-permute-start | bytes 3145736 | tf_op jit(solution)/shard_map/ppermute | solution.py:136
  3.0 47.5 %collective-permute-start.1 = (bf16[2048,256]{1,0:T(8,128)(2,1)}, bf16[2048,256]{1,0:T(8,128)(2,1)}, u32[]{:S(2)}, u32[]{:S(2)}) collective-permute-start(bf16[2048,256]{1,0:T(8,128)(2,1)} %param.9), channel_id=1, source_target_pairs={{0,96},{32,0},{64,32},{96,64},{1,97},{33,1},{65,33},{97,65},{2,98}... | collective-permute-start | bytes 3145736 | tf_op jit(solution)/shard_map/ppermute | solution.py:136
  11.3 39.3 %copy-start = (bf16[2048,256]{1,0:T(8,128)(2,1)S(1)}, bf16[2048,256]{1,0:T(8,128)(2,1)}, u32[]{:S(2)}) copy-start(bf16[2048,256]{1,0:T(8,128)(2,1)} %param.9) | copy-start | bytes 3145732
  11.3 91.0 %all-to-all-start = ((bf16[128,8,2176]{2,1,0:T(8,128)(2,1)}), bf16[128,8,2176]{2,1,0:T(8,128)(2,1)}, u32[]{:S(2)}, u32[]{:S(2)}) async-start(bf16[128,8,2176]{2,1,0:T(8,128)(2,1)} %bitcast.11), calls=%async_computation | async-start | bytes 8912896 | tf_op jit(solution)/shard_map/all_to_all | solution.py:444
  53.8 7.7 %collective-permute-start.3 = (bf16[4,2048,256]{2,1,0:T(8,128)(2,1)}, bf16[4,2048,256]{2,1,0:T(8,128)(2,1)}, u32[]{:S(2)}, u32[]{:S(2)}) collective-permute-start(bf16[4,2048,256]{2,1,0:T(8,128)(2,1)} %pad_maximum_fusion.own_ref), channel_id=1, source_target_pairs={{0,16},{16,0},{1,17},{17,1},{2,18},{18,2},{3,19},{19,3},{4,20},{20... | collective-permute-start | bytes 12582920 | tf_op jit(solution)/shard_map/ppermute | solution.py:141
  119.2 58.7 %all-to-all-start.1 = ((bf16[128,8,2048]{2,1,0:T(8,128)(2,1)}), bf16[128,8,2048]{2,1,0:T(8,128)(2,1)}, u32[]{:S(2)}, u32[]{:S(2)}) async-start(bf16[128,8,2048]{2,1,0:T(8,128)(2,1)} %bitcast.12), calls=%async_computation.1 | async-start | bytes 8388608 | tf_op jit(solution)/shard_map/all_to_all | solution.py:444

commit v3 on v2

--- a/solution.py
+++ b/solution.py
@@ -17,6 +17,7 @@
 BF = jnp.bfloat16
 F32 = jnp.float32
 MB = 60
+HINT = 1
 
 
 def params(megabytes):
@@ -132,13 +133,55 @@
     )(tokens, gain, blocks, weights, cot)
 
 
-def shifted(rows, by):
-    return lax.ppermute(rows, "x", [(i, (i + by) % 4) for i in range(4)])
-
-
-def gather_weight(weight):
-    own = jnp.stack([weight, shifted(weight, 1), shifted(weight, 3), shifted(weight, 2)])
-    return own, lax.ppermute(own, "core", [(0, 1), (1, 0)])
+PART = 256
+SHIFTS = (1, 3, 2)
+
+
+def shifted(rows, axis):
+    return [lax.ppermute(rows, axis, [(i, (i + by) % 4) for i in range(4)]) for by in SHIFTS]
+
+
+def assemble_kernel(at_ref, w_ref, *refs):
+    part, along_y, along_z, out_ref = refs[:3], refs[3:6], refs[6:9], refs[9]
+    width = w_ref.shape[1]
+    out_ref[0] = w_ref[...]
+    for side, lines in ((0, along_y), (1, along_z)):
+        base = side * 4 * PART
+        me = at_ref[side]
+        rows = pl.ds(pl.multiple_of(base + me * PART, 64), PART)
+        for k in range(3):
+            out_ref[k + 1, rows, :] = part[k][side * PART : (side + 1) * PART, :]
+        for line, by in zip(lines, SHIFTS):
+            rows = pl.ds(pl.multiple_of(base + lax.rem(me + 4 - by, 4) * PART, 64), PART)
+            for k in range(3):
+                out_ref[k + 1, rows, :] = line[:, k * width : (k + 1) * width]
+
+
+def assemble(weight, part, along_y, along_z):
+    features, width = weight.shape
+    places = jnp.stack([lax.axis_index("y"), lax.axis_index("z")]).astype(jnp.int32)
+    arrays = [weight, *part, *along_y, *along_z]
+    return pl.pallas_call(
+        assemble_kernel,
+        out_shape=jax.ShapeDtypeStruct((4, features, width), BF),
+        in_specs=[pl.BlockSpec(memory_space=pltpu.SMEM)]
+        + [pl.BlockSpec(memory_space=pltpu.VMEM)] * len(arrays),
+        out_specs=pl.BlockSpec(memory_space=pltpu.VMEM),
+        compiler_params=params(24),
+        cost_estimate=cost(1, HINT),
+    )(places, *arrays)
+
+
+def own_part(weight):
+    y, z = lax.axis_index("y"), lax.axis_index("z")
+    width = weight.shape[1]
+    return jnp.concatenate(
+        [
+            lax.dynamic_slice(weight, (y * PART, 0), (PART, width)),
+            lax.dynamic_slice(weight, (4 * PART + z * PART, 0), (PART, width)),
+        ],
+        axis=0,
+    )
 
 
 def slice_at(step, at):
@@ -449,10 +492,15 @@
     owners = lax.axis_size(ALL)
     at = jnp.stack([lax.axis_index("x"), lax.axis_index("core")]).astype(jnp.int32)
     gain = norm_gain.reshape(1, features)
+    part = shifted(own_part(query_weight), "x")
     payload, targets = build_payload(
         tokens, gain, blocks, weights, out_cotangent, owners, values.shape[0] // BLOCK
     )
-    own, sib = gather_weight(query_weight)
+    set_y = jnp.concatenate([p[:PART] for p in part], axis=1)
+    set_z = jnp.concatenate([p[PART:] for p in part], axis=1)
+    set_y, set_z, payload = lax.optimization_barrier((set_y, set_z, payload))
+    own = assemble(query_weight, part, shifted(set_y, "y"), shifted(set_z, "z"))
+    sib = lax.ppermute(own, "core", [(0, 1), (1, 0)])
     got = exchange(payload)
     fold = fold_weight(at, own, sib, values)
     answers, n, c, g, s = serve(got, fold, values, features)

time: 185 us -> 181 us (0.978)
  waiting for transfers between devices: 86.8 us -> 68.7 us
  starting transfers between devices: 21.9 us -> 33 us
  Pallas kernels: 68.5 us -> 72.1 us
  other arithmetic: 3.9 us -> 1.66 us
    ppermute x4 -> x10, waiting for transfers between devices: 33.6 us -> 13.2 us  [the longest x9 6.74 us: shifted(): lax.ppermute(rows, axis, [(i, (i + by) % 4) for i in range(4)])]
    ppermute x4 -> x10, starting transfers between devices: 2.99 us -> 15.2 us  [the longest x9 13.9 us: shifted(): lax.ppermute(rows, axis, [(i, (i + by) % 4) for i in range(4)])]
    pallas_call x0 -> x1, Pallas kernels: none -> 3.46 us  [assemble(): pl.pallas_call(assemble_kernel, out_shape=jax.ShapeDtypeStruct((4, featur...]
    another operation x1, other arithmetic: 3.24 us -> 0.08 us  [assemble(): jnp.stack([lax.axis_index('y'), lax.axis_index('z')]).astype(jnp.int32)]
    all_to_all x2, waiting for transfers between devices: 53.2 us -> 55.4 us  [exchange(): return lax.all_to_all(rows, ALL, split_axis=0, concat_axis=0, tiled=True)]
  transfers between devices with their start and end apart: 6 -> 12, of which waited for: 6 -> 5; matrix products, arithmetic and copies ran while one was open for 4% -> 2% of each run, Pallas kernels for 24% -> 27%
where the time goes in v3:
time: 181 us; the launch traced here: 180 us
  Pallas kernels  72.1 us (40%)
  waiting for transfers between devices  68.7 us (38%)
  starting transfers between devices  33 us (18%)
  local copies, waits for them, and re-layouts  3.88 us (2%)
    all_to_all x2, waiting for transfers between devices, exchange(): return lax.all_to_all(rows, ALL, split_axis=0, concat_axis=0, tiled=True)  55.4 us
    pallas_call x1, Pallas kernels, value_grads(): pl.pallas_call(grad_kernel, out_shape=jax.ShapeDtypeStruct((value_rows, f...  24.4 us
    all_to_all x2, starting transfers between devices, exchange(): return lax.all_to_all(rows, ALL, split_axis=0, concat_axis=0, tiled=True)  17.8 us
    pallas_call x1, Pallas kernels, serve(): pl.pallas_call(functools.partial(serve_kernel, float(features) ** (-0.5))...  16.9 us
    pallas_call x1, Pallas kernels, fold_weight(): pl.pallas_call(fold_kernel, out_shape=jax.ShapeDtypeStruct((features, val...  15.1 us
    ppermute x9, starting transfers between devices, shifted(): lax.ppermute(rows, axis, [(i, (i + by) % 4) for i in range(4)])  13.9 us
    ppermute x9, waiting for transfers between devices, shifted(): lax.ppermute(rows, axis, [(i, (i + by) % 4) for i in range(4)])  6.74 us
    pallas_call x1, Pallas kernels, finish(): pl.pallas_call(home_kernel, out_shape=(jax.ShapeDtypeStruct((count, featu...  6.73 us
  transfers between devices with their start and end apart: 12, of which 5 were waited for; matrix products, arithmetic and copies ran while one was open for 2% of the time, Pallas kernels for 27%

profile of v3, /device:TPU:7, one launch (start us, length us, event | category | flops | bytes accessed | tf_op | source)
XLA Modules:
  0.0 180.1 jit_solution(2289494289295539870)
XLA Ops:
  0.6 1.0 constant_dynamic-slice_fusion.1
  1.7 1.2 collective-permute-start.2
  2.9 0.0 collective-permute-start.1
  2.9 2.7 %collective-permute-start = (bf16[512,256]{1,0:T(8,128)(2,1)S(1)}, bf16[512,256]{1,0:T(8,128)(2,1)S(1)}, u32[]{:S(2)}, u32[]{:S(2)}) collective-permute-start(bf16[512,256]{1,0:T(8,128)(2,1)S(1)} %pad_maximum_fusion.2), channel_id=1, source_target_pairs={{0,32},{32,64},{64,96},{96,0},{1,33},{33,65},{65,97},{97,1},{2,34}... | collective-permute-start | bytes 786440 | tf_op jit(solution)/shard_map/ppermute | solution.py:141
  5.5 1.4 copy.11.wgt_ref
  7.0 1.4 copy.10.blk_ref
  8.4 5.5 %shard_map.94 = (bf16[1024,2176]{1,0:T(8,128)(2,1)}, s32[128,2]{1,0:T(8,128)}) custom-call(bf16[128,2048]{1,0:T(8,128)(2,1)} %tok_ref.3, f32[1,2048]{1,0:T(1,128)} %bitcast.11, s32[128,2]{1,0:T(8,128)} %copy.10.blk_ref, f32[128,2]{1,0:T(8,128)} %copy.11.wgt_ref, bf16[128,2048]{1,0:T(8,128)(2,1)} %cot_ref.3), custom_call_target="tpu_custom_call" | custom-call | flops 1073741824 | bytes 6291456 | tf_op jit(solution)/shard_map/pallas_call | solution.py:112
  13.9 0.0 collective-permute-done.2.refs_2_
  13.9 3.2 %collective-permute-done.1.refs_1_ = bf16[512,256]{1,0:T(8,128)(2,1)S(1)} collective-permute-done((bf16[512,256]{1,0:T(8,128)(2,1)S(1)}, bf16[512,256]{1,0:T(8,128)(2,1)S(1)}, u32[]{:S(2)}, u32[]{:S(2)}) %collective-permute-start.1) | collective-permute-done | bytes 262176 | tf_op jit(solution)/shard_map/ppermute | solution.py:141
  17.1 0.0 collective-permute-done.refs_0_
  17.1 0.9 pad_maximum_fusion
  18.1 2.9 %collective-permute-start.5 = (bf16[256,768]{1,0:T(8,128)(2,1)}, bf16[256,768]{1,0:T(8,128)(2,1)S(1)}, u32[]{:S(2)}, u32[]{:S(2)}) collective-permute-start(bf16[256,768]{1,0:T(8,128)(2,1)} %get-tuple-element.17), channel_id=1, source_target_pairs={{0,2},{1,3},{2,0},{3,1},{4,6},{5,7},{6,4},{7,5},{8,10},{9,11},{10,... | collective-permute-start | bytes 1179656 | tf_op jit(solution)/shard_map/ppermute | solution.py:141
  21.0 0.8 collective-permute-start.4
  21.8 0.7 collective-permute-start.3
  22.5 3.6 %collective-permute-start.8 = (bf16[256,768]{1,0:T(8,128)(2,1)}, bf16[256,768]{1,0:T(8,128)(2,1)S(1)}, u32[]{:S(2)}, u32[]{:S(2)}) collective-permute-start(bf16[256,768]{1,0:T(8,128)(2,1)} %get-tuple-element.18), channel_id=1, source_target_pairs={{0,8},{4,12},{8,0},{12,4},{1,9},{5,13},{9,1},{13,5},{2,10},{6,14},... | collective-permute-start | bytes 1179656 | tf_op jit(solution)/shard_map/ppermute | solution.py:141
  26.1 0.4 collective-permute-start.7
  26.5 3.5 %collective-permute-done.5.refs_5_ = bf16[256,768]{1,0:T(8,128)(2,1)S(1)} collective-permute-done((bf16[256,768]{1,0:T(8,128)(2,1)}, bf16[256,768]{1,0:T(8,128)(2,1)S(1)}, u32[]{:S(2)}, u32[]{:S(2)}) %collective-permute-start.5) | collective-permute-done | bytes 393248 | tf_op jit(solution)/shard_map/ppermute | solution.py:141
  30.0 1.6 collective-permute-start.6
  31.7 0.0 copy-start
  31.7 12.6 %all-to-all-start = ((bf16[128,8,2176]{2,1,0:T(8,128)(2,1)}), bf16[128,8,2176]{2,1,0:T(8,128)(2,1)}, u32[]{:S(2)}, u32[]{:S(2)}) async-start(bf16[128,8,2176]{2,1,0:T(8,128)(2,1)} %bitcast.9), calls=%async_computation | async-start | bytes 8912896 | tf_op jit(solution)/shard_map/all_to_all | solution.py:487
  44.3 0.1 pad_add_fusion.1.at_ref
  44.3 0.0 collective-permute-done.4.refs_4_
  44.3 0.0 collective-permute-done.3.refs_3_
  44.3 0.0 collective-permute-done.8.refs_8_
  44.3 0.0 collective-permute-done.7.refs_7_
  44.4 0.0 collective-permute-done.6.refs_6_
  44.4 0.0 copy-done
  44.4 3.5 %shard_map.95.own_ref = bf16[4,2048,256]{2,1,0:T(8,128)(2,1)} custom-call(s32[2]{0:T(128)S(1)} %pad_add_fusion.1.at_ref, bf16[2048,256]{1,0:T(8,128)(2,1)S(1)} %copy-done, bf16[512,256]{1,0:T(8,128)(2,1)S(1)} %collective-permute-done.refs_0_, bf16[512,256]{1,0:T(8,128)(2,1)S(1)} %collective-permute-done.1.refs_1_, ...), custom_call_target="tpu_custom_call" | custom-call | flops 1 | bytes 1 | tf_op jit(solution)/shard_map/pallas_call | solution.py:164
  47.8 1.3 collective-permute-start.9
  49.1 0.6 pad_add_fusion.at_ref
  49.7 6.5 %collective-permute-done.9.sib_ref = bf16[4,2048,256]{2,1,0:T(8,128)(2,1)} collective-permute-done((bf16[4,2048,256]{2,1,0:T(8,128)(2,1)}, bf16[4,2048,256]{2,1,0:T(8,128)(2,1)}, u32[]{:S(2)}, u32[]{:S(2)}) %collective-permute-start.9) | collective-permute-done | bytes 4194336 | tf_op jit(solution)/shard_map/ppermute | solution.py:503
  56.2 15.1 %shard_map.96.fold_hbm = bf16[2048,1024]{1,0:T(8,128)(2,1)} custom-call(s32[2]{0:T(128)} %pad_add_fusion.at_ref, bf16[4,2048,256]{2,1,0:T(8,128)(2,1)} %shard_map.95.own_ref, bf16[4,2048,256]{2,1,0:T(8,128)(2,1)} %collective-permute-done.9.sib_ref, bf16[1024,2048]{1,0:T(8,128)(2,1)} %val_hbm.1), custom_call_target="tpu_custom_call" | custom-call | flops 1 | bytes 1 | tf_op jit(solution)/shard_map/pallas_call | solution.py:219
  71.3 27.9 %all-to-all-done = bf16[128,8,2176]{2,1,0:T(8,128)(2,1)} async-done(((bf16[128,8,2176]{2,1,0:T(8,128)(2,1)}), bf16[128,8,2176]{2,1,0:T(8,128)(2,1)}, u32[]{:S(2)}, u32[]{:S(2)}) %all-to-all-start) | async-done | bytes 4456480 | tf_op jit(solution)/shard_map/all_to_all | solution.py:487
  99.2 16.9 %shard_map.97 = (bf16[1024,2048]{1,0:T(8,128)(2,1)}, bf16[512,2048]{1,0:T(8,128)(2,1)}, bf16[512,2048]{1,0:T(8,128)(2,1)}, bf16[512,1024]{1,0:T(8,128)(2,1)}, bf16[512,1024]{1,0:T(8,128)(2,1)}) custom-call(bf16[1024,2176]{1,0:T(8,128)(2,1)} %bitcast.2.x_hbm, bf16[2048,1024]{1,0:T(8,128)(2,1)} %shard_map.96.fold_hbm, bf16[1024,2048]{1,0:T(8,128)(2,1)} %val_hbm.1), custom_call_target="tpu_custom_call" | custom-call | flops 8589934592 | bytes 20971520 | tf_op jit(solution)/shard_map/pallas_call | solution.py:343
  116.1 5.3 %all-to-all-start.1 = ((bf16[128,8,2048]{2,1,0:T(8,128)(2,1)}), bf16[128,8,2048]{2,1,0:T(8,128)(2,1)}, u32[]{:S(2)}, u32[]{:S(2)}) async-start(bf16[128,8,2048]{2,1,0:T(8,128)(2,1)} %bitcast.10), calls=%async_computation.1 | async-start | bytes 8388608 | tf_op jit(solution)/shard_map/all_to_all | solution.py:487
  121.4 24.4 %shard_map.99 = bf16[1024,2048]{1,0:T(8,128)(2,1)} custom-call(s32[2]{0:T(128)} %pad_add_fusion.at_ref, bf16[4,2048,256]{2,1,0:T(8,128)(2,1)} %shard_map.95.own_ref, bf16[4,2048,256]{2,1,0:T(8,128)(2,1)} %collective-permute-done.9.sib_ref, bf16[512,2048]{1,0:T(8,128)(2,1)} %get-tuple-element.23.n_ref, bf16[512,2048]{1,0:T(8,128)(2,1)} %get-tuple-element.24.c_ref, ...), custom_call_target="tpu_custom_call" | custom-call | flops 6442450944 | bytes 25165824 | tf_op jit(solution)/shard_map/pallas_call | solution.py:395
  145.8 27.6 %all-to-all-done.1 = bf16[128,8,2048]{2,1,0:T(8,128)(2,1)} async-done(((bf16[128,8,2048]{2,1,0:T(8,128)(2,1)}), bf16[128,8,2048]{2,1,0:T(8,128)(2,1)}, u32[]{:S(2)}, u32[]{:S(2)}) %all-to-all-start.1) | async-done | bytes 4194336 | tf_op jit(solution)/shard_map/all_to_all | solution.py:487
  173.3 6.7 %shard_map.98 = (f32[128,2048]{1,0:T(8,128)}, f32[128,2048]{1,0:T(8,128)}) custom-call(bf16[1024,2048]{1,0:T(8,128)(2,1)} %bitcast.8.back_ref, s32[128,2]{1,0:T(8,128)} %get-tuple-element.20.tgt_ref, f32[128,2]{1,0:T(8,128)} %copy.11.wgt_ref, bf16[128,2048]{1,0:T(8,128)(2,1)} %tok_ref.3, bf16[128,2048]{1,0:T(8,128)(2,1)} %cot_ref.3, f32[1,2048]{1,0:T(1,128)} %bitcast.12), custom_call_target="tpu_custom_call" | custom-call | flops 1610612736 | bytes 10485760 | tf_op jit(solution)/shard_map/pallas_call | solution.py:459
  (4 shorter events, 0.1 us)
Async XLA Ops:
  1.7 12.2 %collective-permute-start.2 = (bf16[512,256]{1,0:T(8,128)(2,1)S(1)}, bf16[512,256]{1,0:T(8,128)(2,1)S(1)}, u32[]{:S(2)}, u32[]{:S(2)}) collective-permute-start(bf16[512,256]{1,0:T(8,128)(2,1)S(1)} %pad_maximum_fusion.2), channel_id=1, source_target_pairs={{0,64},{32,96},{64,0},{96,32},{1,65},{33,97},{65,1},{97,33},{2,66}... | collective-permute-start | bytes 786440 | tf_op jit(solution)/shard_map/ppermute | solution.py:141
  2.9 14.2 %collective-permute-start.1 = (bf16[512,256]{1,0:T(8,128)(2,1)S(1)}, bf16[512,256]{1,0:T(8,128)(2,1)S(1)}, u32[]{:S(2)}, u32[]{:S(2)}) collective-permute-start(bf16[512,256]{1,0:T(8,128)(2,1)S(1)} %pad_maximum_fusion.2), channel_id=1, source_target_pairs={{0,96},{32,0},{64,32},{96,64},{1,97},{33,1},{65,33},{97,65},{2,98}... | collective-permute-start | bytes 786440 | tf_op jit(solution)/shard_map/ppermute | solution.py:141
  2.9 14.2 %collective-permute-start = (bf16[512,256]{1,0:T(8,128)(2,1)S(1)}, bf16[512,256]{1,0:T(8,128)(2,1)S(1)}, u32[]{:S(2)}, u32[]{:S(2)}) collective-permute-start(bf16[512,256]{1,0:T(8,128)(2,1)S(1)} %pad_maximum_fusion.2), channel_id=1, source_target_pairs={{0,32},{32,64},{64,96},{96,0},{1,33},{33,65},{65,97},{97,1},{2,34}... | collective-permute-start | bytes 786440 | tf_op jit(solution)/shard_map/ppermute | solution.py:141
  18.1 11.9 %collective-permute-start.5 = (bf16[256,768]{1,0:T(8,128)(2,1)}, bf16[256,768]{1,0:T(8,128)(2,1)S(1)}, u32[]{:S(2)}, u32[]{:S(2)}) collective-permute-start(bf16[256,768]{1,0:T(8,128)(2,1)} %get-tuple-element.17), channel_id=1, source_target_pairs={{0,2},{1,3},{2,0},{3,1},{4,6},{5,7},{6,4},{7,5},{8,10},{9,11},{10,... | collective-permute-start | bytes 1179656 | tf_op jit(solution)/shard_map/ppermute | solution.py:141
  21.0 23.3 %collective-permute-start.4 = (bf16[256,768]{1,0:T(8,128)(2,1)}, bf16[256,768]{1,0:T(8,128)(2,1)S(1)}, u32[]{:S(2)}, u32[]{:S(2)}) collective-permute-start(bf16[256,768]{1,0:T(8,128)(2,1)} %get-tuple-element.17), channel_id=1, source_target_pairs={{0,3},{1,0},{2,1},{3,2},{4,7},{5,4},{6,5},{7,6},{8,11},{9,8},{10,9... | collective-permute-start | bytes 1179656 | tf_op jit(solution)/shard_map/ppermute | solution.py:141
  21.8 22.6 %collective-permute-start.3 = (bf16[256,768]{1,0:T(8,128)(2,1)}, bf16[256,768]{1,0:T(8,128)(2,1)S(1)}, u32[]{:S(2)}, u32[]{:S(2)}) collective-permute-start(bf16[256,768]{1,0:T(8,128)(2,1)} %get-tuple-element.17), channel_id=1, source_target_pairs={{0,1},{1,2},{2,3},{3,0},{4,5},{5,6},{6,7},{7,4},{8,9},{9,10},{10,1... | collective-permute-start | bytes 1179656 | tf_op jit(solution)/shard_map/ppermute | solution.py:141
  22.5 21.9 %collective-permute-start.8 = (bf16[256,768]{1,0:T(8,128)(2,1)}, bf16[256,768]{1,0:T(8,128)(2,1)S(1)}, u32[]{:S(2)}, u32[]{:S(2)}) collective-permute-start(bf16[256,768]{1,0:T(8,128)(2,1)} %get-tuple-element.18), channel_id=1, source_target_pairs={{0,8},{4,12},{8,0},{12,4},{1,9},{5,13},{9,1},{13,5},{2,10},{6,14},... | collective-permute-start | bytes 1179656 | tf_op jit(solution)/shard_map/ppermute | solution.py:141
  26.1 18.3 %collective-permute-start.7 = (bf16[256,768]{1,0:T(8,128)(2,1)}, bf16[256,768]{1,0:T(8,128)(2,1)}, u32[]{:S(2)}, u32[]{:S(2)}) collective-permute-start(bf16[256,768]{1,0:T(8,128)(2,1)} %get-tuple-element.18), channel_id=1, source_target_pairs={{0,12},{4,0},{8,4},{12,8},{1,13},{5,1},{9,5},{13,9},{2,14},{6,2},{... | collective-permute-start | bytes 1179656 | tf_op jit(solution)/shard_map/ppermute | solution.py:141
  30.0 14.3 %collective-permute-start.6 = (bf16[256,768]{1,0:T(8,128)(2,1)}, bf16[256,768]{1,0:T(8,128)(2,1)}, u32[]{:S(2)}, u32[]{:S(2)}) collective-permute-start(bf16[256,768]{1,0:T(8,128)(2,1)} %get-tuple-element.18), channel_id=1, source_target_pairs={{0,4},{4,8},{8,12},{12,0},{1,5},{5,9},{9,13},{13,1},{2,6},{6,10},{... | collective-permute-start | bytes 1179656 | tf_op jit(solution)/shard_map/ppermute | solution.py:141
  31.7 12.7 %copy-start = (bf16[2048,256]{1,0:T(8,128)(2,1)S(1)}, bf16[2048,256]{1,0:T(8,128)(2,1)}, u32[]{:S(2)}) copy-start(bf16[2048,256]{1,0:T(8,128)(2,1)} %w_ref.1) | copy-start | bytes 3145732
  31.7 67.6 %all-to-all-start = ((bf16[128,8,2176]{2,1,0:T(8,128)(2,1)}), bf16[128,8,2176]{2,1,0:T(8,128)(2,1)}, u32[]{:S(2)}, u32[]{:S(2)}) async-start(bf16[128,8,2176]{2,1,0:T(8,128)(2,1)} %bitcast.9), calls=%async_computation | async-start | bytes 8912896 | tf_op jit(solution)/shard_map/all_to_all | solution.py:487
  47.8 8.4 %collective-permute-start.9 = (bf16[4,2048,256]{2,1,0:T(8,128)(2,1)}, bf16[4,2048,256]{2,1,0:T(8,128)(2,1)}, u32[]{:S(2)}, u32[]{:S(2)}) collective-permute-start(bf16[4,2048,256]{2,1,0:T(8,128)(2,1)} %shard_map.95.own_ref), channel_id=1, source_target_pairs={{0,16},{16,0},{1,17},{17,1},{2,18},{18,2},{3,19},{19,3},{4,20},{20... | collective-permute-start | bytes 12582920 | tf_op jit(solution)/shard_map/ppermute | solution.py:503
  116.1 57.2 %all-to-all-start.1 = ((bf16[128,8,2048]{2,1,0:T(8,128)(2,1)}), bf16[128,8,2048]{2,1,0:T(8,128)(2,1)}, u32[]{:S(2)}, u32[]{:S(2)}) async-start(bf16[128,8,2048]{2,1,0:T(8,128)(2,1)} %bitcast.10), calls=%async_computation.1 | async-start | bytes 8388608 | tf_op jit(solution)/shard_map/all_to_all | solution.py:487

commit v4 on v2

--- a/solution.py
+++ b/solution.py
@@ -17,6 +17,7 @@
 BF = jnp.bfloat16
 F32 = jnp.float32
 MB = 60
+HINT = 1
 
 
 def params(megabytes):
@@ -132,13 +133,43 @@
     )(tokens, gain, blocks, weights, cot)
 
 
-def shifted(rows, by):
-    return lax.ppermute(rows, "x", [(i, (i + by) % 4) for i in range(4)])
-
-
-def gather_weight(weight):
-    own = jnp.stack([weight, shifted(weight, 1), shifted(weight, 3), shifted(weight, 2)])
-    return own, lax.ppermute(own, "core", [(0, 1), (1, 0)])
+DIRECT = 1024
+SHIFTS = (1, 3, 2)
+
+
+def shifted(rows, axis):
+    return [lax.ppermute(rows, axis, [(i, (i + by) % 4) for i in range(4)]) for by in SHIFTS]
+
+
+def assemble_kernel(at_ref, w_ref, *refs):
+    direct, part, along_y, out_ref = refs[:3], refs[3:6], refs[6:9], refs[9]
+    width = w_ref.shape[1]
+    count = part[0].shape[0]
+    me = at_ref[0]
+    out_ref[0] = w_ref[...]
+    rows = pl.ds(pl.multiple_of(DIRECT + me * count, 64), count)
+    for k in range(3):
+        out_ref[k + 1, :DIRECT, :] = direct[k][...]
+        out_ref[k + 1, rows, :] = part[k][...]
+    for line, by in zip(along_y, SHIFTS):
+        rows = pl.ds(pl.multiple_of(DIRECT + lax.rem(me + 4 - by, 4) * count, 64), count)
+        for k in range(3):
+            out_ref[k + 1, rows, :] = line[:, k * width : (k + 1) * width]
+
+
+def assemble(weight, direct, part, along_y):
+    features, width = weight.shape
+    place = lax.axis_index("y").astype(jnp.int32).reshape(1)
+    arrays = [weight, *direct, *part, *along_y]
+    return pl.pallas_call(
+        assemble_kernel,
+        out_shape=jax.ShapeDtypeStruct((4, features, width), BF),
+        in_specs=[pl.BlockSpec(memory_space=pltpu.SMEM)]
+        + [pl.BlockSpec(memory_space=pltpu.VMEM)] * len(arrays),
+        out_specs=pl.BlockSpec(memory_space=pltpu.VMEM),
+        compiler_params=params(24),
+        cost_estimate=cost(1, HINT),
+    )(place, *arrays)
 
 
 def slice_at(step, at):
@@ -449,10 +480,18 @@
     owners = lax.axis_size(ALL)
     at = jnp.stack([lax.axis_index("x"), lax.axis_index("core")]).astype(jnp.int32)
     gain = norm_gain.reshape(1, features)
+    features, width = query_weight.shape
+    rows = (features - DIRECT) // 4
+    mine = lax.dynamic_slice(query_weight, (DIRECT + lax.axis_index("y") * rows, 0), (rows, width))
+    part = shifted(mine, "x")
+    direct = shifted(query_weight[:DIRECT], "x")
     payload, targets = build_payload(
         tokens, gain, blocks, weights, out_cotangent, owners, values.shape[0] // BLOCK
     )
-    own, sib = gather_weight(query_weight)
+    set_y = jnp.concatenate(part, axis=1)
+    set_y, payload = lax.optimization_barrier((set_y, payload))
+    own = assemble(query_weight, direct, part, shifted(set_y, "y"))
+    sib = lax.ppermute(own, "core", [(0, 1), (1, 0)])
     got = exchange(payload)
     fold = fold_weight(at, own, sib, values)
     answers, n, c, g, s = serve(got, fold, values, features)

time: 185 us -> 188 us (1.016)
  waiting for transfers between devices: 86.8 us -> 61 us
  starting transfers between devices: 21.9 us -> 46.8 us
  Pallas kernels: 68.5 us -> 72.1 us
  local copies, waits for them, and re-layouts: 2.82 us -> 5.61 us
  other arithmetic: 3.9 us -> 1.39 us
    ppermute x4 -> x10, starting transfers between devices: 2.99 us -> 21.9 us  [the longest x1 11.6 us: body(): sib = lax.ppermute(own, 'core', [(0, 1), (1, 0)])]
    all_to_all x2, waiting for transfers between devices: 53.2 us -> 36.9 us  [exchange(): return lax.all_to_all(rows, ALL, split_axis=0, concat_axis=0, tiled=True)]
    ppermute x4 -> x10, waiting for transfers between devices: 33.6 us -> 24.2 us  [the longest x9 17.7 us: shifted(): lax.ppermute(rows, axis, [(i, (i + by) % 4) for i in range(4)])]
    all_to_all x2, starting transfers between devices: 18.9 us -> 24.9 us  [exchange(): return lax.all_to_all(rows, ALL, split_axis=0, concat_axis=0, tiled=True)]
    pallas_call x0 -> x1, Pallas kernels: none -> 3.43 us  [assemble(): pl.pallas_call(assemble_kernel, out_shape=jax.ShapeDtypeStruct((4, featur...]
    another operation x1 -> x0, other arithmetic: 3.24 us -> none  [gather_weight(): jnp.stack([weight, shifted(weight, 1), shifted(weight, 3), shifted(weight...]
  transfers between devices with their start and end apart: 6 -> 12, of which waited for: 6 -> 5; matrix products, arithmetic and copies ran while one was open for 4% -> 3% of each run, Pallas kernels for 24% -> 26%
where the time goes in v4:
time: 188 us
  Pallas kernels  72.1 us (38%)
  waiting for transfers between devices  61 us (32%)
  starting transfers between devices  46.8 us (25%)
  local copies, waits for them, and re-layouts  5.61 us (3%)
    all_to_all x2, waiting for transfers between devices, exchange(): return lax.all_to_all(rows, ALL, split_axis=0, concat_axis=0, tiled=True)  36.9 us
    all_to_all x2, starting transfers between devices, exchange(): return lax.all_to_all(rows, ALL, split_axis=0, concat_axis=0, tiled=True)  24.9 us
    pallas_call x1, Pallas kernels, value_grads(): pl.pallas_call(grad_kernel, out_shape=jax.ShapeDtypeStruct((value_rows, f...  24.4 us
    ppermute x9, waiting for transfers between devices, shifted(): lax.ppermute(rows, axis, [(i, (i + by) % 4) for i in range(4)])  17.7 us
    pallas_call x1, Pallas kernels, serve(): pl.pallas_call(functools.partial(serve_kernel, float(features) ** (-0.5))...  16.9 us
    pallas_call x1, Pallas kernels, fold_weight(): pl.pallas_call(fold_kernel, out_shape=jax.ShapeDtypeStruct((features, val...  15.1 us
    ppermute x1, starting transfers between devices, body(): sib = lax.ppermute(own, 'core', [(0, 1), (1, 0)])  11.6 us
    ppermute x9, starting transfers between devices, shifted(): lax.ppermute(rows, axis, [(i, (i + by) % 4) for i in range(4)])  10.3 us
  transfers between devices with their start and end apart: 12, of which 5 were waited for; matrix products, arithmetic and copies ran while one was open for 3% of the time, Pallas kernels for 26%

profile of v4, /device:TPU:7, one launch (start us, length us, event | category | flops | bytes accessed | tf_op | source)
XLA Modules:
  0.0 187.6 jit_solution(4324619071079314637)
XLA Ops:
  0.6 1.9 slice.3
  2.5 1.1 collective-permute-start.5
  3.6 0.9 constant_dynamic-slice_fusion
  4.5 1.9 %collective-permute-start.2 = (bf16[256,256]{1,0:T(8,128)(2,1)S(1)}, bf16[256,256]{1,0:T(8,128)(2,1)S(1)}, u32[]{:S(2)}, u32[]{:S(2)}) collective-permute-start(bf16[256,256]{1,0:T(8,128)(2,1)S(1)} %constant_dynamic-slice_fusion), channel_id=1, source_target_pairs={{0,64},{32,96},{64,0},{96,32},{1,65},{33,97},{65,1},{97,33},{2,66}... | collective-permute-start | bytes 393224 | tf_op jit(solution)/shard_map/ppermute | solution.py:141
  6.5 0.5 collective-permute-start.1
  7.0 2.1 %collective-permute-start = (bf16[256,256]{1,0:T(8,128)(2,1)S(1)}, bf16[256,256]{1,0:T(8,128)(2,1)S(1)}, u32[]{:S(2)}, u32[]{:S(2)}) collective-permute-start(bf16[256,256]{1,0:T(8,128)(2,1)S(1)} %constant_dynamic-slice_fusion), channel_id=1, source_target_pairs={{0,32},{32,64},{64,96},{96,0},{1,33},{33,65},{65,97},{97,1},{2,34}... | collective-permute-start | bytes 393224 | tf_op jit(solution)/shard_map/ppermute | solution.py:141
  9.1 0.0 collective-permute-start.4
  9.1 1.4 copy.11.wgt_ref
  10.6 1.4 copy.10.blk_ref
  12.0 7.9 %collective-permute-done.2.refs_5_ = bf16[256,256]{1,0:T(8,128)(2,1)S(1)} collective-permute-done((bf16[256,256]{1,0:T(8,128)(2,1)S(1)}, bf16[256,256]{1,0:T(8,128)(2,1)S(1)}, u32[]{:S(2)}, u32[]{:S(2)}) %collective-permute-start.2) | collective-permute-done | bytes 131104 | tf_op jit(solution)/shard_map/ppermute | solution.py:141
  19.9 0.0 collective-permute-start.3
  19.9 5.5 %shard_map.94 = (bf16[1024,2176]{1,0:T(8,128)(2,1)}, s32[128,2]{1,0:T(8,128)}) custom-call(bf16[128,2048]{1,0:T(8,128)(2,1)} %tok_ref.3, f32[1,2048]{1,0:T(1,128)} %bitcast.10, s32[128,2]{1,0:T(8,128)} %copy.10.blk_ref, f32[128,2]{1,0:T(8,128)} %copy.11.wgt_ref, bf16[128,2048]{1,0:T(8,128)(2,1)} %cot_ref.3), custom_call_target="tpu_custom_call" | custom-call | flops 1073741824 | bytes 6291456 | tf_op jit(solution)/shard_map/pallas_call | solution.py:112
  25.4 0.0 collective-permute-done.1.refs_4_
  25.4 0.0 collective-permute-done.refs_3_
  25.4 0.8 pad_maximum_fusion
  26.2 3.1 %collective-permute-start.8 = (bf16[256,768]{1,0:T(8,128)(2,1)}, bf16[256,768]{1,0:T(8,128)(2,1)S(1)}, u32[]{:S(2)}, u32[]{:S(2)}) collective-permute-start(bf16[256,768]{1,0:T(8,128)(2,1)} %pad_maximum_fusion), channel_id=1, source_target_pairs={{0,2},{1,3},{2,0},{3,1},{4,6},{5,7},{6,4},{7,5},{8,10},{9,11},{10,... | collective-permute-start | bytes 1179656 | tf_op jit(solution)/shard_map/ppermute | solution.py:141
  29.3 0.8 collective-permute-start.7
  30.0 0.0 collective-permute-done.5.refs_2_
  30.1 0.7 collective-permute-start.6
  30.7 0.0 copy-start
  30.7 14.1 %all-to-all-start = ((bf16[128,8,2176]{2,1,0:T(8,128)(2,1)}), bf16[128,8,2176]{2,1,0:T(8,128)(2,1)}, u32[]{:S(2)}, u32[]{:S(2)}) async-start(bf16[128,8,2176]{2,1,0:T(8,128)(2,1)} %bitcast.8), calls=%async_computation | async-start | bytes 8912896 | tf_op jit(solution)/shard_map/all_to_all | solution.py:475
  44.9 0.0 collective-permute-done.4.refs_1_
  44.9 0.0 collective-permute-done.3.refs_0_
  44.9 0.0 collective-permute-done.8.refs_8_
  44.9 9.7 %collective-permute-done.7.refs_7_ = bf16[256,768]{1,0:T(8,128)(2,1)} collective-permute-done((bf16[256,768]{1,0:T(8,128)(2,1)}, bf16[256,768]{1,0:T(8,128)(2,1)}, u32[]{:S(2)}, u32[]{:S(2)}) %collective-permute-start.7) | collective-permute-done | bytes 393248 | tf_op jit(solution)/shard_map/ppermute | solution.py:141
  54.7 0.0 collective-permute-done.6.refs_6_
  54.7 0.0 copy-done
  54.7 3.4 %shard_map.95.own_ref = bf16[4,2048,256]{2,1,0:T(8,128)(2,1)} custom-call(s32[1]{0:T(128)} %bitcast.5.at_ref, bf16[2048,256]{1,0:T(8,128)(2,1)S(1)} %copy-done, bf16[1024,256]{1,0:T(8,128)(2,1)S(1)} %collective-permute-done.3.refs_0_, bf16[1024,256]{1,0:T(8,128)(2,1)S(1)} %collective-permute-done.4.refs_1_, ...), custom_call_target="tpu_custom_call" | custom-call | flops 1 | bytes 1 | tf_op jit(solution)/shard_map/pallas_call | solution.py:164
  58.1 11.6 %collective-permute-start.9 = (bf16[4,2048,256]{2,1,0:T(8,128)(2,1)}, bf16[4,2048,256]{2,1,0:T(8,128)(2,1)}, u32[]{:S(2)}, u32[]{:S(2)}) collective-permute-start(bf16[4,2048,256]{2,1,0:T(8,128)(2,1)} %shard_map.95.own_ref), channel_id=1, source_target_pairs={{0,16},{16,0},{1,17},{17,1},{2,18},{18,2},{3,19},{19,3},{4,20},{20... | collective-permute-start | bytes 12582920 | tf_op jit(solution)/shard_map/ppermute | solution.py:494
  69.7 0.6 pad_add_fusion.at_ref
  70.3 6.5 %collective-permute-done.9.sib_ref = bf16[4,2048,256]{2,1,0:T(8,128)(2,1)} collective-permute-done((bf16[4,2048,256]{2,1,0:T(8,128)(2,1)}, bf16[4,2048,256]{2,1,0:T(8,128)(2,1)}, u32[]{:S(2)}, u32[]{:S(2)}) %collective-permute-start.9) | collective-permute-done | bytes 4194336 | tf_op jit(solution)/shard_map/ppermute | solution.py:494
  76.8 15.1 %shard_map.96.fold_hbm = bf16[2048,1024]{1,0:T(8,128)(2,1)} custom-call(s32[2]{0:T(128)} %pad_add_fusion.at_ref, bf16[4,2048,256]{2,1,0:T(8,128)(2,1)} %shard_map.95.own_ref, bf16[4,2048,256]{2,1,0:T(8,128)(2,1)} %collective-permute-done.9.sib_ref, bf16[1024,2048]{1,0:T(8,128)(2,1)} %val_hbm.1), custom_call_target="tpu_custom_call" | custom-call | flops 1 | bytes 1 | tf_op jit(solution)/shard_map/pallas_call | solution.py:207
  92.0 9.4 %all-to-all-done = bf16[128,8,2176]{2,1,0:T(8,128)(2,1)} async-done(((bf16[128,8,2176]{2,1,0:T(8,128)(2,1)}), bf16[128,8,2176]{2,1,0:T(8,128)(2,1)}, u32[]{:S(2)}, u32[]{:S(2)}) %all-to-all-start) | async-done | bytes 4456480 | tf_op jit(solution)/shard_map/all_to_all | solution.py:475
  101.3 16.9 %shard_map.97 = (bf16[1024,2048]{1,0:T(8,128)(2,1)}, bf16[512,2048]{1,0:T(8,128)(2,1)}, bf16[512,2048]{1,0:T(8,128)(2,1)}, bf16[512,1024]{1,0:T(8,128)(2,1)}, bf16[512,1024]{1,0:T(8,128)(2,1)}) custom-call(bf16[1024,2176]{1,0:T(8,128)(2,1)} %bitcast.2.x_hbm, bf16[2048,1024]{1,0:T(8,128)(2,1)} %shard_map.96.fold_hbm, bf16[1024,2048]{1,0:T(8,128)(2,1)} %val_hbm.1), custom_call_target="tpu_custom_call" | custom-call | flops 8589934592 | bytes 20971520 | tf_op jit(solution)/shard_map/pallas_call | solution.py:331
  118.2 10.8 %all-to-all-start.1 = ((bf16[128,8,2048]{2,1,0:T(8,128)(2,1)}), bf16[128,8,2048]{2,1,0:T(8,128)(2,1)}, u32[]{:S(2)}, u32[]{:S(2)}) async-start(bf16[128,8,2048]{2,1,0:T(8,128)(2,1)} %bitcast.9), calls=%async_computation.1 | async-start | bytes 8388608 | tf_op jit(solution)/shard_map/all_to_all | solution.py:475
  129.0 24.4 %shard_map.99 = bf16[1024,2048]{1,0:T(8,128)(2,1)} custom-call(s32[2]{0:T(128)} %pad_add_fusion.at_ref, bf16[4,2048,256]{2,1,0:T(8,128)(2,1)} %shard_map.95.own_ref, bf16[4,2048,256]{2,1,0:T(8,128)(2,1)} %collective-permute-done.9.sib_ref, bf16[512,2048]{1,0:T(8,128)(2,1)} %get-tuple-element.21.n_ref, bf16[512,2048]{1,0:T(8,128)(2,1)} %get-tuple-element.22.c_ref, ...), custom_call_target="tpu_custom_call" | custom-call | flops 6442450944 | bytes 25165824 | tf_op jit(solution)/shard_map/pallas_call | solution.py:383
  153.4 27.5 %all-to-all-done.1 = bf16[128,8,2048]{2,1,0:T(8,128)(2,1)} async-done(((bf16[128,8,2048]{2,1,0:T(8,128)(2,1)}), bf16[128,8,2048]{2,1,0:T(8,128)(2,1)}, u32[]{:S(2)}, u32[]{:S(2)}) %all-to-all-start.1) | async-done | bytes 4194336 | tf_op jit(solution)/shard_map/all_to_all | solution.py:475
  180.9 6.7 %shard_map.98 = (f32[128,2048]{1,0:T(8,128)}, f32[128,2048]{1,0:T(8,128)}) custom-call(bf16[1024,2048]{1,0:T(8,128)(2,1)} %bitcast.7.back_ref, s32[128,2]{1,0:T(8,128)} %get-tuple-element.18.tgt_ref, f32[128,2]{1,0:T(8,128)} %copy.11.wgt_ref, bf16[128,2048]{1,0:T(8,128)(2,1)} %tok_ref.3, bf16[128,2048]{1,0:T(8,128)(2,1)} %cot_ref.3, f32[1,2048]{1,0:T(1,128)} %bitcast.11), custom_call_target="tpu_custom_call" | custom-call | flops 1610612736 | bytes 10485760 | tf_op jit(solution)/shard_map/pallas_call | solution.py:447
Async XLA Ops:
  2.5 27.6 %collective-permute-start.5 = (bf16[1024,256]{1,0:T(8,128)(2,1)}, bf16[1024,256]{1,0:T(8,128)(2,1)S(1)}, u32[]{:S(2)}, u32[]{:S(2)}) collective-permute-start(bf16[1024,256]{1,0:T(8,128)(2,1)} %slice.3), channel_id=1, source_target_pairs={{0,64},{32,96},{64,0},{96,32},{1,65},{33,97},{65,1},{97,33},{2,66}... | collective-permute-start | bytes 1572872 | tf_op jit(solution)/shard_map/ppermute | solution.py:141
  4.5 15.3 %collective-permute-start.2 = (bf16[256,256]{1,0:T(8,128)(2,1)S(1)}, bf16[256,256]{1,0:T(8,128)(2,1)S(1)}, u32[]{:S(2)}, u32[]{:S(2)}) collective-permute-start(bf16[256,256]{1,0:T(8,128)(2,1)S(1)} %constant_dynamic-slice_fusion), channel_id=1, source_target_pairs={{0,64},{32,96},{64,0},{96,32},{1,65},{33,97},{65,1},{97,33},{2,66}... | collective-permute-start | bytes 393224 | tf_op jit(solution)/shard_map/ppermute | solution.py:141
  6.5 18.9 %collective-permute-start.1 = (bf16[256,256]{1,0:T(8,128)(2,1)S(1)}, bf16[256,256]{1,0:T(8,128)(2,1)S(1)}, u32[]{:S(2)}, u32[]{:S(2)}) collective-permute-start(bf16[256,256]{1,0:T(8,128)(2,1)S(1)} %constant_dynamic-slice_fusion), channel_id=1, source_target_pairs={{0,96},{32,0},{64,32},{96,64},{1,97},{33,1},{65,33},{97,65},{2,98}... | collective-permute-start | bytes 393224 | tf_op jit(solution)/shard_map/ppermute | solution.py:141
  7.0 18.4 %collective-permute-start = (bf16[256,256]{1,0:T(8,128)(2,1)S(1)}, bf16[256,256]{1,0:T(8,128)(2,1)S(1)}, u32[]{:S(2)}, u32[]{:S(2)}) collective-permute-start(bf16[256,256]{1,0:T(8,128)(2,1)S(1)} %constant_dynamic-slice_fusion), channel_id=1, source_target_pairs={{0,32},{32,64},{64,96},{96,0},{1,33},{33,65},{65,97},{97,1},{2,34}... | collective-permute-start | bytes 393224 | tf_op jit(solution)/shard_map/ppermute | solution.py:141
  9.1 35.7 %collective-permute-start.4 = (bf16[1024,256]{1,0:T(8,128)(2,1)}, bf16[1024,256]{1,0:T(8,128)(2,1)S(1)}, u32[]{:S(2)}, u32[]{:S(2)}) collective-permute-start(bf16[1024,256]{1,0:T(8,128)(2,1)} %slice.3), channel_id=1, source_target_pairs={{0,96},{32,0},{64,32},{96,64},{1,97},{33,1},{65,33},{97,65},{2,98}... | collective-permute-start | bytes 1572872 | tf_op jit(solution)/shard_map/ppermute | solution.py:141
  19.9 25.0 %collective-permute-start.3 = (bf16[1024,256]{1,0:T(8,128)(2,1)}, bf16[1024,256]{1,0:T(8,128)(2,1)S(1)}, u32[]{:S(2)}, u32[]{:S(2)}) collective-permute-start(bf16[1024,256]{1,0:T(8,128)(2,1)} %slice.3), channel_id=1, source_target_pairs={{0,32},{32,64},{64,96},{96,0},{1,33},{33,65},{65,97},{97,1},{2,34}... | collective-permute-start | bytes 1572872 | tf_op jit(solution)/shard_map/ppermute | solution.py:141
  26.2 18.7 %collective-permute-start.8 = (bf16[256,768]{1,0:T(8,128)(2,1)}, bf16[256,768]{1,0:T(8,128)(2,1)S(1)}, u32[]{:S(2)}, u32[]{:S(2)}) collective-permute-start(bf16[256,768]{1,0:T(8,128)(2,1)} %pad_maximum_fusion), channel_id=1, source_target_pairs={{0,2},{1,3},{2,0},{3,1},{4,6},{5,7},{6,4},{7,5},{8,10},{9,11},{10,... | collective-permute-start | bytes 1179656 | tf_op jit(solution)/shard_map/ppermute | solution.py:141
  29.3 25.4 %collective-permute-start.7 = (bf16[256,768]{1,0:T(8,128)(2,1)}, bf16[256,768]{1,0:T(8,128)(2,1)}, u32[]{:S(2)}, u32[]{:S(2)}) collective-permute-start(bf16[256,768]{1,0:T(8,128)(2,1)} %pad_maximum_fusion), channel_id=1, source_target_pairs={{0,3},{1,0},{2,1},{3,2},{4,7},{5,4},{6,5},{7,6},{8,11},{9,8},{10,9... | collective-permute-start | bytes 1179656 | tf_op jit(solution)/shard_map/ppermute | solution.py:141
  30.1 24.6 %collective-permute-start.6 = (bf16[256,768]{1,0:T(8,128)(2,1)}, bf16[256,768]{1,0:T(8,128)(2,1)}, u32[]{:S(2)}, u32[]{:S(2)}) collective-permute-start(bf16[256,768]{1,0:T(8,128)(2,1)} %pad_maximum_fusion), channel_id=1, source_target_pairs={{0,1},{1,2},{2,3},{3,0},{4,5},{5,6},{6,7},{7,4},{8,9},{9,10},{10,1... | collective-permute-start | bytes 1179656 | tf_op jit(solution)/shard_map/ppermute | solution.py:141
  30.7 23.9 %copy-start = (bf16[2048,256]{1,0:T(8,128)(2,1)S(1)}, bf16[2048,256]{1,0:T(8,128)(2,1)}, u32[]{:S(2)}) copy-start(bf16[2048,256]{1,0:T(8,128)(2,1)} %w_ref.1) | copy-start | bytes 3145732
  30.7 70.6 %all-to-all-start = ((bf16[128,8,2176]{2,1,0:T(8,128)(2,1)}), bf16[128,8,2176]{2,1,0:T(8,128)(2,1)}, u32[]{:S(2)}, u32[]{:S(2)}) async-start(bf16[128,8,2176]{2,1,0:T(8,128)(2,1)} %bitcast.8), calls=%async_computation | async-start | bytes 8912896 | tf_op jit(solution)/shard_map/all_to_all | solution.py:475
  58.1 18.7 %collective-permute-start.9 = (bf16[4,2048,256]{2,1,0:T(8,128)(2,1)}, bf16[4,2048,256]{2,1,0:T(8,128)(2,1)}, u32[]{:S(2)}, u32[]{:S(2)}) collective-permute-start(bf16[4,2048,256]{2,1,0:T(8,128)(2,1)} %shard_map.95.own_ref), channel_id=1, source_target_pairs={{0,16},{16,0},{1,17},{17,1},{2,18},{18,2},{3,19},{19,3},{4,20},{20... | collective-permute-start | bytes 12582920 | tf_op jit(solution)/shard_map/ppermute | solution.py:494
  118.2 62.7 %all-to-all-start.1 = ((bf16[128,8,2048]{2,1,0:T(8,128)(2,1)}), bf16[128,8,2048]{2,1,0:T(8,128)(2,1)}, u32[]{:S(2)}, u32[]{:S(2)}) async-start(bf16[128,8,2048]{2,1,0:T(8,128)(2,1)} %bitcast.9), calls=%async_computation.1 | async-start | bytes 8388608 | tf_op jit(solution)/shard_map/all_to_all | solution.py:475

commit v5 on v4

--- a/solution.py
+++ b/solution.py
@@ -133,34 +133,50 @@
     )(tokens, gain, blocks, weights, cot)
 
 
-DIRECT = 1024
 SHIFTS = (1, 3, 2)
 
 
-def shifted(rows, axis):
-    return [lax.ppermute(rows, axis, [(i, (i + by) % 4) for i in range(4)]) for by in SHIFTS]
+def along_x(rows):
+    return [lax.ppermute(rows, "x", [(i, (i + by) % 4) for i in range(4)]) for by in SHIFTS]
+
+
+def line_step(by):
+    pairs = []
+    for x in range(4):
+        for z in range(4):
+            for y in range(4):
+                at = lambda c, z, y: ((2 * x + c) * 4 + z % 4) * 4 + y % 4
+                pairs.append((at(0, z, y), at(0, z, y + by)))
+                pairs.append((at(1, z, y), at(1, z + by, y)))
+    return pairs
+
+
+def along_line(rows):
+    return [lax.ppermute(rows, ALL, line_step(by)) for by in SHIFTS]
+
+
+def line_place():
+    return jnp.where(lax.axis_index("core") == 0, lax.axis_index("y"), lax.axis_index("z")).astype(jnp.int32)
 
 
 def assemble_kernel(at_ref, w_ref, *refs):
-    direct, part, along_y, out_ref = refs[:3], refs[3:6], refs[6:9], refs[9]
+    part, line, out_ref = refs[:3], refs[3:6], refs[6]
     width = w_ref.shape[1]
     count = part[0].shape[0]
     me = at_ref[0]
     out_ref[0] = w_ref[...]
-    rows = pl.ds(pl.multiple_of(DIRECT + me * count, 64), count)
+    rows = pl.ds(pl.multiple_of(me * count, count), count)
     for k in range(3):
-        out_ref[k + 1, :DIRECT, :] = direct[k][...]
         out_ref[k + 1, rows, :] = part[k][...]
-    for line, by in zip(along_y, SHIFTS):
-        rows = pl.ds(pl.multiple_of(DIRECT + lax.rem(me + 4 - by, 4) * count, 64), count)
+    for other, by in zip(line, SHIFTS):
+        rows = pl.ds(pl.multiple_of(lax.rem(me + 4 - by, 4) * count, count), count)
         for k in range(3):
-            out_ref[k + 1, rows, :] = line[:, k * width : (k + 1) * width]
-
-
-def assemble(weight, direct, part, along_y):
+            out_ref[k + 1, rows, :] = other[:, k * width : (k + 1) * width]
+
+
+def assemble(place, weight, part, line):
     features, width = weight.shape
-    place = lax.axis_index("y").astype(jnp.int32).reshape(1)
-    arrays = [weight, *direct, *part, *along_y]
+    arrays = [weight, *part, *line]
     return pl.pallas_call(
         assemble_kernel,
         out_shape=jax.ShapeDtypeStruct((4, features, width), BF),
@@ -169,7 +185,7 @@
         out_specs=pl.BlockSpec(memory_space=pltpu.VMEM),
         compiler_params=params(24),
         cost_estimate=cost(1, HINT),
-    )(place, *arrays)
+    )(place.reshape(1), *arrays)
 
 
 def slice_at(step, at):
@@ -480,17 +496,15 @@
     owners = lax.axis_size(ALL)
     at = jnp.stack([lax.axis_index("x"), lax.axis_index("core")]).astype(jnp.int32)
     gain = norm_gain.reshape(1, features)
-    features, width = query_weight.shape
-    rows = (features - DIRECT) // 4
-    mine = lax.dynamic_slice(query_weight, (DIRECT + lax.axis_index("y") * rows, 0), (rows, width))
-    part = shifted(mine, "x")
-    direct = shifted(query_weight[:DIRECT], "x")
+    place = line_place()
+    quarter = features // 4
+    part = along_x(lax.dynamic_slice_in_dim(query_weight, place * quarter, quarter, axis=0))
     payload, targets = build_payload(
         tokens, gain, blocks, weights, out_cotangent, owners, values.shape[0] // BLOCK
     )
-    set_y = jnp.concatenate(part, axis=1)
-    set_y, payload = lax.optimization_barrier((set_y, payload))
-    own = assemble(query_weight, direct, part, shifted(set_y, "y"))
+    joined = jnp.concatenate(part, axis=1)
+    joined, payload = lax.optimization_barrier((joined, payload))
+    own = assemble(place, query_weight, part, along_line(joined))
     sib = lax.ppermute(own, "core", [(0, 1), (1, 0)])
     got = exchange(payload)
     fold = fold_weight(at, own, sib, values)

time: 188 us -> 197 us (1.048)
  waiting for transfers between devices: 61 us -> 84.1 us
  starting transfers between devices: 46.8 us -> 34.4 us
    ppermute x9 -> x6, waiting for transfers between devices: 17.7 us -> 50.1 us  [the longest x3 46.8 us: along_line(): return [lax.ppermute(rows, ALL, line_step(by)) for by in SHIFTS]]
    ppermute x1, starting transfers between devices: 11.6 us -> 1.94 us  [body(): sib = lax.ppermute(own, 'core', [(0, 1), (1, 0)])]
    all_to_all x2, waiting for transfers between devices: 36.9 us -> 27.5 us  [exchange(): return lax.all_to_all(rows, ALL, split_axis=0, concat_axis=0, tiled=True)]
    ppermute x9 -> x6, starting transfers between devices: 10.3 us -> 8.94 us  [the longest x3 5.06 us: along_line(): return [lax.ppermute(rows, ALL, line_step(by)) for by in SHIFTS]]
  transfers between devices with their start and end apart: 12 -> 9, of which waited for: 5 -> 5; matrix products, arithmetic and copies ran while one was open for 3% -> 2% of each run, Pallas kernels for 26% -> 25%
where the time goes in v5:
time: 197 us; the launch traced here: 196 us
  waiting for transfers between devices  84.1 us (43%)
  Pallas kernels  71.9 us (36%)
  starting transfers between devices  34.4 us (17%)
  local copies, waits for them, and re-layouts  3.79 us (2%)
    ppermute x3, waiting for transfers between devices, along_line(): return [lax.ppermute(rows, ALL, line_step(by)) for by in SHIFTS]  46.8 us
    all_to_all x2, waiting for transfers between devices, exchange(): return lax.all_to_all(rows, ALL, split_axis=0, concat_axis=0, tiled=True)  27.5 us
    pallas_call x1, Pallas kernels, value_grads(): pl.pallas_call(grad_kernel, out_shape=jax.ShapeDtypeStruct((value_rows, f...  24.4 us
    all_to_all x2, starting transfers between devices, exchange(): return lax.all_to_all(rows, ALL, split_axis=0, concat_axis=0, tiled=True)  23.5 us
    pallas_call x1, Pallas kernels, serve(): pl.pallas_call(functools.partial(serve_kernel, float(features) ** (-0.5))...  16.8 us
    pallas_call x1, Pallas kernels, fold_weight(): pl.pallas_call(fold_kernel, out_shape=jax.ShapeDtypeStruct((features, val...  15.1 us
    pallas_call x1, Pallas kernels, finish(): pl.pallas_call(home_kernel, out_shape=(jax.ShapeDtypeStruct((count, featu...  6.73 us
    ppermute x1, waiting for transfers between devices, body(): sib = lax.ppermute(own, 'core', [(0, 1), (1, 0)])  6.47 us
  transfers between devices with their start and end apart: 9, of which 5 were waited for; matrix products, arithmetic and copies ran while one was open for 2% of the time, Pallas kernels for 25%

profile of v5, /device:TPU:7, one launch (start us, length us, event | category | flops | bytes accessed | tf_op | source)
XLA Modules:
  0.0 196.4 jit_solution(2621061764054490495)
XLA Ops:
  0.6 1.0 constant_dynamic-slice_fusion
  1.6 1.2 collective-permute-start.2
  2.8 0.0 collective-permute-start.1
  2.8 2.7 %collective-permute-start = (bf16[512,256]{1,0:T(8,128)(2,1)S(1)}, bf16[512,256]{1,0:T(8,128)(2,1)S(1)}, u32[]{:S(2)}, u32[]{:S(2)}) collective-permute-start(bf16[512,256]{1,0:T(8,128)(2,1)S(1)} %constant_dynamic-slice_fusion), channel_id=1, source_target_pairs={{0,32},{32,64},{64,96},{96,0},{1,33},{33,65},{65,97},{97,1},{2,34}... | collective-permute-start | bytes 786440 | tf_op jit(solution)/shard_map/ppermute | solution.py:140
  5.5 1.4 copy.11.wgt_ref
  6.9 1.4 copy.10.blk_ref
  8.3 5.4 %shard_map.94 = (bf16[1024,2176]{1,0:T(8,128)(2,1)}, s32[128,2]{1,0:T(8,128)}) custom-call(bf16[128,2048]{1,0:T(8,128)(2,1)} %tok_ref.3, f32[1,2048]{1,0:T(1,128)} %bitcast.10, s32[128,2]{1,0:T(8,128)} %copy.10.blk_ref, f32[128,2]{1,0:T(8,128)} %copy.11.wgt_ref, bf16[128,2048]{1,0:T(8,128)(2,1)} %cot_ref.3), custom_call_target="tpu_custom_call" | custom-call | flops 1073741824 | bytes 6291456 | tf_op jit(solution)/shard_map/pallas_call | solution.py:112
  13.7 0.0 collective-permute-done.2.refs_2_
  13.7 3.3 %collective-permute-done.1.refs_1_ = bf16[512,256]{1,0:T(8,128)(2,1)S(1)} collective-permute-done((bf16[512,256]{1,0:T(8,128)(2,1)S(1)}, bf16[512,256]{1,0:T(8,128)(2,1)S(1)}, u32[]{:S(2)}, u32[]{:S(2)}) %collective-permute-start.1) | collective-permute-done | bytes 262176 | tf_op jit(solution)/shard_map/ppermute | solution.py:140
  17.0 0.0 collective-permute-done.refs_0_
  17.1 0.9 pad_maximum_fusion
  18.0 3.6 %collective-permute-start.5 = (bf16[512,768]{1,0:T(8,128)(2,1)}, bf16[512,768]{1,0:T(8,128)(2,1)S(1)}, u32[]{:S(2)}, u32[]{:S(2)}) collective-permute-start(bf16[512,768]{1,0:T(8,128)(2,1)} %pad_maximum_fusion), channel_id=1, source_target_pairs={{0,2},{16,24},{1,3},{17,25},{2,0},{18,26},{3,1},{19,27},{4,6},{20,... | collective-permute-start | bytes 2359304 | tf_op jit(solution)/shard_map/ppermute | solution.py:155
  21.6 0.4 collective-permute-start.4
  22.0 1.0 collective-permute-start.3
  23.0 0.0 copy-start
  23.0 10.2 %all-to-all-start = ((bf16[128,8,2176]{2,1,0:T(8,128)(2,1)}), bf16[128,8,2176]{2,1,0:T(8,128)(2,1)}, u32[]{:S(2)}, u32[]{:S(2)}) async-start(bf16[128,8,2176]{2,1,0:T(8,128)(2,1)} %bitcast.8), calls=%async_computation | async-start | bytes 8912896 | tf_op jit(solution)/shard_map/all_to_all | solution.py:491
  33.3 0.0 collective-permute-done.5.refs_5_
  33.3 43.5 %collective-permute-done.4.refs_4_ = bf16[512,768]{1,0:T(8,128)(2,1)S(1)} collective-permute-done((bf16[512,768]{1,0:T(8,128)(2,1)}, bf16[512,768]{1,0:T(8,128)(2,1)S(1)}, u32[]{:S(2)}, u32[]{:S(2)}) %collective-permute-start.4) | collective-permute-done | bytes 786464 | tf_op jit(solution)/shard_map/ppermute | solution.py:155
  76.8 3.3 %collective-permute-done.3.refs_3_ = bf16[512,768]{1,0:T(8,128)(2,1)} collective-permute-done((bf16[512,768]{1,0:T(8,128)(2,1)}, bf16[512,768]{1,0:T(8,128)(2,1)}, u32[]{:S(2)}, u32[]{:S(2)}) %collective-permute-start.3) | collective-permute-done | bytes 786464 | tf_op jit(solution)/shard_map/ppermute | solution.py:155
  80.1 0.0 copy-done
  80.1 3.3 %shard_map.95.own_ref = bf16[4,2048,256]{2,1,0:T(8,128)(2,1)} custom-call(s32[1]{0:T(128)} %bitcast.5.at_ref, bf16[2048,256]{1,0:T(8,128)(2,1)S(1)} %copy-done, bf16[512,256]{1,0:T(8,128)(2,1)S(1)} %collective-permute-done.refs_0_, bf16[512,256]{1,0:T(8,128)(2,1)S(1)} %collective-permute-done.1.refs_1_, bf16[512,256]{1,0:T(8,128)(2,1)S(1)} %collective-permute-done.2.refs_2_, ...), custom_call_target="tpu_custom_call" | custom-call | flops 1 | bytes 1 | tf_op jit(solution)/shard_map/pallas_call | solution.py:180
  83.4 1.9 collective-permute-start.6
  85.4 0.7 pad_add_fusion.at_ref
  86.0 6.5 %collective-permute-done.6.sib_ref = bf16[4,2048,256]{2,1,0:T(8,128)(2,1)} collective-permute-done((bf16[4,2048,256]{2,1,0:T(8,128)(2,1)}, bf16[4,2048,256]{2,1,0:T(8,128)(2,1)}, u32[]{:S(2)}, u32[]{:S(2)}) %collective-permute-start.6) | collective-permute-done | bytes 4194336 | tf_op jit(solution)/shard_map/ppermute | solution.py:508
  92.5 15.1 %shard_map.96.fold_hbm = bf16[2048,1024]{1,0:T(8,128)(2,1)} custom-call(s32[2]{0:T(128)} %pad_add_fusion.at_ref, bf16[4,2048,256]{2,1,0:T(8,128)(2,1)} %shard_map.95.own_ref, bf16[4,2048,256]{2,1,0:T(8,128)(2,1)} %collective-permute-done.6.sib_ref, bf16[1024,2048]{1,0:T(8,128)(2,1)} %val_hbm.1), custom_call_target="tpu_custom_call" | custom-call | flops 1 | bytes 1 | tf_op jit(solution)/shard_map/pallas_call | solution.py:223
  107.6 0.0 all-to-all-done
  107.6 16.8 %shard_map.97 = (bf16[1024,2048]{1,0:T(8,128)(2,1)}, bf16[512,2048]{1,0:T(8,128)(2,1)}, bf16[512,2048]{1,0:T(8,128)(2,1)}, bf16[512,1024]{1,0:T(8,128)(2,1)}, bf16[512,1024]{1,0:T(8,128)(2,1)}) custom-call(bf16[1024,2176]{1,0:T(8,128)(2,1)} %bitcast.2.x_hbm, bf16[2048,1024]{1,0:T(8,128)(2,1)} %shard_map.96.fold_hbm, bf16[1024,2048]{1,0:T(8,128)(2,1)} %val_hbm.1), custom_call_target="tpu_custom_call" | custom-call | flops 8589934592 | bytes 20971520 | tf_op jit(solution)/shard_map/pallas_call | solution.py:347
  124.5 13.2 %all-to-all-start.1 = ((bf16[128,8,2048]{2,1,0:T(8,128)(2,1)}), bf16[128,8,2048]{2,1,0:T(8,128)(2,1)}, u32[]{:S(2)}, u32[]{:S(2)}) async-start(bf16[128,8,2048]{2,1,0:T(8,128)(2,1)} %bitcast.9), calls=%async_computation.1 | async-start | bytes 8388608 | tf_op jit(solution)/shard_map/all_to_all | solution.py:491
  137.7 24.4 %shard_map.99 = bf16[1024,2048]{1,0:T(8,128)(2,1)} custom-call(s32[2]{0:T(128)} %pad_add_fusion.at_ref, bf16[4,2048,256]{2,1,0:T(8,128)(2,1)} %shard_map.95.own_ref, bf16[4,2048,256]{2,1,0:T(8,128)(2,1)} %collective-permute-done.6.sib_ref, bf16[512,2048]{1,0:T(8,128)(2,1)} %get-tuple-element.21.n_ref, bf16[512,2048]{1,0:T(8,128)(2,1)} %get-tuple-element.22.c_ref, ...), custom_call_target="tpu_custom_call" | custom-call | flops 6442450944 | bytes 25165824 | tf_op jit(solution)/shard_map/pallas_call | solution.py:399
  162.1 27.5 %all-to-all-done.1 = bf16[128,8,2048]{2,1,0:T(8,128)(2,1)} async-done(((bf16[128,8,2048]{2,1,0:T(8,128)(2,1)}), bf16[128,8,2048]{2,1,0:T(8,128)(2,1)}, u32[]{:S(2)}, u32[]{:S(2)}) %all-to-all-start.1) | async-done | bytes 4194336 | tf_op jit(solution)/shard_map/all_to_all | solution.py:491
  189.6 6.7 %shard_map.98 = (f32[128,2048]{1,0:T(8,128)}, f32[128,2048]{1,0:T(8,128)}) custom-call(bf16[1024,2048]{1,0:T(8,128)(2,1)} %bitcast.7.back_ref, s32[128,2]{1,0:T(8,128)} %get-tuple-element.18.tgt_ref, f32[128,2]{1,0:T(8,128)} %copy.11.wgt_ref, bf16[128,2048]{1,0:T(8,128)(2,1)} %tok_ref.3, bf16[128,2048]{1,0:T(8,128)(2,1)} %cot_ref.3, f32[1,2048]{1,0:T(1,128)} %bitcast.11), custom_call_target="tpu_custom_call" | custom-call | flops 1610612736 | bytes 10485760 | tf_op jit(solution)/shard_map/pallas_call | solution.py:463
Async XLA Ops:
  1.6 12.1 %collective-permute-start.2 = (bf16[512,256]{1,0:T(8,128)(2,1)S(1)}, bf16[512,256]{1,0:T(8,128)(2,1)S(1)}, u32[]{:S(2)}, u32[]{:S(2)}) collective-permute-start(bf16[512,256]{1,0:T(8,128)(2,1)S(1)} %constant_dynamic-slice_fusion), channel_id=1, source_target_pairs={{0,64},{32,96},{64,0},{96,32},{1,65},{33,97},{65,1},{97,33},{2,66}... | collective-permute-start | bytes 786440 | tf_op jit(solution)/shard_map/ppermute | solution.py:140
  2.8 14.2 %collective-permute-start.1 = (bf16[512,256]{1,0:T(8,128)(2,1)S(1)}, bf16[512,256]{1,0:T(8,128)(2,1)S(1)}, u32[]{:S(2)}, u32[]{:S(2)}) collective-permute-start(bf16[512,256]{1,0:T(8,128)(2,1)S(1)} %constant_dynamic-slice_fusion), channel_id=1, source_target_pairs={{0,96},{32,0},{64,32},{96,64},{1,97},{33,1},{65,33},{97,65},{2,98}... | collective-permute-start | bytes 786440 | tf_op jit(solution)/shard_map/ppermute | solution.py:140
  2.8 14.2 %collective-permute-start = (bf16[512,256]{1,0:T(8,128)(2,1)S(1)}, bf16[512,256]{1,0:T(8,128)(2,1)S(1)}, u32[]{:S(2)}, u32[]{:S(2)}) collective-permute-start(bf16[512,256]{1,0:T(8,128)(2,1)S(1)} %constant_dynamic-slice_fusion), channel_id=1, source_target_pairs={{0,32},{32,64},{64,96},{96,0},{1,33},{33,65},{65,97},{97,1},{2,34}... | collective-permute-start | bytes 786440 | tf_op jit(solution)/shard_map/ppermute | solution.py:140
  18.0 15.3 %collective-permute-start.5 = (bf16[512,768]{1,0:T(8,128)(2,1)}, bf16[512,768]{1,0:T(8,128)(2,1)S(1)}, u32[]{:S(2)}, u32[]{:S(2)}) collective-permute-start(bf16[512,768]{1,0:T(8,128)(2,1)} %pad_maximum_fusion), channel_id=1, source_target_pairs={{0,2},{16,24},{1,3},{17,25},{2,0},{18,26},{3,1},{19,27},{4,6},{20,... | collective-permute-start | bytes 2359304 | tf_op jit(solution)/shard_map/ppermute | solution.py:155
  21.6 55.2 %collective-permute-start.4 = (bf16[512,768]{1,0:T(8,128)(2,1)}, bf16[512,768]{1,0:T(8,128)(2,1)S(1)}, u32[]{:S(2)}, u32[]{:S(2)}) collective-permute-start(bf16[512,768]{1,0:T(8,128)(2,1)} %pad_maximum_fusion), channel_id=1, source_target_pairs={{0,3},{16,28},{1,0},{17,29},{2,1},{18,30},{3,2},{19,31},{4,7},{20,... | collective-permute-start | bytes 2359304 | tf_op jit(solution)/shard_map/ppermute | solution.py:155
  22.0 58.1 %collective-permute-start.3 = (bf16[512,768]{1,0:T(8,128)(2,1)}, bf16[512,768]{1,0:T(8,128)(2,1)}, u32[]{:S(2)}, u32[]{:S(2)}) collective-permute-start(bf16[512,768]{1,0:T(8,128)(2,1)} %pad_maximum_fusion), channel_id=1, source_target_pairs={{0,1},{16,20},{1,2},{17,21},{2,3},{18,22},{3,0},{19,23},{4,5},{20,... | collective-permute-start | bytes 2359304 | tf_op jit(solution)/shard_map/ppermute | solution.py:155
  23.0 57.0 %copy-start = (bf16[2048,256]{1,0:T(8,128)(2,1)S(1)}, bf16[2048,256]{1,0:T(8,128)(2,1)}, u32[]{:S(2)}) copy-start(bf16[2048,256]{1,0:T(8,128)(2,1)} %w_ref.1) | copy-start | bytes 3145732
  23.0 84.6 %all-to-all-start = ((bf16[128,8,2176]{2,1,0:T(8,128)(2,1)}), bf16[128,8,2176]{2,1,0:T(8,128)(2,1)}, u32[]{:S(2)}, u32[]{:S(2)}) async-start(bf16[128,8,2176]{2,1,0:T(8,128)(2,1)} %bitcast.8), calls=%async_computation | async-start | bytes 8912896 | tf_op jit(solution)/shard_map/all_to_all | solution.py:491
  83.4 9.1 %collective-permute-start.6 = (bf16[4,2048,256]{2,1,0:T(8,128)(2,1)}, bf16[4,2048,256]{2,1,0:T(8,128)(2,1)}, u32[]{:S(2)}, u32[]{:S(2)}) collective-permute-start(bf16[4,2048,256]{2,1,0:T(8,128)(2,1)} %shard_map.95.own_ref), channel_id=1, source_target_pairs={{0,16},{16,0},{1,17},{17,1},{2,18},{18,2},{3,19},{19,3},{4,20},{20... | collective-permute-start | bytes 12582920 | tf_op jit(solution)/shard_map/ppermute | solution.py:508
  124.5 65.2 %all-to-all-start.1 = ((bf16[128,8,2048]{2,1,0:T(8,128)(2,1)}), bf16[128,8,2048]{2,1,0:T(8,128)(2,1)}, u32[]{:S(2)}, u32[]{:S(2)}) async-start(bf16[128,8,2048]{2,1,0:T(8,128)(2,1)} %bitcast.9), calls=%async_computation.1 | async-start | bytes 8388608 | tf_op jit(solution)/shard_map/all_to_all | solution.py:491

commit v6 on v2

--- a/solution.py
+++ b/solution.py
@@ -132,12 +132,14 @@
     )(tokens, gain, blocks, weights, cot)
 
 
-def shifted(rows, by):
+def turn(rows, by):
     return lax.ppermute(rows, "x", [(i, (i + by) % 4) for i in range(4)])
 
 
-def gather_weight(weight):
-    own = jnp.stack([weight, shifted(weight, 1), shifted(weight, 3), shifted(weight, 2)])
+def gather_weight(weight, before, after):
+    half = weight.shape[0] // 2
+    across = jnp.concatenate([turn(before[:half], 1), turn(after[half:], -1)], axis=0)
+    own = jnp.stack([weight, before, after, across])
     return own, lax.ppermute(own, "core", [(0, 1), (1, 0)])
 
 
@@ -189,7 +191,7 @@
 
 
 def serve_kernel(scale, x_hbm, fold_hbm, val_hbm, y_hbm, n_hbm, c_hbm, g_hbm, s_hbm,
-                 x_buf, fold_buf, val_buf, n_buf, c_buf, id_buf, g_buf, s_buf, y_buf,
+                 x_buf, fold_buf, val_buf, n_buf, c_buf, id_buf, g_buf, s_buf, y_buf, score_buf, cot_buf,
                  x_sem, f_sem, v_sem, y_sem, o_sem):
     rows = x_buf.shape[0]
     features = n_buf.shape[1]
@@ -214,9 +216,10 @@
 
     for i in range(parts):
         x_copy(i).start()
-    for i in range(parts):
-        f_copy(i).start()
-        v_copy(i).start()
+    def load(i):
+        if i < parts:
+            f_copy(i).start()
+            v_copy(i).start()
 
     take = 32
     low = lax.broadcasted_iota(jnp.int32, (take // 16, 8, 1), 1) < SLOTS
@@ -230,6 +233,8 @@
 
     for i in range(parts):
         x_copy(i).wait()
+        if i == parts - 2:
+            load(0)
 
         @pl.loop(i * step_rows // take, (i + 1) * step_rows // take)
         def _(r):
@@ -242,19 +247,28 @@
             id_buf[dst, :] = ident
 
     kept = [pltpu.make_async_copy(n_buf, n_hbm, o_sem.at[0]), pltpu.make_async_copy(c_buf, c_hbm, o_sem.at[1])]
+    def products(j):
+        f_copy(j).wait()
+        v_copy(j).wait()
+        load(j + 1)
+        score_buf[j % 2] = nn(n_buf[...], fold_buf[j])
+        cot_buf[j % 2] = nt(c_buf[...], val_buf[j * step_cols : (j + 1) * step_cols, :])
+
+    def gate(j):
+        block_of = (lax.broadcasted_iota(jnp.int32, (1, step_cols), 1) // BLOCK + j * (step_cols // BLOCK)).astype(F32)
+        mine = id_buf[:, :1] == block_of
+        sig = 1.0 / (1.0 + jnp.exp(score_buf[j % 2] * -scale))
+        g_buf[j] = jnp.where(mine, sig, 0.0).astype(BF)
+        s_buf[j] = jnp.where(mine, cot_buf[j % 2] * sig * (1.0 - sig) * scale, 0.0).astype(BF)
+
+    products(0)
+    for j in range(parts):
+        if j + 1 < parts:
+            products(j + 1)
+        gate(j)
     for copy in kept:
         copy.start()
-
     for j in range(parts):
-        f_copy(j).wait()
-        v_copy(j).wait()
-        scores = nn(n_buf[...], fold_buf[j]) * scale
-        cot_scores = nt(c_buf[...], val_buf[j * step_cols : (j + 1) * step_cols, :])
-        sig = 1.0 / (1.0 + jnp.exp(-scores))
-        block_of = (lax.broadcasted_iota(jnp.int32, (1, step_cols), 1) // BLOCK + j * (step_cols // BLOCK)).astype(F32)
-        mine = id_buf[:, :1] == block_of
-        g_buf[j] = jnp.where(mine, sig, 0.0).astype(BF)
-        s_buf[j] = jnp.where(mine, cot_scores * sig * (1.0 - sig) * scale, 0.0).astype(BF)
         at = pl.ds(j * step_cols, step_cols)
         kept.append(pltpu.make_async_copy(g_buf.at[j], g_hbm.at[:, at], o_sem.at[2 + j]))
         kept.append(pltpu.make_async_copy(s_buf.at[j], s_hbm.at[:, at], o_sem.at[2 + parts + j]))
@@ -294,7 +308,7 @@
     rows = x.shape[0]
     slots = rows // 2
     value_rows = values.shape[0]
-    parts, tiles = 4, 8
+    parts, tiles = 4, 4
     step_cols = value_rows // parts
     any_spec = pl.BlockSpec(memory_space=pl.ANY)
     return pl.pallas_call(
@@ -318,6 +332,8 @@
             pltpu.VMEM((parts, slots, step_cols), BF),
             pltpu.VMEM((parts, slots, step_cols), BF),
             pltpu.VMEM((tiles, rows, features // tiles), BF),
+            pltpu.VMEM((2, slots, step_cols), F32),
+            pltpu.VMEM((2, slots, step_cols), F32),
             pltpu.SemaphoreType.DMA((parts,)),
             pltpu.SemaphoreType.DMA((parts,)),
             pltpu.SemaphoreType.DMA((parts,)),
@@ -449,10 +465,12 @@
     owners = lax.axis_size(ALL)
     at = jnp.stack([lax.axis_index("x"), lax.axis_index("core")]).astype(jnp.int32)
     gain = norm_gain.reshape(1, features)
+    before, after = turn(query_weight, 1), turn(query_weight, -1)
     payload, targets = build_payload(
         tokens, gain, blocks, weights, out_cotangent, owners, values.shape[0] // BLOCK
     )
-    own, sib = gather_weight(query_weight)
+    before, after, payload = lax.optimization_barrier((before, after, payload))
+    own, sib = gather_weight(query_weight, before, after)
     got = exchange(payload)
     fold = fold_weight(at, own, sib, values)
     answers, n, c, g, s = serve(got, fold, values, features)

time: 185 us -> 179 us (0.968)
  waiting for transfers between devices: 86.8 us -> 78.2 us
    ppermute x3 -> x4, waiting for transfers between devices: 27.2 us -> 15.4 us  [turn(): return lax.ppermute(rows, 'x', [(i, (i + by) % 4) for i in range(4)])]
    all_to_all x2, waiting for transfers between devices: 53.2 us -> 56.3 us  [exchange(): return lax.all_to_all(rows, ALL, split_axis=0, concat_axis=0, tiled=True)]
    ppermute x3 -> x4, starting transfers between devices: 2.4 us -> 4.2 us  [turn(): return lax.ppermute(rows, 'x', [(i, (i + by) % 4) for i in range(4)])]
  transfers between devices with their start and end apart: 6 -> 7, of which waited for: 6 -> 5; matrix products, arithmetic and copies ran while one was open for 4% -> 4% of each run, Pallas kernels for 24% -> 25%
where the time goes in v6:
time: 179 us
  waiting for transfers between devices  78.2 us (44%)
  Pallas kernels  68.2 us (38%)
  starting transfers between devices  22.8 us (13%)
  local copies, waits for them, and re-layouts  4.48 us (3%)
  other arithmetic  4.21 us (2%)
    all_to_all x2, waiting for transfers between devices, exchange(): return lax.all_to_all(rows, ALL, split_axis=0, concat_axis=0, tiled=True)  56.3 us
    pallas_call x1, Pallas kernels, value_grads(): pl.pallas_call(grad_kernel, out_shape=jax.ShapeDtypeStruct((value_rows, f...  24.4 us
    all_to_all x2, starting transfers between devices, exchange(): return lax.all_to_all(rows, ALL, split_axis=0, concat_axis=0, tiled=True)  18.3 us
    pallas_call x1, Pallas kernels, serve(): pl.pallas_call(functools.partial(serve_kernel, float(features) ** (-0.5))...  16.5 us
    ppermute x4, waiting for transfers between devices, turn(): return lax.ppermute(rows, 'x', [(i, (i + by) % 4) for i in range(4)])  15.4 us
    pallas_call x1, Pallas kernels, fold_weight(): pl.pallas_call(fold_kernel, out_shape=jax.ShapeDtypeStruct((features, val...  15.1 us
    pallas_call x1, Pallas kernels, finish(): pl.pallas_call(home_kernel, out_shape=(jax.ShapeDtypeStruct((count, featu...  6.73 us
    ppermute x1, waiting for transfers between devices, gather_weight(): return (own, lax.ppermute(own, 'core', [(0, 1), (1, 0)]))  6.48 us
  transfers between devices with their start and end apart: 7, of which 5 were waited for; matrix products, arithmetic and copies ran while one was open for 4% of the time, Pallas kernels for 25%

profile of v6, /device:TPU:7, one launch (start us, length us, event | category | flops | bytes accessed | tf_op | source)
XLA Modules:
  0.0 178.6 jit_solution(18345939927087619710)
XLA Ops:
  0.6 0.1 collective-permute-start
  0.7 1.5 collective-permute-start.1
  2.2 1.4 copy.11.wgt_ref
  3.6 1.4 copy.10.blk_ref
  5.0 5.5 %shard_map.94 = (bf16[1024,2176]{1,0:T(8,128)(2,1)}, s32[128,2]{1,0:T(8,128)}) custom-call(bf16[128,2048]{1,0:T(8,128)(2,1)} %tok_ref.3, f32[1,2048]{1,0:T(1,128)} %bitcast.17, s32[128,2]{1,0:T(8,128)} %copy.10.blk_ref, f32[128,2]{1,0:T(8,128)} %copy.11.wgt_ref, bf16[128,2048]{1,0:T(8,128)(2,1)} %cot_ref.3), custom_call_target="tpu_custom_call" | custom-call | flops 1073741824 | bytes 6291456 | tf_op jit(solution)/shard_map/pallas_call | solution.py:111
  10.5 14.4 %collective-permute-done = bf16[2048,256]{1,0:T(8,128)(2,1)S(1)} collective-permute-done((bf16[2048,256]{1,0:T(8,128)(2,1)}, bf16[2048,256]{1,0:T(8,128)(2,1)S(1)}, u32[]{:S(2)}, u32[]{:S(2)}) %collective-permute-start) | collective-permute-done | bytes 1048608 | tf_op jit(solution)/shard_map/ppermute | solution.py:136
  24.9 0.9 collective-permute-done.1
  25.9 0.8 slice.6
  26.7 0.8 slice.7
  27.5 0.2 collective-permute-start.3
  27.7 2.5 %collective-permute-start.2 = (bf16[1024,256]{1,0:T(8,128)(2,1)}, bf16[1024,256]{1,0:T(8,128)(2,1)}, u32[]{:S(2)}, u32[]{:S(2)}) collective-permute-start(bf16[1024,256]{1,0:T(8,128)(2,1)} %slice.6), channel_id=1, source_target_pairs={{0,32},{32,64},{64,96},{96,0},{1,33},{33,65},{65,97},{97,1},{2,34}... | collective-permute-start | bytes 1572872 | tf_op jit(solution)/shard_map/ppermute | solution.py:136
  30.2 0.0 copy-start
  30.2 12.8 %all-to-all-start = ((bf16[128,8,2176]{2,1,0:T(8,128)(2,1)}), bf16[128,8,2176]{2,1,0:T(8,128)(2,1)}, u32[]{:S(2)}, u32[]{:S(2)}) async-start(bf16[128,8,2176]{2,1,0:T(8,128)(2,1)} %bitcast.12), calls=%async_computation | async-start | bytes 8912896 | tf_op jit(solution)/shard_map/all_to_all | solution.py:460
  43.0 0.0 collective-permute-done.3
  43.1 0.0 collective-permute-done.2
  43.1 1.3 maximum_bitcast_fusion
  44.3 0.0 copy-done
  44.3 2.3 %pad_maximum_fusion.own_ref = bf16[4,2048,256]{2,1,0:T(8,128)(2,1)} fusion(bf16[1,2048,256]{2,1,0:T(8,128)(2,1)S(1)} %maximum_bitcast_fusion, bf16[1,2048,256]{2,1,0:T(8,128)(2,1)S(1)} %bitcast.15, bf16[1,2048,256]{2,1,0:T(8,128)(2,1)S(1)} %bitcast.14, bf16[1,2048,256]{2,1,0:T(8,128)(2,1)S(1)} %bitcast.16), kind=kLoop, calls=%fused_computation | loop fusion | flops 6291456 | bytes 8388608 | tf_op jit(solution)/shard_map/stack | solution.py:142
  46.6 0.4 collective-permute-start.4
  47.0 0.7 pad_add_fusion.at_ref
  47.7 6.5 %collective-permute-done.4.sib_ref = bf16[4,2048,256]{2,1,0:T(8,128)(2,1)} collective-permute-done((bf16[4,2048,256]{2,1,0:T(8,128)(2,1)}, bf16[4,2048,256]{2,1,0:T(8,128)(2,1)}, u32[]{:S(2)}, u32[]{:S(2)}) %collective-permute-start.4) | collective-permute-done | bytes 4194336 | tf_op jit(solution)/shard_map/ppermute | solution.py:143
  54.1 15.1 %shard_map.95.fold_hbm = bf16[2048,1024]{1,0:T(8,128)(2,1)} custom-call(s32[2]{0:T(128)} %pad_add_fusion.at_ref, bf16[4,2048,256]{2,1,0:T(8,128)(2,1)} %pad_maximum_fusion.own_ref, bf16[4,2048,256]{2,1,0:T(8,128)(2,1)} %collective-permute-done.4.sib_ref, bf16[1024,2048]{1,0:T(8,128)(2,1)} %val_hbm.1), custom_call_target="tpu_custom_call" | custom-call | flops 1 | bytes 1 | tf_op jit(solution)/shard_map/pallas_call | solution.py:178
  69.2 28.7 %all-to-all-done = bf16[128,8,2176]{2,1,0:T(8,128)(2,1)} async-done(((bf16[128,8,2176]{2,1,0:T(8,128)(2,1)}), bf16[128,8,2176]{2,1,0:T(8,128)(2,1)}, u32[]{:S(2)}, u32[]{:S(2)}) %all-to-all-start) | async-done | bytes 4456480 | tf_op jit(solution)/shard_map/all_to_all | solution.py:460
  98.0 16.5 %shard_map.96 = (bf16[1024,2048]{1,0:T(8,128)(2,1)}, bf16[512,2048]{1,0:T(8,128)(2,1)}, bf16[512,2048]{1,0:T(8,128)(2,1)}, bf16[512,1024]{1,0:T(8,128)(2,1)}, bf16[512,1024]{1,0:T(8,128)(2,1)}) custom-call(bf16[1024,2176]{1,0:T(8,128)(2,1)} %bitcast.2.x_hbm, bf16[2048,1024]{1,0:T(8,128)(2,1)} %shard_map.95.fold_hbm, bf16[1024,2048]{1,0:T(8,128)(2,1)} %val_hbm.1), custom_call_target="tpu_custom_call" | custom-call | flops 8589934592 | bytes 20971520 | tf_op jit(solution)/shard_map/pallas_call | solution.py:314
  114.4 5.5 %all-to-all-start.1 = ((bf16[128,8,2048]{2,1,0:T(8,128)(2,1)}), bf16[128,8,2048]{2,1,0:T(8,128)(2,1)}, u32[]{:S(2)}, u32[]{:S(2)}) async-start(bf16[128,8,2048]{2,1,0:T(8,128)(2,1)} %bitcast.13), calls=%async_computation.1 | async-start | bytes 8388608 | tf_op jit(solution)/shard_map/all_to_all | solution.py:460
  119.9 24.4 %shard_map.98 = bf16[1024,2048]{1,0:T(8,128)(2,1)} custom-call(s32[2]{0:T(128)} %pad_add_fusion.at_ref, bf16[4,2048,256]{2,1,0:T(8,128)(2,1)} %pad_maximum_fusion.own_ref, bf16[4,2048,256]{2,1,0:T(8,128)(2,1)} %collective-permute-done.4.sib_ref, bf16[512,2048]{1,0:T(8,128)(2,1)} %get-tuple-element.23.n_ref, bf16[512,2048]{1,0:T(8,128)(2,1)} %get-tuple-element.24.c_ref, ...), custom_call_target="tpu_custom_call" | custom-call | flops 6442450944 | bytes 25165824 | tf_op jit(solution)/shard_map/pallas_call | solution.py:368
  144.3 27.6 %all-to-all-done.1 = bf16[128,8,2048]{2,1,0:T(8,128)(2,1)} async-done(((bf16[128,8,2048]{2,1,0:T(8,128)(2,1)}), bf16[128,8,2048]{2,1,0:T(8,128)(2,1)}, u32[]{:S(2)}, u32[]{:S(2)}) %all-to-all-start.1) | async-done | bytes 4194336 | tf_op jit(solution)/shard_map/all_to_all | solution.py:460
  171.9 6.7 %shard_map.97 = (f32[128,2048]{1,0:T(8,128)}, f32[128,2048]{1,0:T(8,128)}) custom-call(bf16[1024,2048]{1,0:T(8,128)(2,1)} %bitcast.10.back_ref, s32[128,2]{1,0:T(8,128)} %get-tuple-element.20.tgt_ref, f32[128,2]{1,0:T(8,128)} %copy.11.wgt_ref, bf16[128,2048]{1,0:T(8,128)(2,1)} %tok_ref.3, bf16[128,2048]{1,0:T(8,128)(2,1)} %cot_ref.3, f32[1,2048]{1,0:T(1,128)} %bitcast.18), custom_call_target="tpu_custom_call" | custom-call | flops 1610612736 | bytes 10485760 | tf_op jit(solution)/shard_map/pallas_call | solution.py:432
Async XLA Ops:
  0.6 24.3 %collective-permute-start = (bf16[2048,256]{1,0:T(8,128)(2,1)}, bf16[2048,256]{1,0:T(8,128)(2,1)S(1)}, u32[]{:S(2)}, u32[]{:S(2)}) collective-permute-start(bf16[2048,256]{1,0:T(8,128)(2,1)} %param.9), channel_id=1, source_target_pairs={{0,32},{32,64},{64,96},{96,0},{1,33},{33,65},{65,97},{97,1},{2,34}... | collective-permute-start | bytes 3145736 | tf_op jit(solution)/shard_map/ppermute | solution.py:136
  0.7 25.2 %collective-permute-start.1 = (bf16[2048,256]{1,0:T(8,128)(2,1)}, bf16[2048,256]{1,0:T(8,128)(2,1)S(1)}, u32[]{:S(2)}, u32[]{:S(2)}) collective-permute-start(bf16[2048,256]{1,0:T(8,128)(2,1)} %param.9), channel_id=1, source_target_pairs={{0,96},{32,0},{64,32},{96,64},{1,97},{33,1},{65,33},{97,65},{2,98}... | collective-permute-start | bytes 3145736 | tf_op jit(solution)/shard_map/ppermute | solution.py:136
  27.5 15.5 %collective-permute-start.3 = (bf16[1024,256]{1,0:T(8,128)(2,1)}, bf16[1024,256]{1,0:T(8,128)(2,1)}, u32[]{:S(2)}, u32[]{:S(2)}) collective-permute-start(bf16[1024,256]{1,0:T(8,128)(2,1)} %slice.7), channel_id=1, source_target_pairs={{0,96},{32,0},{64,32},{96,64},{1,97},{33,1},{65,33},{97,65},{2,98}... | collective-permute-start | bytes 1572872 | tf_op jit(solution)/shard_map/ppermute | solution.py:136
  27.7 15.3 %collective-permute-start.2 = (bf16[1024,256]{1,0:T(8,128)(2,1)}, bf16[1024,256]{1,0:T(8,128)(2,1)}, u32[]{:S(2)}, u32[]{:S(2)}) collective-permute-start(bf16[1024,256]{1,0:T(8,128)(2,1)} %slice.6), channel_id=1, source_target_pairs={{0,32},{32,64},{64,96},{96,0},{1,33},{33,65},{65,97},{97,1},{2,34}... | collective-permute-start | bytes 1572872 | tf_op jit(solution)/shard_map/ppermute | solution.py:136
  30.2 14.1 %copy-start = (bf16[2048,256]{1,0:T(8,128)(2,1)S(1)}, bf16[2048,256]{1,0:T(8,128)(2,1)}, u32[]{:S(2)}) copy-start(bf16[2048,256]{1,0:T(8,128)(2,1)} %param.9) | copy-start | bytes 3145732
  30.2 67.7 %all-to-all-start = ((bf16[128,8,2176]{2,1,0:T(8,128)(2,1)}), bf16[128,8,2176]{2,1,0:T(8,128)(2,1)}, u32[]{:S(2)}, u32[]{:S(2)}) async-start(bf16[128,8,2176]{2,1,0:T(8,128)(2,1)} %bitcast.12), calls=%async_computation | async-start | bytes 8912896 | tf_op jit(solution)/shard_map/all_to_all | solution.py:460
  46.6 7.5 %collective-permute-start.4 = (bf16[4,2048,256]{2,1,0:T(8,128)(2,1)}, bf16[4,2048,256]{2,1,0:T(8,128)(2,1)}, u32[]{:S(2)}, u32[]{:S(2)}) collective-permute-start(bf16[4,2048,256]{2,1,0:T(8,128)(2,1)} %pad_maximum_fusion.own_ref), channel_id=1, source_target_pairs={{0,16},{16,0},{1,17},{17,1},{2,18},{18,2},{3,19},{19,3},{4,20},{20... | collective-permute-start | bytes 12582920 | tf_op jit(solution)/shard_map/ppermute | solution.py:143
  114.4 57.5 %all-to-all-start.1 = ((bf16[128,8,2048]{2,1,0:T(8,128)(2,1)}), bf16[128,8,2048]{2,1,0:T(8,128)(2,1)}, u32[]{:S(2)}, u32[]{:S(2)}) async-start(bf16[128,8,2048]{2,1,0:T(8,128)(2,1)} %bitcast.13), calls=%async_computation.1 | async-start | bytes 8388608 | tf_op jit(solution)/shard_map/all_to_all | solution.py:460

commit v7 on v6

--- a/solution.py
+++ b/solution.py
@@ -137,9 +137,8 @@
 
 
 def gather_weight(weight, before, after):
-    half = weight.shape[0] // 2
-    across = jnp.concatenate([turn(before[:half], 1), turn(after[half:], -1)], axis=0)
-    own = jnp.stack([weight, before, after, across])
+    across = jnp.concatenate([turn(before[0], 1), turn(after[1], -1)], axis=0)
+    own = jnp.stack([weight, jnp.concatenate(before, axis=0), jnp.concatenate(after, axis=0), across])
     return own, lax.ppermute(own, "core", [(0, 1), (1, 0)])
 
 
@@ -465,12 +464,14 @@
     owners = lax.axis_size(ALL)
     at = jnp.stack([lax.axis_index("x"), lax.axis_index("core")]).astype(jnp.int32)
     gain = norm_gain.reshape(1, features)
-    before, after = turn(query_weight, 1), turn(query_weight, -1)
+    top, bottom = query_weight[: features // 2], query_weight[features // 2 :]
+    before_top, after_bottom = turn(top, 1), turn(bottom, -1)
+    before_bottom, after_top = turn(bottom, 1), turn(top, -1)
     payload, targets = build_payload(
         tokens, gain, blocks, weights, out_cotangent, owners, values.shape[0] // BLOCK
     )
-    before, after, payload = lax.optimization_barrier((before, after, payload))
-    own, sib = gather_weight(query_weight, before, after)
+    before_top, after_bottom, payload = lax.optimization_barrier((before_top, after_bottom, payload))
+    own, sib = gather_weight(query_weight, [before_top, before_bottom], [after_top, after_bottom])
     got = exchange(payload)
     fold = fold_weight(at, own, sib, values)
     answers, n, c, g, s = serve(got, fold, values, features)

time: 179 us -> 175 us (0.978)
  waiting for transfers between devices: 78.2 us -> 62.4 us
  starting transfers between devices: 22.8 us -> 34.4 us
    ppermute x4 -> x6, waiting for transfers between devices: 15.4 us -> 7.47 us  [turn(): return lax.ppermute(rows, 'x', [(i, (i + by) % 4) for i in range(4)])]
    all_to_all x2, waiting for transfers between devices: 56.3 us -> 48.5 us  [exchange(): return lax.all_to_all(rows, ALL, split_axis=0, concat_axis=0, tiled=True)]
    ppermute x1, starting transfers between devices: 0.36 us -> 5.16 us  [gather_weight(): return (own, lax.ppermute(own, 'core', [(0, 1), (1, 0)]))]
    all_to_all x2, starting transfers between devices: 18.3 us -> 22.6 us  [exchange(): return lax.all_to_all(rows, ALL, split_axis=0, concat_axis=0, tiled=True)]
    ppermute x4 -> x6, starting transfers between devices: 4.2 us -> 6.57 us  [turn(): return lax.ppermute(rows, 'x', [(i, (i + by) % 4) for i in range(4)])]
    another operation x2 -> x4, other arithmetic: 3.55 us -> 3.71 us  [gather_weight(): jnp.stack([weight, jnp.concatenate(before, axis=0), jnp.concatenate(after...]
  transfers between devices with their start and end apart: 7 -> 9, of which waited for: 5 -> 6; matrix products, arithmetic and copies ran while one was open for 4% -> 4% of each run, Pallas kernels for 25% -> 26%
where the time goes in v7:
time: 175 us; the launch traced here: 174 us
  Pallas kernels  68.2 us (39%)
  waiting for transfers between devices  62.4 us (36%)
  starting transfers between devices  34.4 us (20%)
  other arithmetic  4.36 us (2%)
  local copies, waits for them, and re-layouts  4.09 us (2%)
    all_to_all x2, waiting for transfers between devices, exchange(): return lax.all_to_all(rows, ALL, split_axis=0, concat_axis=0, tiled=True)  48.5 us
    pallas_call x1, Pallas kernels, value_grads(): pl.pallas_call(grad_kernel, out_shape=jax.ShapeDtypeStruct((value_rows, f...  24.4 us
    all_to_all x2, starting transfers between devices, exchange(): return lax.all_to_all(rows, ALL, split_axis=0, concat_axis=0, tiled=True)  22.6 us
    pallas_call x1, Pallas kernels, serve(): pl.pallas_call(functools.partial(serve_kernel, float(features) ** (-0.5))...  16.4 us
    pallas_call x1, Pallas kernels, fold_weight(): pl.pallas_call(fold_kernel, out_shape=jax.ShapeDtypeStruct((features, val...  15.1 us
    ppermute x6, waiting for transfers between devices, turn(): return lax.ppermute(rows, 'x', [(i, (i + by) % 4) for i in range(4)])  7.47 us
    pallas_call x1, Pallas kernels, finish(): pl.pallas_call(home_kernel, out_shape=(jax.ShapeDtypeStruct((count, featu...  6.73 us
    ppermute x6, starting transfers between devices, turn(): return lax.ppermute(rows, 'x', [(i, (i + by) % 4) for i in range(4)])  6.57 us
  transfers between devices with their start and end apart: 9, of which 6 were waited for; matrix products, arithmetic and copies ran while one was open for 4% of the time, Pallas kernels for 26%

profile of v7, /device:TPU:7, one launch (start us, length us, event | category | flops | bytes accessed | tf_op | source)
XLA Modules:
  0.0 174.2 jit_solution(10514167862200587322)
XLA Ops:
  0.6 1.3 fusion
  1.9 0.6 collective-permute-start.1
  2.5 2.1 %collective-permute-start = (bf16[1024,256]{1,0:T(8,128)(2,1)S(1)}, bf16[1024,256]{1,0:T(8,128)(2,1)S(1)}, u32[]{:S(2)}, u32[]{:S(2)}) collective-permute-start(bf16[1024,256]{1,0:T(8,128)(2,1)S(1)} %get-tuple-element.28), channel_id=1, source_target_pairs={{0,32},{32,64},{64,96},{96,0},{1,33},{33,65},{65,97},{97,1},{2,34}... | collective-permute-start | bytes 1572872 | tf_op jit(solution)/shard_map/ppermute | solution.py:136
  4.7 0.0 collective-permute-start.2
  4.7 1.4 collective-permute-start.3
  6.1 1.4 copy.11.wgt_ref
  7.5 1.4 copy.10.blk_ref
  8.9 5.6 %shard_map.94 = (bf16[1024,2176]{1,0:T(8,128)(2,1)}, s32[128,2]{1,0:T(8,128)}) custom-call(bf16[128,2048]{1,0:T(8,128)(2,1)} %tok_ref.3, f32[1,2048]{1,0:T(1,128)} %bitcast.17, s32[128,2]{1,0:T(8,128)} %copy.10.blk_ref, f32[128,2]{1,0:T(8,128)} %copy.11.wgt_ref, bf16[128,2048]{1,0:T(8,128)(2,1)} %cot_ref.3), custom_call_target="tpu_custom_call" | custom-call | flops 1073741824 | bytes 6291456 | tf_op jit(solution)/shard_map/pallas_call | solution.py:111
  14.5 1.5 collective-permute-done.1
  16.0 0.0 collective-permute-done
  16.0 2.4 %collective-permute-start.4 = (bf16[1024,256]{1,0:T(8,128)(2,1)S(1)}, bf16[1024,256]{1,0:T(8,128)(2,1)}, u32[]{:S(2)}, u32[]{:S(2)}) collective-permute-start(bf16[1024,256]{1,0:T(8,128)(2,1)S(1)} %collective-permute-done), channel_id=1, source_target_pairs={{0,32},{32,64},{64,96},{96,0},{1,33},{33,65},{65,97},{97,1},{2,34}... | collective-permute-start | bytes 1572872 | tf_op jit(solution)/shard_map/ppermute | solution.py:136
  18.3 0.0 collective-permute-start.5
  18.3 14.4 %all-to-all-start = ((bf16[128,8,2176]{2,1,0:T(8,128)(2,1)}), bf16[128,8,2176]{2,1,0:T(8,128)(2,1)}, u32[]{:S(2)}, u32[]{:S(2)}) async-start(bf16[128,8,2176]{2,1,0:T(8,128)(2,1)} %bitcast.14), calls=%async_computation | async-start | bytes 8912896 | tf_op jit(solution)/shard_map/all_to_all | solution.py:459
  32.8 0.0 copy-start
  32.8 0.0 collective-permute-done.2
  32.8 0.1 maximum_bitcast_fusion
  32.9 0.0 collective-permute-done.3
  32.9 0.1 maximum_bitcast_fusion.1
  33.0 4.7 %collective-permute-done.4 = bf16[1024,256]{1,0:T(8,128)(2,1)} collective-permute-done((bf16[1024,256]{1,0:T(8,128)(2,1)S(1)}, bf16[1024,256]{1,0:T(8,128)(2,1)}, u32[]{:S(2)}, u32[]{:S(2)}) %collective-permute-start.4) | collective-permute-done | bytes 524320 | tf_op jit(solution)/shard_map/ppermute | solution.py:136
  37.6 1.3 collective-permute-done.5
  38.9 1.3 maximum_bitcast_fusion.2
  40.2 0.0 copy-done
  40.2 2.3 %pad_maximum_fusion.own_ref = bf16[4,2048,256]{2,1,0:T(8,128)(2,1)} fusion(bf16[1,2048,256]{2,1,0:T(8,128)(2,1)S(1)} %maximum_bitcast_fusion.2, bf16[1,2048,256]{2,1,0:T(8,128)(2,1)S(1)} %maximum_bitcast_fusion.1, bf16[1,2048,256]{2,1,0:T(8,128)(2,1)S(1)} %maximum_bitcast_fusion, bf16[1,2048,256]{2,1,0:T(8,128)(2,1)S(1)} %bitcast.16), kind=kLoop, calls=%fused_computation | loop fusion | flops 6291456 | bytes 8388608 | tf_op jit(solution)/shard_map/stack | solution.py:141
  42.5 5.2 %collective-permute-start.6 = (bf16[4,2048,256]{2,1,0:T(8,128)(2,1)}, bf16[4,2048,256]{2,1,0:T(8,128)(2,1)}, u32[]{:S(2)}, u32[]{:S(2)}) collective-permute-start(bf16[4,2048,256]{2,1,0:T(8,128)(2,1)} %pad_maximum_fusion.own_ref), channel_id=1, source_target_pairs={{0,16},{16,0},{1,17},{17,1},{2,18},{18,2},{3,19},{19,3},{4,20},{20... | collective-permute-start | bytes 12582920 | tf_op jit(solution)/shard_map/ppermute | solution.py:142
  47.7 0.7 pad_add_fusion.at_ref
  48.3 6.5 %collective-permute-done.6.sib_ref = bf16[4,2048,256]{2,1,0:T(8,128)(2,1)} collective-permute-done((bf16[4,2048,256]{2,1,0:T(8,128)(2,1)}, bf16[4,2048,256]{2,1,0:T(8,128)(2,1)}, u32[]{:S(2)}, u32[]{:S(2)}) %collective-permute-start.6) | collective-permute-done | bytes 4194336 | tf_op jit(solution)/shard_map/ppermute | solution.py:142
  54.8 15.1 %shard_map.95.fold_hbm = bf16[2048,1024]{1,0:T(8,128)(2,1)} custom-call(s32[2]{0:T(128)} %pad_add_fusion.at_ref, bf16[4,2048,256]{2,1,0:T(8,128)(2,1)} %pad_maximum_fusion.own_ref, bf16[4,2048,256]{2,1,0:T(8,128)(2,1)} %collective-permute-done.6.sib_ref, bf16[1024,2048]{1,0:T(8,128)(2,1)} %val_hbm.1), custom_call_target="tpu_custom_call" | custom-call | flops 1 | bytes 1 | tf_op jit(solution)/shard_map/pallas_call | solution.py:177
  69.9 21.0 %all-to-all-done = bf16[128,8,2176]{2,1,0:T(8,128)(2,1)} async-done(((bf16[128,8,2176]{2,1,0:T(8,128)(2,1)}), bf16[128,8,2176]{2,1,0:T(8,128)(2,1)}, u32[]{:S(2)}, u32[]{:S(2)}) %all-to-all-start) | async-done | bytes 4456480 | tf_op jit(solution)/shard_map/all_to_all | solution.py:459
  90.9 16.4 %shard_map.96 = (bf16[1024,2048]{1,0:T(8,128)(2,1)}, bf16[512,2048]{1,0:T(8,128)(2,1)}, bf16[512,2048]{1,0:T(8,128)(2,1)}, bf16[512,1024]{1,0:T(8,128)(2,1)}, bf16[512,1024]{1,0:T(8,128)(2,1)}) custom-call(bf16[1024,2176]{1,0:T(8,128)(2,1)} %bitcast.2.x_hbm, bf16[2048,1024]{1,0:T(8,128)(2,1)} %shard_map.95.fold_hbm, bf16[1024,2048]{1,0:T(8,128)(2,1)} %val_hbm.1), custom_call_target="tpu_custom_call" | custom-call | flops 8589934592 | bytes 20971520 | tf_op jit(solution)/shard_map/pallas_call | solution.py:313
  107.3 8.2 %all-to-all-start.1 = ((bf16[128,8,2048]{2,1,0:T(8,128)(2,1)}), bf16[128,8,2048]{2,1,0:T(8,128)(2,1)}, u32[]{:S(2)}, u32[]{:S(2)}) async-start(bf16[128,8,2048]{2,1,0:T(8,128)(2,1)} %bitcast.15), calls=%async_computation.1 | async-start | bytes 8388608 | tf_op jit(solution)/shard_map/all_to_all | solution.py:459
  115.5 24.4 %shard_map.98 = bf16[1024,2048]{1,0:T(8,128)(2,1)} custom-call(s32[2]{0:T(128)} %pad_add_fusion.at_ref, bf16[4,2048,256]{2,1,0:T(8,128)(2,1)} %pad_maximum_fusion.own_ref, bf16[4,2048,256]{2,1,0:T(8,128)(2,1)} %collective-permute-done.6.sib_ref, bf16[512,2048]{1,0:T(8,128)(2,1)} %get-tuple-element.23.n_ref, bf16[512,2048]{1,0:T(8,128)(2,1)} %get-tuple-element.24.c_ref, ...), custom_call_target="tpu_custom_call" | custom-call | flops 6442450944 | bytes 25165824 | tf_op jit(solution)/shard_map/pallas_call | solution.py:367
  139.9 27.5 %all-to-all-done.1 = bf16[128,8,2048]{2,1,0:T(8,128)(2,1)} async-done(((bf16[128,8,2048]{2,1,0:T(8,128)(2,1)}), bf16[128,8,2048]{2,1,0:T(8,128)(2,1)}, u32[]{:S(2)}, u32[]{:S(2)}) %all-to-all-start.1) | async-done | bytes 4194336 | tf_op jit(solution)/shard_map/all_to_all | solution.py:459
  167.5 6.7 %shard_map.97 = (f32[128,2048]{1,0:T(8,128)}, f32[128,2048]{1,0:T(8,128)}) custom-call(bf16[1024,2048]{1,0:T(8,128)(2,1)} %bitcast.10.back_ref, s32[128,2]{1,0:T(8,128)} %get-tuple-element.20.tgt_ref, f32[128,2]{1,0:T(8,128)} %copy.11.wgt_ref, bf16[128,2048]{1,0:T(8,128)(2,1)} %tok_ref.3, bf16[128,2048]{1,0:T(8,128)(2,1)} %cot_ref.3, f32[1,2048]{1,0:T(1,128)} %bitcast.18), custom_call_target="tpu_custom_call" | custom-call | flops 1610612736 | bytes 10485760 | tf_op jit(solution)/shard_map/pallas_call | solution.py:431
Async XLA Ops:
  1.9 14.1 %collective-permute-start.1 = (bf16[1024,256]{1,0:T(8,128)(2,1)S(1)}, bf16[1024,256]{1,0:T(8,128)(2,1)S(1)}, u32[]{:S(2)}, u32[]{:S(2)}) collective-permute-start(bf16[1024,256]{1,0:T(8,128)(2,1)S(1)} %get-tuple-element.27), channel_id=1, source_target_pairs={{0,96},{32,0},{64,32},{96,64},{1,97},{33,1},{65,33},{97,65},{2,98}... | collective-permute-start | bytes 1572872 | tf_op jit(solution)/shard_map/ppermute | solution.py:136
  2.5 13.5 %collective-permute-start = (bf16[1024,256]{1,0:T(8,128)(2,1)S(1)}, bf16[1024,256]{1,0:T(8,128)(2,1)S(1)}, u32[]{:S(2)}, u32[]{:S(2)}) collective-permute-start(bf16[1024,256]{1,0:T(8,128)(2,1)S(1)} %get-tuple-element.28), channel_id=1, source_target_pairs={{0,32},{32,64},{64,96},{96,0},{1,33},{33,65},{65,97},{97,1},{2,34}... | collective-permute-start | bytes 1572872 | tf_op jit(solution)/shard_map/ppermute | solution.py:136
  4.7 28.1 %collective-permute-start.2 = (bf16[1024,256]{1,0:T(8,128)(2,1)S(1)}, bf16[1024,256]{1,0:T(8,128)(2,1)S(1)}, u32[]{:S(2)}, u32[]{:S(2)}) collective-permute-start(bf16[1024,256]{1,0:T(8,128)(2,1)S(1)} %get-tuple-element.27), channel_id=1, source_target_pairs={{0,32},{32,64},{64,96},{96,0},{1,33},{33,65},{65,97},{97,1},{2,34}... | collective-permute-start | bytes 1572872 | tf_op jit(solution)/shard_map/ppermute | solution.py:136
  4.7 28.2 %collective-permute-start.3 = (bf16[1024,256]{1,0:T(8,128)(2,1)S(1)}, bf16[1024,256]{1,0:T(8,128)(2,1)S(1)}, u32[]{:S(2)}, u32[]{:S(2)}) collective-permute-start(bf16[1024,256]{1,0:T(8,128)(2,1)S(1)} %get-tuple-element.28), channel_id=1, source_target_pairs={{0,96},{32,0},{64,32},{96,64},{1,97},{33,1},{65,33},{97,65},{2,98}... | collective-permute-start | bytes 1572872 | tf_op jit(solution)/shard_map/ppermute | solution.py:136
  16.0 21.6 %collective-permute-start.4 = (bf16[1024,256]{1,0:T(8,128)(2,1)S(1)}, bf16[1024,256]{1,0:T(8,128)(2,1)}, u32[]{:S(2)}, u32[]{:S(2)}) collective-permute-start(bf16[1024,256]{1,0:T(8,128)(2,1)S(1)} %collective-permute-done), channel_id=1, source_target_pairs={{0,32},{32,64},{64,96},{96,0},{1,33},{33,65},{65,97},{97,1},{2,34}... | collective-permute-start | bytes 1572872 | tf_op jit(solution)/shard_map/ppermute | solution.py:136
  18.3 20.6 %collective-permute-start.5 = (bf16[1024,256]{1,0:T(8,128)(2,1)S(1)}, bf16[1024,256]{1,0:T(8,128)(2,1)}, u32[]{:S(2)}, u32[]{:S(2)}) collective-permute-start(bf16[1024,256]{1,0:T(8,128)(2,1)S(1)} %collective-permute-done.1), channel_id=1, source_target_pairs={{0,96},{32,0},{64,32},{96,64},{1,97},{33,1},{65,33},{97,65},{2,98}... | collective-permute-start | bytes 1572872 | tf_op jit(solution)/shard_map/ppermute | solution.py:136
  18.3 72.5 %all-to-all-start = ((bf16[128,8,2176]{2,1,0:T(8,128)(2,1)}), bf16[128,8,2176]{2,1,0:T(8,128)(2,1)}, u32[]{:S(2)}, u32[]{:S(2)}) async-start(bf16[128,8,2176]{2,1,0:T(8,128)(2,1)} %bitcast.14), calls=%async_computation | async-start | bytes 8912896 | tf_op jit(solution)/shard_map/all_to_all | solution.py:459
  32.8 7.4 %copy-start = (bf16[2048,256]{1,0:T(8,128)(2,1)S(1)}, bf16[2048,256]{1,0:T(8,128)(2,1)}, u32[]{:S(2)}) copy-start(bf16[2048,256]{1,0:T(8,128)(2,1)} %param.9) | copy-start | bytes 3145732
  42.5 12.3 %collective-permute-start.6 = (bf16[4,2048,256]{2,1,0:T(8,128)(2,1)}, bf16[4,2048,256]{2,1,0:T(8,128)(2,1)}, u32[]{:S(2)}, u32[]{:S(2)}) collective-permute-start(bf16[4,2048,256]{2,1,0:T(8,128)(2,1)} %pad_maximum_fusion.own_ref), channel_id=1, source_target_pairs={{0,16},{16,0},{1,17},{17,1},{2,18},{18,2},{3,19},{19,3},{4,20},{20... | collective-permute-start | bytes 12582920 | tf_op jit(solution)/shard_map/ppermute | solution.py:142
  107.3 60.1 %all-to-all-start.1 = ((bf16[128,8,2048]{2,1,0:T(8,128)(2,1)}), bf16[128,8,2048]{2,1,0:T(8,128)(2,1)}, u32[]{:S(2)}, u32[]{:S(2)}) async-start(bf16[128,8,2048]{2,1,0:T(8,128)(2,1)} %bitcast.15), calls=%async_computation.1 | async-start | bytes 8388608 | tf_op jit(solution)/shard_map/all_to_all | solution.py:459

commit v8 on v7

--- a/solution.py
+++ b/solution.py
@@ -466,11 +466,13 @@
     gain = norm_gain.reshape(1, features)
     top, bottom = query_weight[: features // 2], query_weight[features // 2 :]
     before_top, after_bottom = turn(top, 1), turn(bottom, -1)
-    before_bottom, after_top = turn(bottom, 1), turn(top, -1)
     payload, targets = build_payload(
         tokens, gain, blocks, weights, out_cotangent, owners, values.shape[0] // BLOCK
     )
-    before_top, after_bottom, payload = lax.optimization_barrier((before_top, after_bottom, payload))
+    before_top, after_bottom, top, bottom, payload = lax.optimization_barrier(
+        (before_top, after_bottom, top, bottom, payload)
+    )
+    before_bottom, after_top = turn(bottom, 1), turn(top, -1)
     own, sib = gather_weight(query_weight, [before_top, before_bottom], [after_top, after_bottom])
     got = exchange(payload)
     fold = fold_weight(at, own, sib, values)

time: 175 us -> 180 us (1.029)
  starting transfers between devices: 34.4 us -> 38.9 us
    ppermute x1, starting transfers between devices: 5.16 us -> 9.25 us  [gather_weight(): return (own, lax.ppermute(own, 'core', [(0, 1), (1, 0)]))]
  transfers between devices with their start and end apart: 9 -> 9, of which waited for: 6 -> 6; matrix products, arithmetic and copies ran while one was open for 4% -> 5% of each run, Pallas kernels for 26% -> 25%
where the time goes in v8:
time: 180 us; the launch traced here: 179 us
  Pallas kernels  68.2 us (38%)
  waiting for transfers between devices  62.1 us (34%)
  starting transfers between devices  38.9 us (22%)
  other arithmetic  5.33 us (3%)
  local copies, waits for them, and re-layouts  4.09 us (2%)
    all_to_all x2, waiting for transfers between devices, exchange(): return lax.all_to_all(rows, ALL, split_axis=0, concat_axis=0, tiled=True)  47 us
    pallas_call x1, Pallas kernels, value_grads(): pl.pallas_call(grad_kernel, out_shape=jax.ShapeDtypeStruct((value_rows, f...  24.4 us
    all_to_all x2, starting transfers between devices, exchange(): return lax.all_to_all(rows, ALL, split_axis=0, concat_axis=0, tiled=True)  21.9 us
    pallas_call x1, Pallas kernels, serve(): pl.pallas_call(functools.partial(serve_kernel, float(features) ** (-0.5))...  16.4 us
    pallas_call x1, Pallas kernels, fold_weight(): pl.pallas_call(fold_kernel, out_shape=jax.ShapeDtypeStruct((features, val...  15.1 us
    ppermute x1, starting transfers between devices, gather_weight(): return (own, lax.ppermute(own, 'core', [(0, 1), (1, 0)]))  9.25 us
    ppermute x6, waiting for transfers between devices, turn(): return lax.ppermute(rows, 'x', [(i, (i + by) % 4) for i in range(4)])  8.62 us
    ppermute x6, starting transfers between devices, turn(): return lax.ppermute(rows, 'x', [(i, (i + by) % 4) for i in range(4)])  7.78 us
  transfers between devices with their start and end apart: 9, of which 6 were waited for; matrix products, arithmetic and copies ran while one was open for 5% of the time, Pallas kernels for 25%

profile of v8, /device:TPU:7, one launch (start us, length us, event | category | flops | bytes accessed | tf_op | source)
XLA Modules:
  0.0 179.3 jit_solution(2121944598432721791)
XLA Ops:
  0.6 1.3 fusion
  1.9 0.6 collective-permute-start.1
  2.5 2.1 %collective-permute-start = (bf16[1024,256]{1,0:T(8,128)(2,1)S(1)}, bf16[1024,256]{1,0:T(8,128)(2,1)S(1)}, u32[]{:S(2)}, u32[]{:S(2)}) collective-permute-start(bf16[1024,256]{1,0:T(8,128)(2,1)S(1)} %get-tuple-element.21), channel_id=1, source_target_pairs={{0,32},{32,64},{64,96},{96,0},{1,33},{33,65},{65,97},{97,1},{2,34}... | collective-permute-start | bytes 1572872 | tf_op jit(solution)/shard_map/ppermute | solution.py:136
  4.7 1.4 copy.11.wgt_ref
  6.1 1.4 copy.10.blk_ref
  7.5 5.5 %shard_map.94 = (bf16[1024,2176]{1,0:T(8,128)(2,1)}, s32[128,2]{1,0:T(8,128)}) custom-call(bf16[128,2048]{1,0:T(8,128)(2,1)} %tok_ref.3, f32[1,2048]{1,0:T(1,128)} %bitcast.17, s32[128,2]{1,0:T(8,128)} %copy.10.blk_ref, f32[128,2]{1,0:T(8,128)} %copy.11.wgt_ref, bf16[128,2048]{1,0:T(8,128)(2,1)} %cot_ref.3), custom_call_target="tpu_custom_call" | custom-call | flops 1073741824 | bytes 6291456 | tf_op jit(solution)/shard_map/pallas_call | solution.py:111
  13.0 3.0 %collective-permute-done.1 = bf16[1024,256]{1,0:T(8,128)(2,1)S(1)} collective-permute-done((bf16[1024,256]{1,0:T(8,128)(2,1)S(1)}, bf16[1024,256]{1,0:T(8,128)(2,1)S(1)}, u32[]{:S(2)}, u32[]{:S(2)}) %collective-permute-start.1) | collective-permute-done | bytes 524320 | tf_op jit(solution)/shard_map/ppermute | solution.py:136
  16.0 0.0 collective-permute-done
  16.0 2.4 %collective-permute-start.2 = (bf16[1024,256]{1,0:T(8,128)(2,1)S(1)}, bf16[1024,256]{1,0:T(8,128)(2,1)}, u32[]{:S(2)}, u32[]{:S(2)}) collective-permute-start(bf16[1024,256]{1,0:T(8,128)(2,1)S(1)} %get-tuple-element.20), channel_id=1, source_target_pairs={{0,32},{32,64},{64,96},{96,0},{1,33},{33,65},{65,97},{97,1},{2,34}... | collective-permute-start | bytes 1572872 | tf_op jit(solution)/shard_map/ppermute | solution.py:136
  18.3 0.0 collective-permute-start.3
  18.3 2.7 %collective-permute-start.4 = (bf16[1024,256]{1,0:T(8,128)(2,1)S(1)}, bf16[1024,256]{1,0:T(8,128)(2,1)S(1)}, u32[]{:S(2)}, u32[]{:S(2)}) collective-permute-start(bf16[1024,256]{1,0:T(8,128)(2,1)S(1)} %collective-permute-done), channel_id=1, source_target_pairs={{0,32},{32,64},{64,96},{96,0},{1,33},{33,65},{65,97},{97,1},{2,34}... | collective-permute-start | bytes 1572872 | tf_op jit(solution)/shard_map/ppermute | solution.py:136
  21.0 0.0 collective-permute-start.5
  21.0 13.5 %all-to-all-start = ((bf16[128,8,2176]{2,1,0:T(8,128)(2,1)}), bf16[128,8,2176]{2,1,0:T(8,128)(2,1)}, u32[]{:S(2)}, u32[]{:S(2)}) async-start(bf16[128,8,2176]{2,1,0:T(8,128)(2,1)} %bitcast.14), calls=%async_computation | async-start | bytes 8912896 | tf_op jit(solution)/shard_map/all_to_all | solution.py:459
  34.5 0.0 copy-start
  34.5 0.0 collective-permute-done.2
  34.6 1.2 maximum_bitcast_fusion
  35.8 0.0 collective-permute-done.3
  35.8 1.1 maximum_bitcast_fusion.1
  36.9 2.3 %collective-permute-done.4 = bf16[1024,256]{1,0:T(8,128)(2,1)S(1)} collective-permute-done((bf16[1024,256]{1,0:T(8,128)(2,1)S(1)}, bf16[1024,256]{1,0:T(8,128)(2,1)S(1)}, u32[]{:S(2)}, u32[]{:S(2)}) %collective-permute-start.4) | collective-permute-done | bytes 524320 | tf_op jit(solution)/shard_map/ppermute | solution.py:136
  39.2 3.3 %collective-permute-done.5 = bf16[1024,256]{1,0:T(8,128)(2,1)S(1)} collective-permute-done((bf16[1024,256]{1,0:T(8,128)(2,1)S(1)}, bf16[1024,256]{1,0:T(8,128)(2,1)S(1)}, u32[]{:S(2)}, u32[]{:S(2)}) %collective-permute-start.5) | collective-permute-done | bytes 524320 | tf_op jit(solution)/shard_map/ppermute | solution.py:136
  42.5 0.1 maximum_bitcast_fusion.2
  42.6 0.0 copy-done
  42.6 2.3 %pad_maximum_fusion.own_ref = bf16[4,2048,256]{2,1,0:T(8,128)(2,1)} fusion(bf16[1,2048,256]{2,1,0:T(8,128)(2,1)S(1)} %maximum_bitcast_fusion.2, bf16[1,2048,256]{2,1,0:T(8,128)(2,1)S(1)} %maximum_bitcast_fusion.1, bf16[1,2048,256]{2,1,0:T(8,128)(2,1)S(1)} %maximum_bitcast_fusion, bf16[1,2048,256]{2,1,0:T(8,128)(2,1)S(1)} %bitcast.16), kind=kLoop, calls=%fused_computation | loop fusion | flops 6291456 | bytes 8388608 | tf_op jit(solution)/shard_map/stack | solution.py:141
  44.9 9.3 %collective-permute-start.6 = (bf16[4,2048,256]{2,1,0:T(8,128)(2,1)}, bf16[4,2048,256]{2,1,0:T(8,128)(2,1)}, u32[]{:S(2)}, u32[]{:S(2)}) collective-permute-start(bf16[4,2048,256]{2,1,0:T(8,128)(2,1)} %pad_maximum_fusion.own_ref), channel_id=1, source_target_pairs={{0,16},{16,0},{1,17},{17,1},{2,18},{18,2},{3,19},{19,3},{4,20},{20... | collective-permute-start | bytes 12582920 | tf_op jit(solution)/shard_map/ppermute | solution.py:142
  54.2 0.7 pad_add_fusion.at_ref
  54.8 6.5 %collective-permute-done.6.sib_ref = bf16[4,2048,256]{2,1,0:T(8,128)(2,1)} collective-permute-done((bf16[4,2048,256]{2,1,0:T(8,128)(2,1)}, bf16[4,2048,256]{2,1,0:T(8,128)(2,1)}, u32[]{:S(2)}, u32[]{:S(2)}) %collective-permute-start.6) | collective-permute-done | bytes 4194336 | tf_op jit(solution)/shard_map/ppermute | solution.py:142
  61.3 15.1 %shard_map.95.fold_hbm = bf16[2048,1024]{1,0:T(8,128)(2,1)} custom-call(s32[2]{0:T(128)} %pad_add_fusion.at_ref, bf16[4,2048,256]{2,1,0:T(8,128)(2,1)} %pad_maximum_fusion.own_ref, bf16[4,2048,256]{2,1,0:T(8,128)(2,1)} %collective-permute-done.6.sib_ref, bf16[1024,2048]{1,0:T(8,128)(2,1)} %val_hbm.1), custom_call_target="tpu_custom_call" | custom-call | flops 1 | bytes 1 | tf_op jit(solution)/shard_map/pallas_call | solution.py:177
  76.4 19.5 %all-to-all-done = bf16[128,8,2176]{2,1,0:T(8,128)(2,1)} async-done(((bf16[128,8,2176]{2,1,0:T(8,128)(2,1)}), bf16[128,8,2176]{2,1,0:T(8,128)(2,1)}, u32[]{:S(2)}, u32[]{:S(2)}) %all-to-all-start) | async-done | bytes 4456480 | tf_op jit(solution)/shard_map/all_to_all | solution.py:459
  95.9 16.4 %shard_map.96 = (bf16[1024,2048]{1,0:T(8,128)(2,1)}, bf16[512,2048]{1,0:T(8,128)(2,1)}, bf16[512,2048]{1,0:T(8,128)(2,1)}, bf16[512,1024]{1,0:T(8,128)(2,1)}, bf16[512,1024]{1,0:T(8,128)(2,1)}) custom-call(bf16[1024,2176]{1,0:T(8,128)(2,1)} %bitcast.2.x_hbm, bf16[2048,1024]{1,0:T(8,128)(2,1)} %shard_map.95.fold_hbm, bf16[1024,2048]{1,0:T(8,128)(2,1)} %val_hbm.1), custom_call_target="tpu_custom_call" | custom-call | flops 8589934592 | bytes 20971520 | tf_op jit(solution)/shard_map/pallas_call | solution.py:313
  112.3 8.3 %all-to-all-start.1 = ((bf16[128,8,2048]{2,1,0:T(8,128)(2,1)}), bf16[128,8,2048]{2,1,0:T(8,128)(2,1)}, u32[]{:S(2)}, u32[]{:S(2)}) async-start(bf16[128,8,2048]{2,1,0:T(8,128)(2,1)} %bitcast.15), calls=%async_computation.1 | async-start | bytes 8388608 | tf_op jit(solution)/shard_map/all_to_all | solution.py:459
  120.7 24.4 %shard_map.98 = bf16[1024,2048]{1,0:T(8,128)(2,1)} custom-call(s32[2]{0:T(128)} %pad_add_fusion.at_ref, bf16[4,2048,256]{2,1,0:T(8,128)(2,1)} %pad_maximum_fusion.own_ref, bf16[4,2048,256]{2,1,0:T(8,128)(2,1)} %collective-permute-done.6.sib_ref, bf16[512,2048]{1,0:T(8,128)(2,1)} %get-tuple-element.27.n_ref, bf16[512,2048]{1,0:T(8,128)(2,1)} %get-tuple-element.28.c_ref, ...), custom_call_target="tpu_custom_call" | custom-call | flops 6442450944 | bytes 25165824 | tf_op jit(solution)/shard_map/pallas_call | solution.py:367
  145.1 27.5 %all-to-all-done.1 = bf16[128,8,2048]{2,1,0:T(8,128)(2,1)} async-done(((bf16[128,8,2048]{2,1,0:T(8,128)(2,1)}), bf16[128,8,2048]{2,1,0:T(8,128)(2,1)}, u32[]{:S(2)}, u32[]{:S(2)}) %all-to-all-start.1) | async-done | bytes 4194336 | tf_op jit(solution)/shard_map/all_to_all | solution.py:459
  172.6 6.7 %shard_map.97 = (f32[128,2048]{1,0:T(8,128)}, f32[128,2048]{1,0:T(8,128)}) custom-call(bf16[1024,2048]{1,0:T(8,128)(2,1)} %bitcast.10.back_ref, s32[128,2]{1,0:T(8,128)} %get-tuple-element.24.tgt_ref, f32[128,2]{1,0:T(8,128)} %copy.11.wgt_ref, bf16[128,2048]{1,0:T(8,128)(2,1)} %tok_ref.3, bf16[128,2048]{1,0:T(8,128)(2,1)} %cot_ref.3, f32[1,2048]{1,0:T(1,128)} %bitcast.18), custom_call_target="tpu_custom_call" | custom-call | flops 1610612736 | bytes 10485760 | tf_op jit(solution)/shard_map/pallas_call | solution.py:431
Async XLA Ops:
  1.9 14.1 %collective-permute-start.1 = (bf16[1024,256]{1,0:T(8,128)(2,1)S(1)}, bf16[1024,256]{1,0:T(8,128)(2,1)S(1)}, u32[]{:S(2)}, u32[]{:S(2)}) collective-permute-start(bf16[1024,256]{1,0:T(8,128)(2,1)S(1)} %get-tuple-element.20), channel_id=1, source_target_pairs={{0,96},{32,0},{64,32},{96,64},{1,97},{33,1},{65,33},{97,65},{2,98}... | collective-permute-start | bytes 1572872 | tf_op jit(solution)/shard_map/ppermute | solution.py:136
  2.5 13.5 %collective-permute-start = (bf16[1024,256]{1,0:T(8,128)(2,1)S(1)}, bf16[1024,256]{1,0:T(8,128)(2,1)S(1)}, u32[]{:S(2)}, u32[]{:S(2)}) collective-permute-start(bf16[1024,256]{1,0:T(8,128)(2,1)S(1)} %get-tuple-element.21), channel_id=1, source_target_pairs={{0,32},{32,64},{64,96},{96,0},{1,33},{33,65},{65,97},{97,1},{2,34}... | collective-permute-start | bytes 1572872 | tf_op jit(solution)/shard_map/ppermute | solution.py:136
  16.0 18.6 %collective-permute-start.2 = (bf16[1024,256]{1,0:T(8,128)(2,1)S(1)}, bf16[1024,256]{1,0:T(8,128)(2,1)}, u32[]{:S(2)}, u32[]{:S(2)}) collective-permute-start(bf16[1024,256]{1,0:T(8,128)(2,1)S(1)} %get-tuple-element.20), channel_id=1, source_target_pairs={{0,32},{32,64},{64,96},{96,0},{1,33},{33,65},{65,97},{97,1},{2,34}... | collective-permute-start | bytes 1572872 | tf_op jit(solution)/shard_map/ppermute | solution.py:136
  18.3 17.4 %collective-permute-start.3 = (bf16[1024,256]{1,0:T(8,128)(2,1)S(1)}, bf16[1024,256]{1,0:T(8,128)(2,1)}, u32[]{:S(2)}, u32[]{:S(2)}) collective-permute-start(bf16[1024,256]{1,0:T(8,128)(2,1)S(1)} %get-tuple-element.21), channel_id=1, source_target_pairs={{0,96},{32,0},{64,32},{96,64},{1,97},{33,1},{65,33},{97,65},{2,98}... | collective-permute-start | bytes 1572872 | tf_op jit(solution)/shard_map/ppermute | solution.py:136
  18.3 20.9 %collective-permute-start.4 = (bf16[1024,256]{1,0:T(8,128)(2,1)S(1)}, bf16[1024,256]{1,0:T(8,128)(2,1)S(1)}, u32[]{:S(2)}, u32[]{:S(2)}) collective-permute-start(bf16[1024,256]{1,0:T(8,128)(2,1)S(1)} %collective-permute-done), channel_id=1, source_target_pairs={{0,32},{32,64},{64,96},{96,0},{1,33},{33,65},{65,97},{97,1},{2,34}... | collective-permute-start | bytes 1572872 | tf_op jit(solution)/shard_map/ppermute | solution.py:136
  21.0 21.5 %collective-permute-start.5 = (bf16[1024,256]{1,0:T(8,128)(2,1)S(1)}, bf16[1024,256]{1,0:T(8,128)(2,1)S(1)}, u32[]{:S(2)}, u32[]{:S(2)}) collective-permute-start(bf16[1024,256]{1,0:T(8,128)(2,1)S(1)} %collective-permute-done.1), channel_id=1, source_target_pairs={{0,96},{32,0},{64,32},{96,64},{1,97},{33,1},{65,33},{97,65},{2,98}... | collective-permute-start | bytes 1572872 | tf_op jit(solution)/shard_map/ppermute | solution.py:136
  21.0 74.9 %all-to-all-start = ((bf16[128,8,2176]{2,1,0:T(8,128)(2,1)}), bf16[128,8,2176]{2,1,0:T(8,128)(2,1)}, u32[]{:S(2)}, u32[]{:S(2)}) async-start(bf16[128,8,2176]{2,1,0:T(8,128)(2,1)} %bitcast.14), calls=%async_computation | async-start | bytes 8912896 | tf_op jit(solution)/shard_map/all_to_all | solution.py:459
  34.5 8.1 %copy-start = (bf16[2048,256]{1,0:T(8,128)(2,1)S(1)}, bf16[2048,256]{1,0:T(8,128)(2,1)}, u32[]{:S(2)}) copy-start(bf16[2048,256]{1,0:T(8,128)(2,1)} %param.9) | copy-start | bytes 3145732
  44.9 16.4 %collective-permute-start.6 = (bf16[4,2048,256]{2,1,0:T(8,128)(2,1)}, bf16[4,2048,256]{2,1,0:T(8,128)(2,1)}, u32[]{:S(2)}, u32[]{:S(2)}) collective-permute-start(bf16[4,2048,256]{2,1,0:T(8,128)(2,1)} %pad_maximum_fusion.own_ref), channel_id=1, source_target_pairs={{0,16},{16,0},{1,17},{17,1},{2,18},{18,2},{3,19},{19,3},{4,20},{20... | collective-permute-start | bytes 12582920 | tf_op jit(solution)/shard_map/ppermute | solution.py:142
  112.3 60.3 %all-to-all-start.1 = ((bf16[128,8,2048]{2,1,0:T(8,128)(2,1)}), bf16[128,8,2048]{2,1,0:T(8,128)(2,1)}, u32[]{:S(2)}, u32[]{:S(2)}) async-start(bf16[128,8,2048]{2,1,0:T(8,128)(2,1)} %bitcast.15), calls=%async_computation.1 | async-start | bytes 8388608 | tf_op jit(solution)/shard_map/all_to_all | solution.py:459

commit v9 on v7

--- a/solution.py
+++ b/solution.py
@@ -426,7 +426,7 @@
 def finish(back, targets, weights, tokens, cot, gain):
     count, features = tokens.shape
     rows = back.shape[0]
-    steps = 4
+    steps = 8
     width = features // steps
     return pl.pallas_call(
         home_kernel,

time: 175 us -> 177 us (1.011)
  Pallas kernels: 68.2 us -> 70.4 us
    pallas_call x1, Pallas kernels: 6.73 us -> 8.91 us  [finish(): pl.pallas_call(home_kernel, out_shape=(jax.ShapeDtypeStruct((count, featu...]
where the time goes in v9:
time: 177 us; the launch traced here: 176 us
  Pallas kernels  70.4 us (40%)
  waiting for transfers between devices  62.4 us (35%)
  starting transfers between devices  34.4 us (19%)
  other arithmetic  4.36 us (2%)
  local copies, waits for them, and re-layouts  4.09 us (2%)
    all_to_all x2, waiting for transfers between devices, exchange(): return lax.all_to_all(rows, ALL, split_axis=0, concat_axis=0, tiled=True)  48.5 us
    pallas_call x1, Pallas kernels, value_grads(): pl.pallas_call(grad_kernel, out_shape=jax.ShapeDtypeStruct((value_rows, f...  24.4 us
    all_to_all x2, starting transfers between devices, exchange(): return lax.all_to_all(rows, ALL, split_axis=0, concat_axis=0, tiled=True)  22.6 us
    pallas_call x1, Pallas kernels, serve(): pl.pallas_call(functools.partial(serve_kernel, float(features) ** (-0.5))...  16.4 us
    pallas_call x1, Pallas kernels, fold_weight(): pl.pallas_call(fold_kernel, out_shape=jax.ShapeDtypeStruct((features, val...  15.1 us
    pallas_call x1, Pallas kernels, finish(): pl.pallas_call(home_kernel, out_shape=(jax.ShapeDtypeStruct((count, featu...  8.91 us
    ppermute x6, waiting for transfers between devices, turn(): return lax.ppermute(rows, 'x', [(i, (i + by) % 4) for i in range(4)])  7.47 us
    ppermute x6, starting transfers between devices, turn(): return lax.ppermute(rows, 'x', [(i, (i + by) % 4) for i in range(4)])  6.57 us
  transfers between devices with their start and end apart: 9, of which 6 were waited for; matrix products, arithmetic and copies ran while one was open for 4% of the time, Pallas kernels for 26%

profile of v9, /device:TPU:7, one launch (start us, length us, event | category | flops | bytes accessed | tf_op | source)
XLA Modules:
  0.0 176.4 jit_solution(17179541358198581853)
XLA Ops:
  0.6 1.3 fusion
  1.9 0.6 collective-permute-start.1
  2.5 2.1 %collective-permute-start = (bf16[1024,256]{1,0:T(8,128)(2,1)S(1)}, bf16[1024,256]{1,0:T(8,128)(2,1)S(1)}, u32[]{:S(2)}, u32[]{:S(2)}) collective-permute-start(bf16[1024,256]{1,0:T(8,128)(2,1)S(1)} %get-tuple-element.28), channel_id=1, source_target_pairs={{0,32},{32,64},{64,96},{96,0},{1,33},{33,65},{65,97},{97,1},{2,34}... | collective-permute-start | bytes 1572872 | tf_op jit(solution)/shard_map/ppermute | solution.py:136
  4.7 0.0 collective-permute-start.2
  4.7 1.4 collective-permute-start.3
  6.1 1.4 copy.11.wgt_ref
  7.5 1.4 copy.10.blk_ref
  8.9 5.6 %shard_map.94 = (bf16[1024,2176]{1,0:T(8,128)(2,1)}, s32[128,2]{1,0:T(8,128)}) custom-call(bf16[128,2048]{1,0:T(8,128)(2,1)} %tok_ref.3, f32[1,2048]{1,0:T(1,128)} %bitcast.17, s32[128,2]{1,0:T(8,128)} %copy.10.blk_ref, f32[128,2]{1,0:T(8,128)} %copy.11.wgt_ref, bf16[128,2048]{1,0:T(8,128)(2,1)} %cot_ref.3), custom_call_target="tpu_custom_call" | custom-call | flops 1073741824 | bytes 6291456 | tf_op jit(solution)/shard_map/pallas_call | solution.py:111
  14.5 1.5 collective-permute-done.1
  16.0 0.0 collective-permute-done
  16.0 2.4 %collective-permute-start.4 = (bf16[1024,256]{1,0:T(8,128)(2,1)S(1)}, bf16[1024,256]{1,0:T(8,128)(2,1)}, u32[]{:S(2)}, u32[]{:S(2)}) collective-permute-start(bf16[1024,256]{1,0:T(8,128)(2,1)S(1)} %collective-permute-done), channel_id=1, source_target_pairs={{0,32},{32,64},{64,96},{96,0},{1,33},{33,65},{65,97},{97,1},{2,34}... | collective-permute-start | bytes 1572872 | tf_op jit(solution)/shard_map/ppermute | solution.py:136
  18.3 0.0 collective-permute-start.5
  18.3 14.4 %all-to-all-start = ((bf16[128,8,2176]{2,1,0:T(8,128)(2,1)}), bf16[128,8,2176]{2,1,0:T(8,128)(2,1)}, u32[]{:S(2)}, u32[]{:S(2)}) async-start(bf16[128,8,2176]{2,1,0:T(8,128)(2,1)} %bitcast.14), calls=%async_computation | async-start | bytes 8912896 | tf_op jit(solution)/shard_map/all_to_all | solution.py:459
  32.8 0.0 copy-start
  32.8 0.0 collective-permute-done.2
  32.8 0.1 maximum_bitcast_fusion
  32.9 0.0 collective-permute-done.3
  32.9 0.1 maximum_bitcast_fusion.1
  33.0 4.7 %collective-permute-done.4 = bf16[1024,256]{1,0:T(8,128)(2,1)} collective-permute-done((bf16[1024,256]{1,0:T(8,128)(2,1)S(1)}, bf16[1024,256]{1,0:T(8,128)(2,1)}, u32[]{:S(2)}, u32[]{:S(2)}) %collective-permute-start.4) | collective-permute-done | bytes 524320 | tf_op jit(solution)/shard_map/ppermute | solution.py:136
  37.6 1.3 collective-permute-done.5
  38.9 1.3 maximum_bitcast_fusion.2
  40.2 0.0 copy-done
  40.2 2.3 %pad_maximum_fusion.own_ref = bf16[4,2048,256]{2,1,0:T(8,128)(2,1)} fusion(bf16[1,2048,256]{2,1,0:T(8,128)(2,1)S(1)} %maximum_bitcast_fusion.2, bf16[1,2048,256]{2,1,0:T(8,128)(2,1)S(1)} %maximum_bitcast_fusion.1, bf16[1,2048,256]{2,1,0:T(8,128)(2,1)S(1)} %maximum_bitcast_fusion, bf16[1,2048,256]{2,1,0:T(8,128)(2,1)S(1)} %bitcast.16), kind=kLoop, calls=%fused_computation | loop fusion | flops 6291456 | bytes 8388608 | tf_op jit(solution)/shard_map/stack | solution.py:141
  42.5 5.2 %collective-permute-start.6 = (bf16[4,2048,256]{2,1,0:T(8,128)(2,1)}, bf16[4,2048,256]{2,1,0:T(8,128)(2,1)}, u32[]{:S(2)}, u32[]{:S(2)}) collective-permute-start(bf16[4,2048,256]{2,1,0:T(8,128)(2,1)} %pad_maximum_fusion.own_ref), channel_id=1, source_target_pairs={{0,16},{16,0},{1,17},{17,1},{2,18},{18,2},{3,19},{19,3},{4,20},{20... | collective-permute-start | bytes 12582920 | tf_op jit(solution)/shard_map/ppermute | solution.py:142
  47.7 0.7 pad_add_fusion.at_ref
  48.3 6.5 %collective-permute-done.6.sib_ref = bf16[4,2048,256]{2,1,0:T(8,128)(2,1)} collective-permute-done((bf16[4,2048,256]{2,1,0:T(8,128)(2,1)}, bf16[4,2048,256]{2,1,0:T(8,128)(2,1)}, u32[]{:S(2)}, u32[]{:S(2)}) %collective-permute-start.6) | collective-permute-done | bytes 4194336 | tf_op jit(solution)/shard_map/ppermute | solution.py:142
  54.8 15.1 %shard_map.95.fold_hbm = bf16[2048,1024]{1,0:T(8,128)(2,1)} custom-call(s32[2]{0:T(128)} %pad_add_fusion.at_ref, bf16[4,2048,256]{2,1,0:T(8,128)(2,1)} %pad_maximum_fusion.own_ref, bf16[4,2048,256]{2,1,0:T(8,128)(2,1)} %collective-permute-done.6.sib_ref, bf16[1024,2048]{1,0:T(8,128)(2,1)} %val_hbm.1), custom_call_target="tpu_custom_call" | custom-call | flops 1 | bytes 1 | tf_op jit(solution)/shard_map/pallas_call | solution.py:177
  69.9 21.0 %all-to-all-done = bf16[128,8,2176]{2,1,0:T(8,128)(2,1)} async-done(((bf16[128,8,2176]{2,1,0:T(8,128)(2,1)}), bf16[128,8,2176]{2,1,0:T(8,128)(2,1)}, u32[]{:S(2)}, u32[]{:S(2)}) %all-to-all-start) | async-done | bytes 4456480 | tf_op jit(solution)/shard_map/all_to_all | solution.py:459
  90.9 16.4 %shard_map.96 = (bf16[1024,2048]{1,0:T(8,128)(2,1)}, bf16[512,2048]{1,0:T(8,128)(2,1)}, bf16[512,2048]{1,0:T(8,128)(2,1)}, bf16[512,1024]{1,0:T(8,128)(2,1)}, bf16[512,1024]{1,0:T(8,128)(2,1)}) custom-call(bf16[1024,2176]{1,0:T(8,128)(2,1)} %bitcast.2.x_hbm, bf16[2048,1024]{1,0:T(8,128)(2,1)} %shard_map.95.fold_hbm, bf16[1024,2048]{1,0:T(8,128)(2,1)} %val_hbm.1), custom_call_target="tpu_custom_call" | custom-call | flops 8589934592 | bytes 20971520 | tf_op jit(solution)/shard_map/pallas_call | solution.py:313
  107.3 8.2 %all-to-all-start.1 = ((bf16[128,8,2048]{2,1,0:T(8,128)(2,1)}), bf16[128,8,2048]{2,1,0:T(8,128)(2,1)}, u32[]{:S(2)}, u32[]{:S(2)}) async-start(bf16[128,8,2048]{2,1,0:T(8,128)(2,1)} %bitcast.15), calls=%async_computation.1 | async-start | bytes 8388608 | tf_op jit(solution)/shard_map/all_to_all | solution.py:459
  115.5 24.4 %shard_map.98 = bf16[1024,2048]{1,0:T(8,128)(2,1)} custom-call(s32[2]{0:T(128)} %pad_add_fusion.at_ref, bf16[4,2048,256]{2,1,0:T(8,128)(2,1)} %pad_maximum_fusion.own_ref, bf16[4,2048,256]{2,1,0:T(8,128)(2,1)} %collective-permute-done.6.sib_ref, bf16[512,2048]{1,0:T(8,128)(2,1)} %get-tuple-element.23.n_ref, bf16[512,2048]{1,0:T(8,128)(2,1)} %get-tuple-element.24.c_ref, ...), custom_call_target="tpu_custom_call" | custom-call | flops 6442450944 | bytes 25165824 | tf_op jit(solution)/shard_map/pallas_call | solution.py:367
  139.9 27.5 %all-to-all-done.1 = bf16[128,8,2048]{2,1,0:T(8,128)(2,1)} async-done(((bf16[128,8,2048]{2,1,0:T(8,128)(2,1)}), bf16[128,8,2048]{2,1,0:T(8,128)(2,1)}, u32[]{:S(2)}, u32[]{:S(2)}) %all-to-all-start.1) | async-done | bytes 4194336 | tf_op jit(solution)/shard_map/all_to_all | solution.py:459
  167.5 8.9 %shard_map.97 = (f32[128,2048]{1,0:T(8,128)}, f32[128,2048]{1,0:T(8,128)}) custom-call(bf16[1024,2048]{1,0:T(8,128)(2,1)} %bitcast.10.back_ref, s32[128,2]{1,0:T(8,128)} %get-tuple-element.20.tgt_ref, f32[128,2]{1,0:T(8,128)} %copy.11.wgt_ref, bf16[128,2048]{1,0:T(8,128)(2,1)} %tok_ref.3, bf16[128,2048]{1,0:T(8,128)(2,1)} %cot_ref.3, f32[1,2048]{1,0:T(1,128)} %bitcast.18), custom_call_target="tpu_custom_call" | custom-call | flops 1610612736 | bytes 10485760 | tf_op jit(solution)/shard_map/pallas_call | solution.py:431
Async XLA Ops:
  1.9 14.1 %collective-permute-start.1 = (bf16[1024,256]{1,0:T(8,128)(2,1)S(1)}, bf16[1024,256]{1,0:T(8,128)(2,1)S(1)}, u32[]{:S(2)}, u32[]{:S(2)}) collective-permute-start(bf16[1024,256]{1,0:T(8,128)(2,1)S(1)} %get-tuple-element.27), channel_id=1, source_target_pairs={{0,96},{32,0},{64,32},{96,64},{1,97},{33,1},{65,33},{97,65},{2,98}... | collective-permute-start | bytes 1572872 | tf_op jit(solution)/shard_map/ppermute | solution.py:136
  2.5 13.5 %collective-permute-start = (bf16[1024,256]{1,0:T(8,128)(2,1)S(1)}, bf16[1024,256]{1,0:T(8,128)(2,1)S(1)}, u32[]{:S(2)}, u32[]{:S(2)}) collective-permute-start(bf16[1024,256]{1,0:T(8,128)(2,1)S(1)} %get-tuple-element.28), channel_id=1, source_target_pairs={{0,32},{32,64},{64,96},{96,0},{1,33},{33,65},{65,97},{97,1},{2,34}... | collective-permute-start | bytes 1572872 | tf_op jit(solution)/shard_map/ppermute | solution.py:136
  4.7 28.1 %collective-permute-start.2 = (bf16[1024,256]{1,0:T(8,128)(2,1)S(1)}, bf16[1024,256]{1,0:T(8,128)(2,1)S(1)}, u32[]{:S(2)}, u32[]{:S(2)}) collective-permute-start(bf16[1024,256]{1,0:T(8,128)(2,1)S(1)} %get-tuple-element.27), channel_id=1, source_target_pairs={{0,32},{32,64},{64,96},{96,0},{1,33},{33,65},{65,97},{97,1},{2,34}... | collective-permute-start | bytes 1572872 | tf_op jit(solution)/shard_map/ppermute | solution.py:136
  4.7 28.2 %collective-permute-start.3 = (bf16[1024,256]{1,0:T(8,128)(2,1)S(1)}, bf16[1024,256]{1,0:T(8,128)(2,1)S(1)}, u32[]{:S(2)}, u32[]{:S(2)}) collective-permute-start(bf16[1024,256]{1,0:T(8,128)(2,1)S(1)} %get-tuple-element.28), channel_id=1, source_target_pairs={{0,96},{32,0},{64,32},{96,64},{1,97},{33,1},{65,33},{97,65},{2,98}... | collective-permute-start | bytes 1572872 | tf_op jit(solution)/shard_map/ppermute | solution.py:136
  16.0 21.6 %collective-permute-start.4 = (bf16[1024,256]{1,0:T(8,128)(2,1)S(1)}, bf16[1024,256]{1,0:T(8,128)(2,1)}, u32[]{:S(2)}, u32[]{:S(2)}) collective-permute-start(bf16[1024,256]{1,0:T(8,128)(2,1)S(1)} %collective-permute-done), channel_id=1, source_target_pairs={{0,32},{32,64},{64,96},{96,0},{1,33},{33,65},{65,97},{97,1},{2,34}... | collective-permute-start | bytes 1572872 | tf_op jit(solution)/shard_map/ppermute | solution.py:136
  18.3 20.6 %collective-permute-start.5 = (bf16[1024,256]{1,0:T(8,128)(2,1)S(1)}, bf16[1024,256]{1,0:T(8,128)(2,1)}, u32[]{:S(2)}, u32[]{:S(2)}) collective-permute-start(bf16[1024,256]{1,0:T(8,128)(2,1)S(1)} %collective-permute-done.1), channel_id=1, source_target_pairs={{0,96},{32,0},{64,32},{96,64},{1,97},{33,1},{65,33},{97,65},{2,98}... | collective-permute-start | bytes 1572872 | tf_op jit(solution)/shard_map/ppermute | solution.py:136
  18.3 72.5 %all-to-all-start = ((bf16[128,8,2176]{2,1,0:T(8,128)(2,1)}), bf16[128,8,2176]{2,1,0:T(8,128)(2,1)}, u32[]{:S(2)}, u32[]{:S(2)}) async-start(bf16[128,8,2176]{2,1,0:T(8,128)(2,1)} %bitcast.14), calls=%async_computation | async-start | bytes 8912896 | tf_op jit(solution)/shard_map/all_to_all | solution.py:459
  32.8 7.4 %copy-start = (bf16[2048,256]{1,0:T(8,128)(2,1)S(1)}, bf16[2048,256]{1,0:T(8,128)(2,1)}, u32[]{:S(2)}) copy-start(bf16[2048,256]{1,0:T(8,128)(2,1)} %param.9) | copy-start | bytes 3145732
  42.5 12.3 %collective-permute-start.6 = (bf16[4,2048,256]{2,1,0:T(8,128)(2,1)}, bf16[4,2048,256]{2,1,0:T(8,128)(2,1)}, u32[]{:S(2)}, u32[]{:S(2)}) collective-permute-start(bf16[4,2048,256]{2,1,0:T(8,128)(2,1)} %pad_maximum_fusion.own_ref), channel_id=1, source_target_pairs={{0,16},{16,0},{1,17},{17,1},{2,18},{18,2},{3,19},{19,3},{4,20},{20... | collective-permute-start | bytes 12582920 | tf_op jit(solution)/shard_map/ppermute | solution.py:142
  107.3 60.1 %all-to-all-start.1 = ((bf16[128,8,2048]{2,1,0:T(8,128)(2,1)}), bf16[128,8,2048]{2,1,0:T(8,128)(2,1)}, u32[]{:S(2)}, u32[]{:S(2)}) async-start(bf16[128,8,2048]{2,1,0:T(8,128)(2,1)} %bitcast.15), calls=%async_computation.1 | async-start | bytes 8388608 | tf_op jit(solution)/shard_map/all_to_all | solution.py:459
